TPU v7x, 512 devices: a whole 4x8x8 slice. The times are simulated.
512 devices in a mesh: tm: 16 (over z, core), space: 32 (over y, x).
Axes of the slice: x: 4, y: 8, z: 8, core: 2. Of those that a mesh axis runs over, the one named last changes fastest.
Arguments:
- tokens: bfloat16 [131072, 1024], P(('tm', 'space')), may hold values from -6 to 6
- latents: bfloat16 [512, 1024], replicated, may hold values from -300 to 300
- up_weight: bfloat16 [1024, 4096], P(None, 'tm'), may hold values from -0.1875 to 0.1875
- down_weight: bfloat16 [4096, 1024], P('tm'), may hold values from -0.09375 to 0.09375
Outputs:
- new_tokens: bfloat16 [131072, 1024], P(('tm', 'space'))
- new_latents: bfloat16 [512, 1024], P('space')
All inputs are finite; a program needn't handle non-finite values.
Results may differ from a plain program's by a relative error of at most 0.012.
The roundings to bfloat16 on the way count: a program that leaves them out, or rounds other values in their place, can miss the bound.
Values may be sent and summed in bfloat16 or wider, within the bound.
No kernel may reach another device: no remote copies, remote signals or barrier semaphores. Data moves between devices by JAX's collectives and lax.ppermute only.
A program may use at most 64 MiB of HBM per device.

v0:
```python
import jax
import jax.numpy as jnp
from jax import lax
from jax.sharding import Mesh
from jax.sharding import PartitionSpec as P

H = 16
SPACE = ("space_0", "space_1")
TM_SPACE = ("tm_0", "tm_1", "space_0", "space_1")
TM = ("tm_0", "tm_1")


epsilon = 1e-05
head_groups = 4


def by_axis(shard, axes):
    for axis in axes:
        shard = lax.pmax(shard, axis)
    return shard


def cut_along(shard, dim, size):
    before, after = (shard.shape[:dim], shard.shape[dim + 1 :])
    return jnp.moveaxis(shard.reshape(*before, size, -1, *after), dim, 0)


def summed_on_arrival(shard, axis, dim):
    size = lax.axis_size(axis)
    tiles = lax.all_to_all(cut_along(shard, dim, size), axis, 0, 0, tiled=True)
    return jnp.sum(tiles.astype(jnp.float32), axis=0)


def in_one_piece(arrays, axis, dim, along):
    both = jnp.concatenate(arrays, axis=along)
    whole, at, outs = (summed_on_arrival(both, axis, dim), 0, [])
    for a in arrays:
        outs.append(lax.slice_in_dim(whole, at, at + a.shape[along], axis=along))
        at += a.shape[along]
    return tuple(outs)


def from_everyone(shard, axis):
    copies = jnp.broadcast_to(shard, (lax.axis_size(axis), *shard.shape))
    return lax.all_to_all(copies, axis, split_axis=0, concat_axis=0, tiled=True)


def over_copies(shard, axis):
    everything = from_everyone(shard, axis)
    return jnp.sum(everything.astype(jnp.float32), axis=0)


def in_order(tiles, dim):
    tiles = jnp.moveaxis(tiles, 0, dim)
    dims = tiles.shape
    return tiles.reshape(*dims[:dim], dims[dim] * dims[dim + 1], *dims[dim + 2 :])


def collect(shard, axis, dim):
    tiles = from_everyone(shard, axis)
    return in_order(tiles, dim)


def layer_norm(values):
    center = values - jnp.mean(values, axis=-1, keepdims=True)
    spread = jnp.mean(center * center, axis=-1, keepdims=True)
    return center * lax.rsqrt(spread + epsilon)


def split_heads(matrix, head_count):
    row_count = matrix.shape[0]
    head_size = matrix.shape[1] // head_count
    return matrix.reshape(row_count, head_groups, head_count // head_groups, head_size).transpose(
        1, 2, 0, 3
    )


def per_head(weighted, factor):
    row_count = weighted.shape[0]
    return (weighted.reshape(row_count, factor.shape[1], -1) * factor[:, :, None]).reshape(
        row_count, weighted.shape[1]
    )


def read_partial(queries, keys_tok, tokens, head_count):
    score_scale = (queries.shape[1] // head_count) ** (-0.5)

    def read_one_group(operands):
        query_part, key_part, value_part = operands
        scores = (
            jnp.einsum("hld,htd->hlt", query_part, key_part, preferred_element_type=jnp.float32)
            * score_scale
        )
        row_peak = jnp.max(scores, axis=-1)
        weights = jnp.exp(scores - row_peak[..., None])
        row_total = jnp.sum(weights, axis=-1)
        weighted = jnp.einsum(
            "hlt,htd->lhd",
            weights.astype(jnp.bfloat16),
            value_part,
            preferred_element_type=jnp.float32,
        )
        return (row_peak, row_total, weighted)

    row_peak, row_total, weighted = lax.map(
        read_one_group,
        (
            split_heads(queries, head_count),
            split_heads(keys_tok, head_count),
            split_heads(tokens, head_count),
        ),
    )
    latent_count = queries.shape[0]
    row_peak = row_peak.reshape(head_count, latent_count).T
    row_total = row_total.reshape(head_count, latent_count).T
    weighted = weighted.transpose(1, 0, 2, 3).reshape(latent_count, queries.shape[1])
    return (row_peak, row_total, weighted)


def write_tokens(keys_tok, all_latents, tokens, head_count):
    score_scale = (all_latents.shape[1] // head_count) ** (-0.5)
    write_values = layer_norm(all_latents.astype(jnp.float32)).astype(jnp.bfloat16)

    def write_one_group(operands):
        query_part, key_part, value_part = operands
        scores = (
            jnp.einsum("htd,hld->htl", query_part, key_part, preferred_element_type=jnp.float32)
            * score_scale
        )
        weights = jnp.exp(scores - jnp.max(scores, axis=-1, keepdims=True))
        shares = (weights / jnp.sum(weights, axis=-1, keepdims=True)).astype(jnp.bfloat16)
        return jnp.einsum("htl,hld->thd", shares, value_part, preferred_element_type=jnp.float32)

    attended = lax.map(
        write_one_group,
        (
            split_heads(keys_tok, head_count),
            split_heads(all_latents, head_count),
            split_heads(write_values, head_count),
        ),
    )
    token_count = tokens.shape[0]
    attended = attended.transpose(1, 0, 2, 3).reshape(token_count, tokens.shape[1])
    return (tokens.astype(jnp.float32) + attended).astype(jnp.bfloat16)


def on_device(tokens, latents, up_weight, down_weight):
    head_count = H
    keys_tok = layer_norm(tokens.astype(jnp.float32)).astype(jnp.bfloat16)
    row_peak, row_total, weighted = read_partial(latents, keys_tok, tokens, head_count)
    owner_rows = latents.shape[0] // lax.axis_size(SPACE)
    row_start = lax.axis_index(SPACE) * owner_rows
    global_peak = by_axis(row_peak.astype(jnp.bfloat16), TM_SPACE).astype(row_peak.dtype)
    factor = jnp.exp(row_peak - global_peak)
    scaled_total = row_total * factor
    scaled_weighted = per_head(weighted, factor)
    row_total, weighted = in_one_piece(
        (scaled_total.astype(jnp.bfloat16), scaled_weighted.astype(jnp.bfloat16)), SPACE, 0, 1
    )
    row_total, weighted = (
        over_copies(row_total.astype(jnp.bfloat16), TM).astype(jnp.float32),
        over_copies(weighted.astype(jnp.bfloat16), TM).astype(jnp.float32),
    )
    read_out = (weighted.reshape(owner_rows, head_count, -1) / row_total[:, :, None]).reshape(
        owner_rows, latents.shape[1]
    )
    own_latents = lax.dynamic_slice_in_dim(latents, row_start, owner_rows, 0).astype(jnp.float32)
    middle = own_latents + read_out
    normed = layer_norm(middle).astype(jnp.bfloat16)
    hidden_part = jax.nn.gelu(
        jnp.dot(normed, up_weight, preferred_element_type=jnp.float32), approximate=False
    ).astype(jnp.bfloat16)
    mlp_part = jnp.dot(hidden_part, down_weight, preferred_element_type=jnp.float32)
    new_latents = (
        middle + over_copies(mlp_part.astype(jnp.bfloat16), TM).astype(jnp.float32)
    ).astype(jnp.bfloat16)
    all_latents = collect(new_latents, SPACE, 0)
    new_tokens = write_tokens(keys_tok, all_latents, tokens, head_count)
    return (new_tokens, new_latents)


def solution(mesh):
    split = Mesh(mesh.devices.reshape(8, 2, 8, 4), ("tm_0", "tm_1", "space_0", "space_1"))
    in_specs = (P(TM_SPACE, None), P(), P(None, TM), P(TM, None))
    out_specs = (P(TM_SPACE, None), P(SPACE, None))
    return jax.shard_map(
        on_device, mesh=split, in_specs=in_specs, out_specs=out_specs, check_vma=False
    )
```

profile of v0, /device:TPU:1, one launch (start us, length us, event | category | flops | bytes accessed | tf_op | source)
XLA Modules:
  0.0 255.4 jit_solution(14696693872098825342)
XLA Ops:
  2.5 1.5 copy.32
  4.0 8.8 %while.24 = (s32[]{:T(128)}, f32[4,4,512]{2,1,0:T(4,128)S(1)}, f32[4,4,512]{2,1,0:T(4,128)S(1)}, f32[4,512,4,64]{1,3,2,0:T(8,128)}, bf16[4,4,512,64]{2,3,1,0:T(8...) while((s32[]{:T(128)}, f32[4,4,512]{2,1,0:T(4,128)S(1)}, ...), condition=%wide.region_5.6_spmd, body=%wide.region_2.5_spmd.sunk | while | flops 138407936 | bytes 7407705 | solution.py:105
  7.1 1.3 fusion.169
  9.3 1.3 fusion.169
  11.5 1.3 fusion.169
  12.8 29.8 %pmax.28 = bf16[512,16]{0,1:T(8,128)(2,1)S(1)} all-reduce(bf16[512,16]{0,1:T(8,128)(2,1)S(1)} %bitcast_convert_fusion), channel_id=1, replica_groups=mesh['tm_0'=8,'tm_1'=2,'space_0'=8,'space_1'=4] {'tm_0'}, use_global_device_ids=true, to_apply=%region_6.7 | all-reduce | flops 8192 | bytes 32768 | tf_op jit(solution)/shard_map/pmax | solution.py:19
  42.6 10.8 %pmax.29 = bf16[512,16]{0,1:T(8,128)(2,1)S(1)} all-reduce(bf16[512,16]{0,1:T(8,128)(2,1)S(1)} %pmax.28), channel_id=1, replica_groups=mesh['tm_0'=8,'tm_1'=2,'space_0'=8,'space_1'=4] {'tm_1'}, use_global_device_ids=true, to_apply=%region_7.8 | all-reduce | flops 8192 | bytes 32768 | tf_op jit(solution)/shard_map/pmax | solution.py:19
  53.4 23.2 %pmax.30 = bf16[512,16]{0,1:T(8,128)(2,1)S(1)} all-reduce(bf16[512,16]{0,1:T(8,128)(2,1)S(1)} %pmax.29), channel_id=1, replica_groups=mesh['tm_0'=8,'tm_1'=2,'space_0'=8,'space_1'=4] {'space_0'}, use_global_device_ids=true, to_apply=%region_8.9 | all-reduce | flops 8192 | bytes 32768 | tf_op jit(solution)/shard_map/pmax | solution.py:19
  76.6 13.5 %pmax.31 = bf16[512,16]{0,1:T(8,128)(2,1)S(1)} all-reduce(bf16[512,16]{0,1:T(8,128)(2,1)S(1)} %pmax.30), channel_id=1, replica_groups=mesh['tm_0'=8,'tm_1'=2,'space_0'=8,'space_1'=4] {'space_1'}, use_global_device_ids=true, to_apply=%region_9.10 | all-reduce | flops 8192 | bytes 32768 | tf_op jit(solution)/shard_map/pmax | solution.py:19
  90.1 1.9 fusion.64
  92.8 25.0 %all_to_all.25 = bf16[32,16,1040]{2,1,0:T(8,128)(2,1)S(1)} all-to-all(bf16[32,16,1040]{2,1,0:T(8,128)(2,1)S(1)} %bitcast.124), channel_id=1, replica_groups=mesh['tm_0'=8,'tm_1'=2,'space_0'=8,'space_1'=4] {'space_0','space_1'}, dimensions={0} | all-to-all | bytes 2129920 | tf_op jit(solution)/shard_map/all_to_all | solution.py:30
  118.8 16.3 %all-to-all-start.2 = ((bf16[16,2,128]{2,1,0:T(2,128)(2,1)}), bf16[16,2,128]{2,1,0:T(2,128)(2,1)S(1)}, u32[]{:S(2)}, u32[]{:S(2)}) async-start(bf16[16,2,128]{2,1,0:T(2,128)(2,1)} %reshape.113), calls=%async_computation.2 | async-start | bytes 16384 | tf_op jit(solution)/shard_map/all_to_all | solution.py:45
  135.1 6.9 %all-to-all-done.2 = bf16[16,2,128]{2,1,0:T(2,128)(2,1)S(1)} async-done(((bf16[16,2,128]{2,1,0:T(2,128)(2,1)}), bf16[16,2,128]{2,1,0:T(2,128)(2,1)S(1)}, u32[]{:S(2)}, u32[]{:S(2)}) %all-to-all-start.2) | async-done | bytes 8224 | tf_op jit(solution)/shard_map/all_to_all | solution.py:45
  142.9 4.0 %all-to-all-start.1 = ((bf16[16,16,1024]{2,1,0:T(8,128)(2,1)}), bf16[16,16,1024]{2,1,0:T(8,128)(2,1)S(1)}, u32[]{:S(2)}, u32[]{:S(2)}) async-start(bf16[16,16,1024]{2,1,0:T(8,128)(2,1)} %broadcast_in_dim.46), calls=%async_computation.1 | async-start | bytes 1048576 | tf_op jit(solution)/shard_map/all_to_all | solution.py:45
  147.3 17.0 %all-to-all-done.1 = bf16[16,16,1024]{2,1,0:T(8,128)(2,1)S(1)} async-done(((bf16[16,16,1024]{2,1,0:T(8,128)(2,1)}), bf16[16,16,1024]{2,1,0:T(8,128)(2,1)S(1)}, u32[]{:S(2)}, u32[]{:S(2)}) %all-to-all-start.1) | async-done | bytes 524320 | tf_op jit(solution)/shard_map/all_to_all | solution.py:45
  166.1 19.9 %all_to_all.26 = bf16[16,16,1024]{2,1,0:T(8,128)(2,1)S(1)} all-to-all(bf16[16,16,1024]{2,1,0:T(8,128)(2,1)S(1)} %broadcast_in_dim.48), channel_id=1, replica_groups=mesh['tm_0'=8,'tm_1'=2,'space_0'=8,'space_1'=4] {'tm_0','tm_1'}, dimensions={0} | all-to-all | bytes 1048576 | tf_op jit(solution)/shard_map/all_to_all | solution.py:45
  187.2 4.1 %all-to-all-start.4 = ((bf16[32,16,1024]{2,1,0:T(8,128)(2,1)}), bf16[32,16,1024]{2,1,0:T(8,128)(2,1)S(1)}, u32[]{:S(2)}, u32[]{:S(2)}) async-start(bf16[32,16,1024]{2,1,0:T(8,128)(2,1)} %broadcast_in_dim.49), calls=%async_computation.4 | async-start | bytes 2097152 | tf_op jit(solution)/shard_map/all_to_all | solution.py:45
  191.3 27.7 %all-to-all-done.4 = bf16[32,16,1024]{2,1,0:T(8,128)(2,1)S(1)} async-done(((bf16[32,16,1024]{2,1,0:T(8,128)(2,1)}), bf16[32,16,1024]{2,1,0:T(8,128)(2,1)S(1)}, u32[]{:S(2)}, u32[]{:S(2)}) %all-to-all-start.4) | async-done | bytes 1048608 | tf_op jit(solution)/shard_map/all_to_all | solution.py:45
  220.1 4.1 %reshape_reshape.7 = bf16[512,4,4,64]{3,2,1,0:T(4,128)(2,1)S(1)} reshape(bf16[32,16,1024]{2,1,0:T(8,128)(2,1)} %copy-done.1) | data formatting | bytes 2097152 | tf_op jit(solution)/shard_map/reshape;reshape | solution.py:73
  224.3 3.0 %fusion.63 = bf16[4,4,512,64]{3,1,0,2:T(4,128)(2,1)} fusion(bf16[512,4,4,64]{3,2,1,0:T(4,128)(2,1)S(1)} %reshape_reshape.7, f32[512]{0:T(512)S(1)} %rsqrt.30, f32[512]{0:T(512)S(1)} %div.47), kind=kLoop, calls=%fused_computation.48 | loop fusion | flops 2097152 | bytes 2101248 | tf_op jit(solution)/shard_map/transpose | solution.py:73
  227.3 4.1 %copy.35 = bf16[4,4,512,64]{2,3,1,0:T(8,128)(2,1)} copy(bf16[4,4,512,64]{3,1,0,2:T(4,128)(2,1)} %fusion.63) | data formatting | bytes 2097152 | tf_op jit(solution)/shard_map/while | solution.py:134
  231.4 2.8 %copy.36 = bf16[4,4,512,64]{2,3,1,0:T(8,128)(2,1)} copy(bf16[4,4,512,64]{3,1,0,2:T(4,128)(2,1)S(1)} %bitcast.122) | data formatting | bytes 2097152 | tf_op jit(solution)/shard_map/while | solution.py:134
  234.2 18.9 %while.25 = (s32[]{:T(128)}, f32[4,256,4,64]{1,3,2,0:T(8,128)}, bf16[4,4,512,64]{2,3,1,0:T(8,128)(2,1)}, bf16[4,4,256,64]{2,3,1,0:T(8,128)(2,1)}, bf16[4,4,512,64]{2,3,1,0:T(8,128)(2,1)}, /*index=5*/s32[]{:T(128)}) while((s32[]{:T(128)}, f32[4,256,4,64]{1,3,2,0:T(8,128)}, bf16[4,4,512,64]{2,3,1,0:T(8,128)(2,1)}, ...), condition=%wide.region_21.22_spmd, body=%wide.region_18.21_spmd.sunk | while | flops 204998656 | bytes 1322053 | solution.py:134
  234.2 1.9 fusion.176
  236.0 2.9 %fusion.177 = f32[4,256,4,64]{1,3,2,0:T(8,128)} fusion(f32[4,256,4,64]{1,3,2,0:T(8,128)} %get-tuple-element.238, s32[]{:T(128)} %get-tuple-element.237, f32[4,256]{1,0:T(4,128)S(1)} %fusion.176, bf16[4,4,512,64]{2,3,1,0:T(8,128)(2,1)} %get-tuple-element.245, bf16[4,4,512,64]{2,3,1,0:T(8,128)(2,1)} %get-tuple-element.247, ...), kind=kOutput, calls=%fused_computation.26.clone.1 | convolution fusion | flops 136316416 | bytes 923648 | tf_op jit(solution)/shard_map/while/body/eval_jaxpr/htl,hld->thd/dot_general | solution.py:132
  238.9 1.9 fusion.176
  240.8 2.8 %fusion.177 = f32[4,256,4,64]{1,3,2,0:T(8,128)} fusion(f32[4,256,4,64]{1,3,2,0:T(8,128)} %get-tuple-element.238, s32[]{:T(128)} %get-tuple-element.237, f32[4,256]{1,0:T(4,128)S(1)} %fusion.176, bf16[4,4,512,64]{2,3,1,0:T(8,128)(2,1)} %get-tuple-element.245, bf16[4,4,512,64]{2,3,1,0:T(8,128)(2,1)} %get-tuple-element.247, ...), kind=kOutput, calls=%fused_computation.26.clone.1 | convolution fusion | flops 136316416 | bytes 923648 | tf_op jit(solution)/shard_map/while/body/eval_jaxpr/htl,hld->thd/dot_general | solution.py:132
  243.6 1.9 fusion.176
  245.5 2.8 %fusion.177 = f32[4,256,4,64]{1,3,2,0:T(8,128)} fusion(f32[4,256,4,64]{1,3,2,0:T(8,128)} %get-tuple-element.238, s32[]{:T(128)} %get-tuple-element.237, f32[4,256]{1,0:T(4,128)S(1)} %fusion.176, bf16[4,4,512,64]{2,3,1,0:T(8,128)(2,1)} %get-tuple-element.245, bf16[4,4,512,64]{2,3,1,0:T(8,128)(2,1)} %get-tuple-element.247, ...), kind=kOutput, calls=%fused_computation.26.clone.1 | convolution fusion | flops 136316416 | bytes 923648 | tf_op jit(solution)/shard_map/while/body/eval_jaxpr/htl,hld->thd/dot_general | solution.py:132
  248.3 1.9 fusion.176
  250.2 2.8 %fusion.177 = f32[4,256,4,64]{1,3,2,0:T(8,128)} fusion(f32[4,256,4,64]{1,3,2,0:T(8,128)} %get-tuple-element.238, s32[]{:T(128)} %get-tuple-element.237, f32[4,256]{1,0:T(4,128)S(1)} %fusion.176, bf16[4,4,512,64]{2,3,1,0:T(8,128)(2,1)} %get-tuple-element.245, bf16[4,4,512,64]{2,3,1,0:T(8,128)(2,1)} %get-tuple-element.247, ...), kind=kOutput, calls=%fused_computation.26.clone.1 | convolution fusion | flops 136316416 | bytes 923648 | tf_op jit(solution)/shard_map/while/body/eval_jaxpr/htl,hld->thd/dot_general | solution.py:132
  253.0 1.3 fusion.69
  (66 shorter events, 14.6 us)
Async XLA Ops:
  0.6 164.8 %copy-start = (bf16[256,1024]{1,0:T(8,128)(2,1)S(1)}, bf16[256,1024]{1,0:T(8,128)(2,1)}, u32[]{:S(2)}) copy-start(bf16[256,1024]{1,0:T(8,128)(2,1)} %param.11) | copy-start | bytes 1572868
  12.8 79.3 %copy-start.2 = (bf16[4,4,256,64]{2,3,1,0:T(8,128)(2,1)}, bf16[4,4,256,64]{2,3,1,0:T(8,128)(2,1)S(1)}, u32[]{:S(2)}) copy-start(bf16[4,4,256,64]{2,3,1,0:T(8,128)(2,1)S(1)} %get-tuple-element.251) | copy-start | bytes 1572868
  117.9 47.6 %copy-start.3 = (bf16[1024,256]{1,0:T(8,128)(2,1)S(1)}, bf16[1024,256]{1,0:T(8,128)(2,1)}, u32[]{:S(2)}) copy-start(bf16[1024,256]{1,0:T(8,128)(2,1)} %param.10) | copy-start | bytes 1572868
  118.8 23.3 %all-to-all-start.2 = ((bf16[16,2,128]{2,1,0:T(2,128)(2,1)}), bf16[16,2,128]{2,1,0:T(2,128)(2,1)S(1)}, u32[]{:S(2)}, u32[]{:S(2)}) async-start(bf16[16,2,128]{2,1,0:T(2,128)(2,1)} %reshape.113), calls=%async_computation.2 | async-start | bytes 16384 | tf_op jit(solution)/shard_map/all_to_all | solution.py:45
  142.9 21.3 %all-to-all-start.1 = ((bf16[16,16,1024]{2,1,0:T(8,128)(2,1)}), bf16[16,16,1024]{2,1,0:T(8,128)(2,1)S(1)}, u32[]{:S(2)}, u32[]{:S(2)}) async-start(bf16[16,16,1024]{2,1,0:T(8,128)(2,1)} %broadcast_in_dim.46), calls=%async_computation.1 | async-start | bytes 1048576 | tf_op jit(solution)/shard_map/all_to_all | solution.py:45
  186.1 33.2 %copy-start.4 = (bf16[16,1024]{1,0:T(8,128)(2,1)}, bf16[16,1024]{1,0:T(8,128)(2,1)S(1)}, u32[]{:S(2)}) copy-start(bf16[16,1024]{1,0:T(8,128)(2,1)S(1)} %add_convert_fusion) | copy-start | bytes 98308
  187.2 31.9 %all-to-all-start.4 = ((bf16[32,16,1024]{2,1,0:T(8,128)(2,1)}), bf16[32,16,1024]{2,1,0:T(8,128)(2,1)S(1)}, u32[]{:S(2)}, u32[]{:S(2)}) async-start(bf16[32,16,1024]{2,1,0:T(8,128)(2,1)} %broadcast_in_dim.49), calls=%async_computation.4 | async-start | bytes 2097152 | tf_op jit(solution)/shard_map/all_to_all | solution.py:45
  219.1 1.0 copy-start.1
where the time goes:
time: 256 us; the launch traced here: 255 us
  blocking collectives  122 us (48%)
  waiting for transfers between devices  51.7 us (20%)
  matrix products  26.6 us (10%)
  starting transfers between devices  24.4 us (10%)
  local copies, waits for them, and re-layouts  19.1 us (7%)
  other arithmetic  10.4 us (4%)
    pmax x4, blocking collectives, by_axis(): shard = lax.pmax(shard, axis)  77.3 us
    all_to_all x3, waiting for transfers between devices, from_everyone(): return lax.all_to_all(copies, axis, split_axis=0, concat_axis=0, tiled=True)  51.7 us
    all_to_all x1, blocking collectives, summed_on_arrival(): tiles = lax.all_to_all(cut_along(shard, dim, size), axis, 0, 0, tiled=True)  25 us
    all_to_all x3, starting transfers between devices, from_everyone(): return lax.all_to_all(copies, axis, split_axis=0, concat_axis=0, tiled=True)  24.4 us
    all_to_all x1, blocking collectives, from_everyone(): return lax.all_to_all(copies, axis, split_axis=0, concat_axis=0, tiled=True)  19.9 us
    dot_general x4, matrix products, write_one_group(): jnp.einsum('htl,hld->thd', shares, value_part, preferred_element_type=jnp...  11.4 us
    sub x4, matrix products, write_one_group(): weights = jnp.exp(scores - jnp.max(scores, axis=-1, keepdims=True))  7.49 us
    while x2, local copies, waits for them, and re-layouts, write_tokens(): lax.map(write_one_group, (split_heads(keys_tok, head_count), split_heads(...  6.83 us
  transfers between devices with their start and end apart: 3, of which 3 were waited for; matrix products, arithmetic and copies ran while one was open for 0% of the time, Pallas kernels for 0%

commit v1 on v0

v1 whole, which is shorter than its diff:
```python
import functools
import math

import jax
import jax.numpy as jnp
from jax import lax
from jax.experimental import pallas as pl
from jax.experimental.pallas import tpu as pltpu
from jax.sharding import Mesh
from jax.sharding import PartitionSpec as P

H = 16
HD = 64
Z, CORE = "tm_0", "tm_1"
SPACE = ("space_0", "space_1")
TM = (Z, CORE)
TM_SPACE = TM + SPACE
epsilon = 1e-05
LOG2E = math.log2(math.e)
STATS = 128
f32, bf16 = jnp.float32, jnp.bfloat16
HIGHEST = lax.Precision.HIGHEST


def layer_norm(values):
    center = values - jnp.mean(values, axis=-1, keepdims=True)
    spread = jnp.mean(center * center, axis=-1, keepdims=True)
    return center * lax.rsqrt(spread + epsilon)


def cols_dot(a, b):
    return lax.dot_general(a, b, (((1,), (1,)), ((), ())), preferred_element_type=f32)


def attend(keys, queries, values_t, head, state):
    pair = pl.ds((head // 2) * 2 * HD, 2 * HD)
    query = queries[:, pair]
    lane = lax.broadcasted_iota(jnp.int32, query.shape, 1)
    query = jnp.where((lane >= HD) == (head % 2 == 1), query, jnp.zeros_like(query))
    scores = cols_dot(keys[:, pair], query) * (HD**-0.5 * LOG2E)
    peak = jnp.max(scores, axis=0, keepdims=True)
    if state is not None:
        peak = jnp.maximum(peak, state[0])
    weights = jnp.exp2(scores - peak)
    total = jnp.sum(weights, axis=0, keepdims=True)
    summed = jnp.dot(
        values_t[head * HD : (head + 1) * HD, :], weights.astype(bf16), preferred_element_type=f32
    )
    if state is not None:
        old = jnp.exp2(state[0] - peak)
        total = total + state[1] * old
        summed = summed + state[2] * old
    return peak, total, summed


def load_state(state, head):
    peaks, totals, sums = state
    return peaks[head : head + 1, :], totals[head : head + 1, :], sums[head * HD : (head + 1) * HD, :]


def read_first(tokens, latents, keys, peaks, totals, sums, values_t):
    value = tokens[...]
    keys[...] = layer_norm(value.astype(f32)).astype(bf16)
    values_t[...] = value.T
    for head in range(H):
        peak, total, summed = attend(keys, latents, values_t, head, None)
        peaks[head : head + 1, :] = peak
        totals[head : head + 1, :] = total
        sums[head * HD : (head + 1) * HD, :] = summed


def read_second(tokens, latents, peaks, totals, sums, packed, keys, values_t, packed_t):
    value = tokens[...]
    keys[...] = layer_norm(value.astype(f32)).astype(bf16)
    values_t[...] = value.T
    width = H * HD
    packed_t[width:, :] = jnp.zeros_like(packed_t[width:, :])
    for head in range(H):
        state = load_state((peaks, totals, sums), head)
        peak, total, summed = attend(keys, latents, values_t, head, state)
        sent = peak.astype(bf16).astype(f32)
        scale = jnp.exp2(peak - sent)
        packed_t[head * HD : (head + 1) * HD, :] = summed * scale
        packed_t[width + head : width + head + 1, :] = total * scale
        packed_t[width + H + head : width + H + head + 1, :] = sent
    packed[...] = packed_t[...].T.reshape(packed.shape).astype(bf16)


def expand(factor):
    head = lax.broadcasted_iota(jnp.int32, (H, H * HD), 0)
    lane = lax.broadcasted_iota(jnp.int32, (H, H * HD), 1)
    spread = (lane // HD == head).astype(f32)
    return jnp.dot(factor, spread, precision=HIGHEST, preferred_element_type=f32)


def combine(tiles):
    n, rows, _ = tiles.shape
    width = H * HD
    totals, peaks = tiles[:, :, width : width + H], tiles[:, :, width + H : width + 2 * H]
    peak = jnp.max(peaks, axis=0)
    factor = jnp.exp2(peaks - peak[None])
    total = jnp.sum(totals * factor, axis=0)
    wide = expand(factor.reshape(n * rows, H)).reshape(n, rows, width)
    return jnp.sum(tiles[:, :, :width] * wide, axis=0), total, peak


def combine_space(arrived, out):
    summed, total, peak = combine(arrived[...].astype(f32))
    rest = jnp.zeros((summed.shape[0], STATS - 2 * H), f32)
    tile = jnp.concatenate([summed, total, peak, rest], axis=1).astype(bf16)
    out[...] = jnp.broadcast_to(tile[None], out.shape)


def mlp(position, arrived, latents, up, down, out, middle_own):
    tiles = arrived[...].astype(f32)
    rows = tiles.shape[1]
    tiles = tiles.reshape(tiles.shape[0] // 2, 2 * rows, tiles.shape[2])
    summed, total, _ = combine(tiles)
    read_out = summed * expand(1.0 / total)
    middle = latents[...].astype(f32).reshape(2 * rows, H * HD) + read_out
    normed = layer_norm(middle).astype(bf16)
    hidden = jnp.dot(normed, up[...], preferred_element_type=f32)
    hidden = (0.5 * hidden * (1.0 + lax.erf(hidden * math.sqrt(0.5)))).astype(bf16)
    part = jnp.dot(hidden, down[...], preferred_element_type=f32)
    part = part.reshape(1, 2, rows, H * HD).astype(bf16)
    out[...] = jnp.broadcast_to(part, out.shape)
    middle_own[...] = jnp.where(position[1] == 0, middle[:rows], middle[rows:])


def finish(parts, middle, out):
    new = (middle[...] + jnp.sum(parts[...].astype(f32), axis=0)).astype(bf16)
    out[...] = jnp.broadcast_to(new[None], out.shape)


def prepare_write(latents, lat, values_t):
    new = latents[...].astype(f32)
    new = new.reshape(new.shape[0] * new.shape[1], new.shape[2])
    lat[...] = new.astype(bf16)
    values_t[...] = layer_norm(new).T.astype(bf16)


def write_first(latents, keys, peaks, totals, sums, lat, values_t):
    prepare_write(latents, lat, values_t)
    for head in range(H):
        peak, total, summed = attend(lat, keys, values_t, head, None)
        peaks[head : head + 1, :] = peak
        totals[head : head + 1, :] = total
        sums[head * HD : (head + 1) * HD, :] = summed


def write_second(latents, keys, tokens, peaks, totals, sums, out, lat, values_t, out_t):
    prepare_write(latents, lat, values_t)
    for head in range(H):
        state = load_state((peaks, totals, sums), head)
        _, total, summed = attend(lat, keys, values_t, head, state)
        out_t[head * HD : (head + 1) * HD, :] = summed * (1.0 / total)
    out[...] = (tokens[...].astype(f32) + out_t[...].T).astype(bf16)


def call(kernel, outs, scratch=(), in_specs=None, prefetch=0, flops=0, **kw):
    whole = pl.BlockSpec(memory_space=pltpu.VMEM)
    single = not isinstance(outs, (list, tuple))
    out_list = [outs] if single else list(outs)
    spec = dict(
        out_shape=outs,
        compiler_params=pltpu.CompilerParams(vmem_limit_bytes=48 << 20),
        name=kernel.__name__,
        cost_estimate=pl.CostEstimate(flops=flops, transcendentals=flops // 256, bytes_accessed=1 << 20),
    )
    if prefetch:
        grid_spec = pltpu.PrefetchScalarGridSpec(
            num_scalar_prefetch=prefetch,
            grid=(1,),
            in_specs=in_specs,
            out_specs=whole if single else [whole] * len(out_list),
            scratch_shapes=list(scratch),
        )
        return pl.pallas_call(kernel, grid_spec=grid_spec, **spec)
    return pl.pallas_call(
        kernel,
        in_specs=[whole] * in_specs,
        out_specs=whole if single else [whole] * len(out_list),
        scratch_shapes=list(scratch),
        **spec,
    )


def on_device(tokens, latents, up_weight, down_weight):
    shape = jax.ShapeDtypeStruct
    n_space, n_z = lax.axis_size(SPACE), lax.axis_size(Z)
    count, width = tokens.shape
    half = latents.shape[0] // 2
    rows = half // n_space
    core, place = lax.axis_index(CORE), lax.axis_index(SPACE)
    heavy = 4 * half * count * width

    other = lax.ppermute(tokens, CORE, [(0, 1), (1, 0)])
    own = lax.dynamic_slice_in_dim(latents, core * half, half, 0)
    state = [shape((H, half), f32), shape((H, half), f32), shape((width, half), f32)]
    keys, *part = call(
        read_first,
        [shape((count, width), bf16), *state],
        [pltpu.VMEM((width, count), bf16)],
        in_specs=2,
        flops=heavy,
    )(tokens, own)
    packed = call(
        read_second,
        shape((n_space, rows, width + STATS), bf16),
        [
            pltpu.VMEM((count, width), bf16),
            pltpu.VMEM((width, count), bf16),
            pltpu.VMEM((width + STATS, half), f32),
        ],
        in_specs=5,
        flops=heavy,
    )(other, own, *part)
    packed = lax.all_to_all(packed, SPACE, 0, 0, tiled=True)
    tiles = call(combine_space, shape((2 * n_z, rows, width + STATS), bf16), in_specs=1)(packed)
    tiles = lax.all_to_all(tiles, TM, 0, 0, tiled=True)
    whole = pl.BlockSpec(memory_space=pltpu.VMEM)
    parts, middle = call(
        mlp,
        [shape((n_z, 2, rows, width), bf16), shape((rows, width), f32)],
        in_specs=[
            whole,
            pl.BlockSpec((2, 1, rows, width), lambda i, position: (0, position[0], 0, 0)),
            whole,
            whole,
        ],
        prefetch=1,
    )(
        jnp.stack([place, core]).astype(jnp.int32),
        tiles,
        latents.reshape(2, n_space, rows, width),
        up_weight,
        down_weight,
    )
    parts = lax.all_to_all(parts.reshape(2 * n_z, rows, width), TM, 0, 0, tiled=True)
    new = call(finish, shape((n_space, rows, width), bf16), in_specs=2)(parts, middle)
    mine = lax.all_to_all(new, SPACE, 0, 0, tiled=True)
    theirs = lax.ppermute(mine, CORE, [(0, 1), (1, 0)])
    work = [pltpu.VMEM((half, width), bf16), pltpu.VMEM((width, half), bf16)]
    state = [shape((H, count), f32), shape((H, count), f32), shape((width, count), f32)]
    part = call(write_first, state, work, in_specs=2, flops=heavy)(mine, keys)
    new_tokens = call(
        write_second,
        shape((count, width), bf16),
        [*work, pltpu.VMEM((width, count), f32)],
        in_specs=6,
        flops=heavy,
    )(theirs, keys, tokens, *part)
    owned = half * 2 // n_space
    first = place * owned
    source = jnp.where((first >= half) == (core == 1), mine.reshape(half, width), theirs.reshape(half, width))
    new_latents = lax.dynamic_slice_in_dim(source, first % half, owned, 0)
    return (new_tokens, new_latents)


def solution(mesh):
    tm, space = mesh.shape["tm"], mesh.shape["space"]
    split = Mesh(
        mesh.devices.reshape(tm // 2, 2, space // 4, 4), ("tm_0", "tm_1", "space_0", "space_1")
    )
    in_specs = (P(TM_SPACE, None), P(), P(None, TM), P(TM, None))
    out_specs = (P(TM_SPACE, None), P(SPACE, None))
    return jax.shard_map(
        on_device, mesh=split, in_specs=in_specs, out_specs=out_specs, check_vma=False
    )
```

time: 256 us -> 122 us (0.48)
  blocking collectives: 122 us -> 58.4 us
  waiting for transfers between devices: 51.7 us -> 12.2 us
  matrix products: 26.6 us -> 0 us
  Pallas kernels: 0 us -> 24.7 us
  local copies, waits for them, and re-layouts: 19.1 us -> 1.83 us
  other arithmetic: 10.4 us -> 0.14 us
    pmax x4 -> x0, blocking collectives: 77.3 us -> none  [by_axis(): shard = lax.pmax(shard, axis)]
    all_to_all x3 -> x1, waiting for transfers between devices: 51.7 us -> 12.2 us  [on_device(): tiles = lax.all_to_all(tiles, TM, 0, 0, tiled=True)]
    pallas_call x0 -> x7, Pallas kernels: none -> 24.7 us  [the longest x1 5.86 us: on_device(): call(write_second, shape((count, width), bf16), [*work, pltpu.VMEM((width...]
    dot_general x13 -> x0, matrix products: 19.1 us -> none  [the longest x4 11.4 us: write_one_group(): jnp.einsum('htl,hld->thd', shares, value_part, preferred_element_type=jnp...]
    all_to_all x2 -> x3, blocking collectives: 45 us -> 58.4 us  [the longest x1 22.3 us: on_device(): packed = lax.all_to_all(packed, SPACE, 0, 0, tiled=True)]
    all_to_all x3 -> x1, starting transfers between devices: 24.4 us -> 12.4 us  [on_device(): tiles = lax.all_to_all(tiles, TM, 0, 0, tiled=True)]
    ppermute x0 -> x2, starting transfers between devices: none -> 11.4 us  [the longest x1 8.75 us: on_device(): other = lax.ppermute(tokens, CORE, [(0, 1), (1, 0)])]
    sub x4 -> x0, matrix products: 7.49 us -> none  [write_one_group(): weights = jnp.exp(scores - jnp.max(scores, axis=-1, keepdims=True))]
  transfers between devices with their start and end apart: 3 -> 3, of which waited for: 3 -> 1; matrix products, arithmetic and copies ran while one was open for 0% -> 1% of each run, Pallas kernels for 0% -> 8%
where the time goes in v1:
time: 122 us
  blocking collectives  58.4 us (48%)
  Pallas kernels  24.7 us (20%)
  starting transfers between devices  23.8 us (20%)
  waiting for transfers between devices  12.2 us (10%)
  local copies, waits for them, and re-layouts  1.83 us (2%)
    all_to_all x1, blocking collectives, on_device(): packed = lax.all_to_all(packed, SPACE, 0, 0, tiled=True)  22.3 us
    all_to_all x1, blocking collectives, on_device(): mine = lax.all_to_all(new, SPACE, 0, 0, tiled=True)  21.7 us
    all_to_all x1, blocking collectives, on_device(): lax.all_to_all(parts.reshape(2 * n_z, rows, width), TM, 0, 0, tiled=True)  14.4 us
    all_to_all x1, starting transfers between devices, on_device(): tiles = lax.all_to_all(tiles, TM, 0, 0, tiled=True)  12.4 us
    all_to_all x1, waiting for transfers between devices, on_device(): tiles = lax.all_to_all(tiles, TM, 0, 0, tiled=True)  12.2 us
    ppermute x1, starting transfers between devices, on_device(): other = lax.ppermute(tokens, CORE, [(0, 1), (1, 0)])  8.75 us
    pallas_call x1, Pallas kernels, on_device(): call(write_second, shape((count, width), bf16), [*work, pltpu.VMEM((width...  5.86 us
    pallas_call x1, Pallas kernels, on_device(): call(read_second, shape((n_space, rows, width + STATS), bf16), [pltpu.VME...  5.18 us
  transfers between devices with their start and end apart: 3, of which 1 were waited for; matrix products, arithmetic and copies ran while one was open for 1% of the time, Pallas kernels for 8%

profile of v1, /device:TPU:1, one launch (start us, length us, event | category | flops | bytes accessed | tf_op | source)
XLA Modules:
  0.0 121.8 jit_solution(3390405766897494368)
XLA Ops:
  0.6 8.7 %collective-permute-start = (bf16[256,1024]{1,0:T(8,128)(2,1)}, bf16[256,1024]{1,0:T(8,128)(2,1)S(1)}, u32[]{:S(2)}, u32[]{:S(2)}) collective-permute-start(bf16[256,1024]{1,0:T(8,128)(2,1)} %tokens.3), channel_id=1, source_target_pairs={{0,32},{32,0},{1,33},{33,1},{2,34},{34,2},{3,35},{35,3},{4,36},{36... | collective-permute-start | bytes 1572872 | tf_op jit(solution)/shard_map/ppermute | solution.py:197
  9.4 0.0 copy-start.1
  9.4 1.1 constant_dynamic-slice_fusion.1.latents
  10.5 0.0 copy-done.1
  10.6 5.0 %read_first.1 = (bf16[256,1024]{1,0:T(8,128)(2,1)S(1)}, f32[16,256]{1,0:T(8,128)S(1)}, f32[16,256]{1,0:T(8,128)S(1)}, f32[1024,256]{1,0:T(8,128)S(1)}) custom-call(bf16[256,1024]{1,0:T(8,128)(2,1)S(1)} %copy-done.1, bf16[256,1024]{1,0:T(8,128)(2,1)S(1)} %constant_dynamic-slice_fusion.1.latents), custom_call_target="tpu_custom_call" | custom-call | flops 268435456 | bytes 1048576 | tf_op jit(solution)/shard_map/read_first/pallas_call | solution.py:200
  15.6 0.0 collective-permute-done.tokens
  15.7 5.2 %read_second.1 = bf16[32,8,1152]{2,1,0:T(8,128)(2,1)S(1)} custom-call(bf16[256,1024]{1,0:T(8,128)(2,1)S(1)} %collective-permute-done.tokens, bf16[256,1024]{1,0:T(8,128)(2,1)S(1)} %constant_dynamic-slice_fusion.1.latents, f32[16,256]{1,0:T(8,128)S(1)} %get-tuple-element.11.peaks, f32[16,256]{1,0:T(8,128)S(1)} %get-tuple-element.12.totals, ...), custom_call_target="tpu_custom_call" | custom-call | flops 268435456 | bytes 1048576 | tf_op jit(solution)/shard_map/read_second/pallas_call | solution.py:207
  20.8 0.0 copy-start
  20.9 22.3 %all_to_all.20.arrived = bf16[32,8,1152]{2,1,0:T(8,128)(2,1)S(1)} all-to-all(bf16[32,8,1152]{2,1,0:T(8,128)(2,1)S(1)} %read_second.1), channel_id=1, replica_groups=mesh['tm_0'=8,'tm_1'=2,'space_0'=8,'space_1'=4] {'space_0','space_1'}, dimensions={0} | all-to-all | bytes 1179648 | tf_op jit(solution)/shard_map/all_to_all | solution.py:218
  43.1 0.0 copy-start.3
  43.1 1.8 %combine_space.1 = bf16[16,8,1152]{2,1,0:T(8,128)(2,1)} custom-call(bf16[32,8,1152]{2,1,0:T(8,128)(2,1)S(1)} %all_to_all.20.arrived), custom_call_target="tpu_custom_call" | custom-call | bytes 1048576 | tf_op jit(solution)/shard_map/combine_space/pallas_call | solution.py:219
  44.9 0.0 copy-start.2
  44.9 12.4 %all-to-all-start.1 = ((bf16[16,8,1152]{2,1,0:T(8,128)(2,1)}), bf16[16,8,1152]{2,1,0:T(8,128)(2,1)S(1)}, u32[]{:S(2)}, u32[]{:S(2)}) async-start(bf16[16,8,1152]{2,1,0:T(8,128)(2,1)} %combine_space.1), calls=%async_computation.1 | async-start | bytes 589824 | tf_op jit(solution)/shard_map/all_to_all | solution.py:220
  57.3 0.1 pad_add_fusion.position
  57.4 12.2 %all-to-all-done.1.arrived = bf16[16,8,1152]{2,1,0:T(8,128)(2,1)S(1)} async-done(((bf16[16,8,1152]{2,1,0:T(8,128)(2,1)}), bf16[16,8,1152]{2,1,0:T(8,128)(2,1)S(1)}, u32[]{:S(2)}, u32[]{:S(2)}) %all-to-all-start.1) | async-done | bytes 294944 | tf_op jit(solution)/shard_map/all_to_all | solution.py:220
  69.6 0.0 copy-done
  69.6 0.0 copy-done.3
  69.6 0.0 copy-done.2
  69.6 1.8 %mlp.1 = (bf16[8,2,8,1024]{3,2,1,0:T(8,128)(2,1)S(1)}, f32[8,1024]{1,0:T(8,128)S(1)}) custom-call(s32[2]{0:T(128)S(1)} %pad_add_fusion.position, bf16[16,8,1152]{2,1,0:T(8,128)(2,1)S(1)} %all-to-all-done.1.arrived, bf16[2,32,8,1024]{3,2,1,0:T(8,128)(2,1)S(1)} %bitcast.6, bf16[1024,256]{1,0:T(8,128)(2,1)S(1)} %copy-done.2, bf16[256,1024]{1,0:T(8,128)(2,1)S(1)} %copy-done.3), custom_call_target="tpu_custom_call" | custom-call | bytes 1048576 | tf_op jit(solution)/shard_map/mlp/pallas_call | solution.py:222
  71.5 14.4 %all_to_all.21.parts = bf16[16,8,1024]{2,1,0:T(8,128)(2,1)S(1)} all-to-all(bf16[16,8,1024]{2,1,0:T(8,128)(2,1)S(1)} %bitcast.7), channel_id=1, replica_groups=mesh['tm_0'=8,'tm_1'=2,'space_0'=8,'space_1'=4] {'tm_0','tm_1'}, dimensions={0} | all-to-all | bytes 524288 | tf_op jit(solution)/shard_map/all_to_all | solution.py:239
  85.9 0.1 finish.1
  85.9 21.7 %all_to_all.22.latents = bf16[32,8,1024]{2,1,0:T(8,128)(2,1)S(1)} all-to-all(bf16[32,8,1024]{2,1,0:T(8,128)(2,1)S(1)} %finish.1), channel_id=1, replica_groups=mesh['tm_0'=8,'tm_1'=2,'space_0'=8,'space_1'=4] {'space_0','space_1'}, dimensions={0} | all-to-all | bytes 1048576 | tf_op jit(solution)/shard_map/all_to_all | solution.py:241
  107.6 2.7 %collective-permute-start.1 = (bf16[32,8,1024]{2,1,0:T(8,128)(2,1)S(1)}, bf16[32,8,1024]{2,1,0:T(8,128)(2,1)S(1)}, u32[]{:S(2)}, u32[]{:S(2)}) collective-permute-start(bf16[32,8,1024]{2,1,0:T(8,128)(2,1)S(1)} %all_to_all.22.latents), channel_id=1, source_target_pairs={{0,32},{32,0},{1,33},{33,1},{2,34},{34,2},{3,35},{35,3},{4,36},{36... | collective-permute-start | bytes 1572872 | tf_op jit(solution)/shard_map/ppermute | solution.py:242
  110.3 4.9 %write_first.1 = (f32[16,256]{1,0:T(8,128)S(1)}, f32[16,256]{1,0:T(8,128)S(1)}, f32[1024,256]{1,0:T(8,128)S(1)}) custom-call(bf16[32,8,1024]{2,1,0:T(8,128)(2,1)S(1)} %all_to_all.22.latents, bf16[256,1024]{1,0:T(8,128)(2,1)S(1)} %get-tuple-element.16.keys), custom_call_target="tpu_custom_call" | custom-call | flops 268435456 | bytes 1048576 | tf_op jit(solution)/shard_map/write_first/pallas_call | solution.py:245
  115.2 0.0 collective-permute-done.1.latents
  115.2 0.1 select_bitcast_fusion
  115.3 0.6 constant_dynamic-slice_fusion
  115.9 5.9 %write_second.1 = bf16[256,1024]{1,0:T(8,128)(2,1)} custom-call(bf16[32,8,1024]{2,1,0:T(8,128)(2,1)S(1)} %collective-permute-done.1.latents, bf16[256,1024]{1,0:T(8,128)(2,1)S(1)} %get-tuple-element.16.keys, bf16[256,1024]{1,0:T(8,128)(2,1)S(1)} %copy-done.1, f32[16,256]{1,0:T(8,128)S(1)} %get-tuple-element.17.peaks, ...), custom_call_target="tpu_custom_call" | custom-call | flops 268435456 | bytes 1048576 | tf_op jit(solution)/shard_map/write_second/pallas_call | solution.py:246
Async XLA Ops:
  0.6 15.0 %collective-permute-start = (bf16[256,1024]{1,0:T(8,128)(2,1)}, bf16[256,1024]{1,0:T(8,128)(2,1)S(1)}, u32[]{:S(2)}, u32[]{:S(2)}) collective-permute-start(bf16[256,1024]{1,0:T(8,128)(2,1)} %tokens.3), channel_id=1, source_target_pairs={{0,32},{32,0},{1,33},{33,1},{2,34},{34,2},{3,35},{35,3},{4,36},{36... | collective-permute-start | bytes 1572872 | tf_op jit(solution)/shard_map/ppermute | solution.py:197
  9.4 1.2 copy-start.1
  20.8 48.8 %copy-start = (bf16[512,1024]{1,0:T(8,128)(2,1)S(1)}, bf16[512,1024]{1,0:T(8,128)(2,1)}, u32[]{:S(2)}) copy-start(bf16[512,1024]{1,0:T(8,128)(2,1)} %param.5) | copy-start | bytes 3145732
  43.1 26.5 %copy-start.3 = (bf16[256,1024]{1,0:T(8,128)(2,1)S(1)}, bf16[256,1024]{1,0:T(8,128)(2,1)}, u32[]{:S(2)}) copy-start(bf16[256,1024]{1,0:T(8,128)(2,1)} %down.1) | copy-start | bytes 1572868
  44.9 24.7 %copy-start.2 = (bf16[1024,256]{1,0:T(8,128)(2,1)S(1)}, bf16[1024,256]{1,0:T(8,128)(2,1)}, u32[]{:S(2)}) copy-start(bf16[1024,256]{1,0:T(8,128)(2,1)} %up.1) | copy-start | bytes 1572868
  44.9 24.7 %all-to-all-start.1 = ((bf16[16,8,1152]{2,1,0:T(8,128)(2,1)}), bf16[16,8,1152]{2,1,0:T(8,128)(2,1)S(1)}, u32[]{:S(2)}, u32[]{:S(2)}) async-start(bf16[16,8,1152]{2,1,0:T(8,128)(2,1)} %combine_space.1), calls=%async_computation.1 | async-start | bytes 589824 | tf_op jit(solution)/shard_map/all_to_all | solution.py:220
  107.6 7.6 %collective-permute-start.1 = (bf16[32,8,1024]{2,1,0:T(8,128)(2,1)S(1)}, bf16[32,8,1024]{2,1,0:T(8,128)(2,1)S(1)}, u32[]{:S(2)}, u32[]{:S(2)}) collective-permute-start(bf16[32,8,1024]{2,1,0:T(8,128)(2,1)S(1)} %all_to_all.22.latents), channel_id=1, source_target_pairs={{0,32},{32,0},{1,33},{33,1},{2,34},{34,2},{3,35},{35,3},{4,36},{36... | collective-permute-start | bytes 1572872 | tf_op jit(solution)/shard_map/ppermute | solution.py:242

commit v2 on v1

v2 whole, which is shorter than its diff:
```python
import functools
import math

import jax
import jax.numpy as jnp
from jax import lax
from jax.experimental import pallas as pl
from jax.experimental.pallas import tpu as pltpu
from jax.sharding import Mesh
from jax.sharding import PartitionSpec as P

H = 16
HD = 64
WIDTH = H * HD
Z, CORE = "tm_0", "tm_1"
SPACE = ("space_0", "space_1")
TM = (Z, CORE)
TM_SPACE = TM + SPACE
epsilon = 1e-05
SCALE = HD**-0.5 * math.log2(math.e)
STATS = 128
ONES = 16
SLOTS = 3
CHUNK = 64
f32, bf16 = jnp.float32, jnp.bfloat16


def layer_norm(values):
    center = values - jnp.mean(values, axis=-1, keepdims=True)
    spread = jnp.mean(center * center, axis=-1, keepdims=True)
    return center * lax.rsqrt(spread + epsilon)


def put_values(values_t, values):
    rows = values.shape[0]
    for pair in range(H // 2):
        part = values[:, 2 * HD * pair : 2 * HD * (pair + 1)].T
        for side in range(2):
            values_t[2 * pair + side, :HD, :] = part[side * HD : (side + 1) * HD, :]
    for head in range(H):
        values_t[head, HD:, :] = jnp.ones((ONES, rows), bf16)


def attend(keys, queries, values_t, scores, weights, old_peak, emit):
    peaks = {}

    def score(head):
        pair = slice((head // 2) * 2 * HD, (head // 2 + 1) * 2 * HD)
        query = queries(pair)
        lane = lax.broadcasted_iota(jnp.int32, query.shape, 1)
        query = jnp.where((lane >= HD) == (head % 2 == 1), query, jnp.zeros_like(query))
        found = lax.dot_general(
            keys[:, pair], query, (((1,), (1,)), ((), ())), preferred_element_type=f32
        )
        scores[head % SLOTS] = found
        peak = jnp.max(found, axis=0, keepdims=True) * SCALE
        peaks[head] = peak if old_peak is None else jnp.maximum(peak, old_peak(head))

    def weigh(head):
        peak = jnp.broadcast_to(peaks[head], (CHUNK, peaks[head].shape[1]))
        for at in range(0, scores.shape[1], CHUNK):
            rows = slice(at, at + CHUNK)
            weights[head % SLOTS, rows, :] = jnp.exp2(scores[head % SLOTS, rows, :] * SCALE - peak).astype(bf16)

    def apply(head):
        summed = jnp.dot(values_t[head], weights[head % SLOTS], preferred_element_type=f32)
        emit(head, peaks[head], summed[:HD], summed[HD : HD + 1])

    for step in range(H + 2):
        if step < H:
            score(step)
        if 0 <= step - 1 < H:
            weigh(step - 1)
        if 0 <= step - 2 < H:
            apply(step - 2)


def keep_in(peaks, totals, sums):
    def emit(head, peak, summed, total):
        peaks[head : head + 1, :] = peak
        totals[head : head + 1, :] = total
        sums[head * HD : (head + 1) * HD, :] = summed

    return emit


def joined(peaks, totals, sums, then):
    def emit(head, peak, summed, total):
        old = jnp.exp2(peaks[head : head + 1, :] - peak)
        total = total + totals[head : head + 1, :] * old
        then(head, peak, summed + sums[head * HD : (head + 1) * HD, :] * old, total)

    return emit


def half_of(latents, core, half):
    return lambda pair: latents[pl.ds(pl.multiple_of(core * half, half), half), pair]


def read_first(position, tokens, latents, keys, peaks, totals, sums, values_t, scores, weights):
    value = tokens[...]
    keys[...] = layer_norm(value.astype(f32)).astype(bf16)
    put_values(values_t, value)
    queries = half_of(latents, position[1], latents.shape[0] // 2)
    attend(keys, queries, values_t, scores, weights, None, keep_in(peaks, totals, sums))


def read_second(position, tokens, latents, peaks, totals, sums, packed, keys, values_t, scores, weights, stats):
    value = tokens[...]
    keys[...] = layer_norm(value.astype(f32)).astype(bf16)
    put_values(values_t, value)
    queries = half_of(latents, position[1], latents.shape[0] // 2)
    tiles, rows, _ = packed.shape
    stats[...] = jnp.zeros_like(stats)
    held = {}

    def pack(part):
        return part.T.reshape(tiles, rows, part.shape[0]).astype(bf16)

    def then(head, peak, summed, total):
        sent = peak.astype(bf16).astype(f32)
        scale = jnp.exp2(peak - sent)
        stats[head : head + 1, :] = total * scale
        stats[H + head : H + head + 1, :] = sent
        held[head] = summed * scale
        if head % 2 == 1:
            both = jnp.concatenate([held[head - 1], held[head]], axis=0)
            packed[:, :, (head - 1) * HD : (head + 1) * HD] = pack(both)

    attend(
        keys, queries, values_t, scores, weights,
        lambda head: peaks[head : head + 1, :],
        joined(peaks, totals, sums, then),
    )
    packed[:, :, WIDTH:] = pack(stats[...])


def expand(factor):
    high = factor.astype(bf16)
    rest = factor - high.astype(f32)
    middle = rest.astype(bf16)
    low = (rest - middle.astype(f32)).astype(bf16)
    head = lax.broadcasted_iota(jnp.int32, (3 * H, WIDTH), 0)
    lane = lax.broadcasted_iota(jnp.int32, (3 * H, WIDTH), 1)
    spread = jnp.where(lax.rem(head, H) == lax.div(lane, HD), 1.0, 0.0).astype(bf16)
    return jnp.dot(
        jnp.concatenate([high, middle, low], axis=1), spread, preferred_element_type=f32
    )


def combine(tiles):
    n, rows, _ = tiles.shape
    totals, peaks = tiles[:, :, WIDTH : WIDTH + H], tiles[:, :, WIDTH + H : WIDTH + 2 * H]
    peak = jnp.max(peaks, axis=0)
    factor = jnp.exp2(peaks - peak[None])
    total = jnp.sum(totals * factor, axis=0)
    wide = expand(factor.reshape(n * rows, H)).reshape(n, rows, WIDTH)
    return jnp.sum(tiles[:, :, :WIDTH] * wide, axis=0), total, peak


def combine_space(arrived, out):
    summed, total, peak = combine(arrived[...].astype(f32))
    rest = jnp.zeros((summed.shape[0], STATS - 2 * H), f32)
    tile = jnp.concatenate([summed, total, peak, rest], axis=1).astype(bf16)
    out[...] = jnp.broadcast_to(tile[None], out.shape)


def mlp(position, arrived, latents, up, down, up_other, down_other, out, middle):
    summed, total, _ = combine(arrived[...].astype(f32))
    own = latents[position[1], position[0]].astype(f32)
    middle[...] = own + summed * expand(1.0 / total)
    normed = layer_norm(middle[...]).astype(bf16)
    part = None
    for rise, fall in ((up, down), (up_other, down_other)):
        hidden = jnp.dot(normed, rise[...], preferred_element_type=f32)
        hidden = (0.5 * hidden * (1.0 + lax.erf(hidden * math.sqrt(0.5)))).astype(bf16)
        term = jnp.dot(hidden, fall[...], preferred_element_type=f32)
        part = term if part is None else part + term
    out[...] = jnp.broadcast_to(part.astype(bf16)[None], out.shape)


def finish(parts, middle, out):
    new = (middle[...] + jnp.sum(parts[...].astype(f32), axis=0)).astype(bf16)
    out[...] = jnp.broadcast_to(new[None], out.shape)


def prepare_write(latents, lat, values_t):
    new = latents[...].astype(f32)
    new = new.reshape(new.shape[0] * new.shape[1], new.shape[2])
    lat[...] = new.astype(bf16)
    put_values(values_t, layer_norm(new).astype(bf16))


def write_first(latents, keys, peaks, totals, sums, lat, values_t, scores, weights):
    prepare_write(latents, lat, values_t)
    attend(
        lat, lambda pair: keys[:, pair], values_t, scores, weights, None,
        keep_in(peaks, totals, sums),
    )


def write_second(
    position, latents, mine, keys, tokens, peaks, totals, sums, out, owned, lat, values_t, scores, weights
):
    prepare_write(latents, lat, values_t)
    per = owned.shape[0]
    first = position[0] * per
    tiles = latents.shape[0]
    start = lax.rem(first, tiles)
    theirs = (lax.div(first, tiles) == position[1]).astype(jnp.int32) == 0

    @pl.when(theirs)
    def _():
        owned[...] = latents[pl.ds(start, per)]

    @pl.when(jnp.logical_not(theirs))
    def _():
        owned[...] = mine[pl.ds(start, per)]

    held = {}

    def then(head, peak, summed, total):
        held[head] = summed * (1.0 / total)
        if head % 2 == 1:
            both = jnp.concatenate([held[head - 1], held[head]], axis=0)
            pair = slice((head - 1) * HD, (head + 1) * HD)
            out[:, pair] = (tokens[:, pair].astype(f32) + both.T).astype(bf16)

    attend(
        lat, lambda pair: keys[:, pair], values_t, scores, weights,
        lambda head: peaks[head : head + 1, :],
        joined(peaks, totals, sums, then),
    )


def call(kernel, outs, scratch=(), inputs=1, scalars=False, flops=0):
    whole = pl.BlockSpec(memory_space=pltpu.VMEM)
    single = not isinstance(outs, (list, tuple))
    specs = [whole] * inputs
    if scalars:
        specs = [pl.BlockSpec(memory_space=pltpu.SMEM)] + specs
    return pl.pallas_call(
        kernel,
        out_shape=outs,
        in_specs=specs,
        out_specs=whole if single else [whole] * len(outs),
        scratch_shapes=list(scratch),
        compiler_params=pltpu.CompilerParams(vmem_limit_bytes=48 << 20),
        name=kernel.__name__,
        cost_estimate=pl.CostEstimate(flops=flops, transcendentals=flops // 256, bytes_accessed=1 << 20),
    )


def on_device(tokens, latents, up_weight, down_weight):
    shape = jax.ShapeDtypeStruct
    n_space, n_z = lax.axis_size(SPACE), lax.axis_size(Z)
    count, width = tokens.shape
    half = latents.shape[0] // 2
    rows = half // n_space
    core, place = lax.axis_index(CORE), lax.axis_index(SPACE)
    position = jnp.stack([place, core]).astype(jnp.int32)
    heavy = 4 * half * count * width
    swap = [(0, 1), (1, 0)]

    def work(keys, queries):
        return [
            pltpu.VMEM((H, HD + ONES, keys), bf16),
            pltpu.VMEM((SLOTS, keys, queries), f32),
            pltpu.VMEM((SLOTS, keys, queries), bf16),
        ]

    def state(queries):
        return [shape((H, queries), f32), shape((H, queries), f32), shape((width, queries), f32)]

    other = lax.ppermute(tokens, CORE, swap)
    keys, *part = call(
        read_first, [shape((count, width), bf16), *state(half)], work(count, half),
        inputs=2, scalars=True, flops=heavy,
    )(position, tokens, latents)
    packed = call(
        read_second,
        shape((n_space, rows, width + STATS), bf16),
        [pltpu.VMEM((count, width), bf16), *work(count, half), pltpu.VMEM((STATS, half), f32)],
        inputs=5, scalars=True, flops=heavy,
    )(position, other, latents, *part)
    packed, up_late, down_late = lax.optimization_barrier((packed, up_weight, down_weight))
    packed = lax.all_to_all(packed, SPACE, 0, 0, tiled=True)
    up_other, down_other = lax.ppermute(up_late, CORE, swap), lax.ppermute(down_late, CORE, swap)
    tiles = call(combine_space, shape((n_z, rows, width + STATS), bf16))(packed)
    tiles = lax.all_to_all(tiles, Z, 0, 0, tiled=True)
    parts, middle = call(
        mlp, [shape((n_z, rows, width), bf16), shape((rows, width), f32)], inputs=6, scalars=True
    )(
        position, tiles, latents.reshape(2, n_space, rows, width),
        up_weight, down_weight, up_other, down_other,
    )
    parts = lax.all_to_all(parts, Z, 0, 0, tiled=True)
    new = call(finish, shape((n_space, rows, width), bf16), inputs=2)(parts, middle)
    mine = lax.all_to_all(new, SPACE, 0, 0, tiled=True)
    theirs = lax.ppermute(mine, CORE, swap)
    lat = pltpu.VMEM((half, width), bf16)
    part = call(write_first, state(count), [lat, *work(half, count)], inputs=2, flops=heavy)(mine, keys)
    new_tokens, new_latents = call(
        write_second,
        [shape((count, width), bf16), shape((2, rows, width), bf16)],
        [lat, *work(half, count)],
        inputs=7, scalars=True, flops=heavy,
    )(position, theirs, mine, keys, tokens, *part)
    return (new_tokens, new_latents.reshape(2 * rows, width))


def solution(mesh):
    tm, space = mesh.shape["tm"], mesh.shape["space"]
    split = Mesh(
        mesh.devices.reshape(tm // 2, 2, space // 4, 4), ("tm_0", "tm_1", "space_0", "space_1")
    )
    in_specs = (P(TM_SPACE, None), P(), P(None, TM), P(TM, None))
    out_specs = (P(TM_SPACE, None), P(SPACE, None))
    return jax.shard_map(
        on_device, mesh=split, in_specs=in_specs, out_specs=out_specs, check_vma=False
    )
```

time: 122 us -> 106 us (0.87)
  blocking collectives: 58.4 us -> 28 us
  starting transfers between devices: 23.8 us -> 35.8 us
  waiting for transfers between devices: 12.2 us -> 21.9 us
  Pallas kernels: 24.7 us -> 16.7 us
    all_to_all x2 -> x1, blocking collectives: 36.7 us -> 10.4 us  [on_device(): parts = lax.all_to_all(parts, Z, 0, 0, tiled=True)]
    ppermute x2 -> x4, starting transfers between devices: 11.4 us -> 21.3 us  [the longest x1 8.75 us: on_device(): other = lax.ppermute(tokens, CORE, swap)]
    all_to_all x1 -> x2, waiting for transfers between devices: 12.2 us -> 21.9 us  [the longest x1 13.7 us: on_device(): packed = lax.all_to_all(packed, SPACE, 0, 0, tiled=True)]
    pallas_call x6, Pallas kernels: 19.5 us -> 12.7 us  [the longest x1 4.2 us: on_device(): call(write_second, [shape((count, width), bf16), shape((2, rows, width),...]
    all_to_all x1, blocking collectives: 21.7 us -> 17.6 us  [on_device(): mine = lax.all_to_all(new, SPACE, 0, 0, tiled=True)]
    unnamed x8 -> x12, local copies, waits for them, and re-layouts: 0.07 us -> 2.28 us
    all_to_all x1 -> x2, starting transfers between devices: 12.4 us -> 14.5 us  [the longest x1 10.1 us: on_device(): tiles = lax.all_to_all(tiles, Z, 0, 0, tiled=True)]
    dynamic_slice x2 -> x0, local copies, waits for them, and re-layouts: 1.76 us -> none  [the longest x1 1.14 us: on_device(): own = lax.dynamic_slice_in_dim(latents, core * half, half, 0)]
  transfers between devices with their start and end apart: 3 -> 6, of which waited for: 1 -> 2; matrix products, arithmetic and copies ran while one was open for 1% -> 0% of each run, Pallas kernels for 8% -> 6%
where the time goes in v2:
time: 106 us
  starting transfers between devices  35.8 us (34%)
  blocking collectives  28 us (26%)
  waiting for transfers between devices  21.9 us (21%)
  Pallas kernels  16.7 us (16%)
  local copies, waits for them, and re-layouts  2.28 us (2%)
    all_to_all x1, blocking collectives, on_device(): mine = lax.all_to_all(new, SPACE, 0, 0, tiled=True)  17.6 us
    all_to_all x1, waiting for transfers between devices, on_device(): packed = lax.all_to_all(packed, SPACE, 0, 0, tiled=True)  13.7 us
    all_to_all x1, blocking collectives, on_device(): parts = lax.all_to_all(parts, Z, 0, 0, tiled=True)  10.4 us
    all_to_all x1, starting transfers between devices, on_device(): tiles = lax.all_to_all(tiles, Z, 0, 0, tiled=True)  10.1 us
    ppermute x1, starting transfers between devices, on_device(): other = lax.ppermute(tokens, CORE, swap)  8.75 us
    ppermute x1, starting transfers between devices, on_device(): theirs = lax.ppermute(mine, CORE, swap)  8.25 us
    all_to_all x1, waiting for transfers between devices, on_device(): tiles = lax.all_to_all(tiles, Z, 0, 0, tiled=True)  8.19 us
    all_to_all x1, starting transfers between devices, on_device(): packed = lax.all_to_all(packed, SPACE, 0, 0, tiled=True)  4.46 us
  transfers between devices with their start and end apart: 6, of which 2 were waited for; matrix products, arithmetic and copies ran while one was open for 0% of the time, Pallas kernels for 6%

profile of v2, /device:TPU:1, one launch (start us, length us, event | category | flops | bytes accessed | tf_op | source)
XLA Modules:
  0.0 105.5 jit_solution(9448684926804945458)
XLA Ops:
  0.6 8.7 %collective-permute-start = (bf16[256,1024]{1,0:T(8,128)(2,1)}, bf16[256,1024]{1,0:T(8,128)(2,1)S(1)}, u32[]{:S(2)}, u32[]{:S(2)}) collective-permute-start(bf16[256,1024]{1,0:T(8,128)(2,1)} %tokens.3), channel_id=1, source_target_pairs={{0,32},{32,0},{1,33},{33,1},{2,34},{34,2},{3,35},{35,3},{4,36},{36... | collective-permute-start | bytes 1572872 | tf_op jit(solution)/shard_map/ppermute | solution.py:275
  9.4 0.1 pad_add_fusion.position
  9.5 0.0 copy-start
  9.5 1.2 %copy-done = bf16[512,1024]{1,0:T(8,128)(2,1)S(1)} copy-done((bf16[512,1024]{1,0:T(8,128)(2,1)S(1)}, bf16[512,1024]{1,0:T(8,128)(2,1)}, u32[]{:S(2)}) %copy-start) | copy-done | bytes 1048600
  10.7 0.0 copy-start.4
  10.7 1.0 copy-done.4
  11.7 0.0 copy-start.1
  11.7 3.1 %read_first.1 = (bf16[256,1024]{1,0:T(8,128)(2,1)S(1)}, f32[16,256]{1,0:T(8,128)S(1)}, f32[16,256]{1,0:T(8,128)S(1)}, f32[1024,256]{1,0:T(8,128)S(1)}) custom-call(s32[2]{0:T(128)S(1)} %pad_add_fusion.position, bf16[256,1024]{1,0:T(8,128)(2,1)S(1)} %copy-done.4, bf16[512,1024]{1,0:T(8,128)(2,1)S(1)} %copy-done), custom_call_target="tpu_custom_call" | custom-call | flops 268435456 | bytes 1048576 | tf_op jit(solution)/shard_map/read_first/pallas_call | solution.py:276
  14.8 0.0 collective-permute-done.tokens
  14.8 0.0 copy-done.1
  14.8 4.0 %read_second.1 = bf16[32,8,1152]{2,1,0:T(8,128)(2,1)} custom-call(s32[2]{0:T(128)S(1)} %pad_add_fusion.position, bf16[256,1024]{1,0:T(8,128)(2,1)S(1)} %collective-permute-done.tokens, bf16[512,1024]{1,0:T(8,128)(2,1)S(1)} %copy-done.1, f32[16,256]{1,0:T(8,128)S(1)} %get-tuple-element.16.peaks, f32[16,256]{1,0:T(8,128)S(1)} %get-tuple-element.17.totals, ...), custom_call_target="tpu_custom_call" | custom-call | flops 268435456 | bytes 1048576 | tf_op jit(solution)/shard_map/read_second/pallas_call | solution.py:280
  18.8 4.5 %all-to-all-start = ((bf16[32,8,1152]{2,1,0:T(8,128)(2,1)}), bf16[32,8,1152]{2,1,0:T(8,128)(2,1)S(1)}, u32[]{:S(2)}, u32[]{:S(2)}) async-start(bf16[32,8,1152]{2,1,0:T(8,128)(2,1)} %read_second.1), calls=%async_computation | async-start | bytes 1179648 | tf_op jit(solution)/shard_map/all_to_all | solution.py:287
  23.3 0.0 copy-done.2
  23.3 2.2 %collective-permute-start.1 = (bf16[1024,256]{1,0:T(8,128)(2,1)S(1)}, bf16[1024,256]{1,0:T(8,128)(2,1)}, u32[]{:S(2)}, u32[]{:S(2)}) collective-permute-start(bf16[1024,256]{1,0:T(8,128)(2,1)S(1)} %copy-done.2), channel_id=1, source_target_pairs={{0,32},{32,0},{1,33},{33,1},{2,34},{34,2},{3,35},{35,3},{4,36},{36... | collective-permute-start | bytes 1572872 | tf_op jit(solution)/shard_map/ppermute | solution.py:288
  25.5 0.0 copy-done.3
  25.5 2.1 %collective-permute-start.2 = (bf16[256,1024]{1,0:T(8,128)(2,1)S(1)}, bf16[256,1024]{1,0:T(8,128)(2,1)}, u32[]{:S(2)}, u32[]{:S(2)}) collective-permute-start(bf16[256,1024]{1,0:T(8,128)(2,1)S(1)} %copy-done.3), channel_id=1, source_target_pairs={{0,32},{32,0},{1,33},{33,1},{2,34},{34,2},{3,35},{35,3},{4,36},{36... | collective-permute-start | bytes 1572872 | tf_op jit(solution)/shard_map/ppermute | solution.py:288
  27.7 13.7 %all-to-all-done.arrived = bf16[32,8,1152]{2,1,0:T(8,128)(2,1)S(1)} async-done(((bf16[32,8,1152]{2,1,0:T(8,128)(2,1)}), bf16[32,8,1152]{2,1,0:T(8,128)(2,1)S(1)}, u32[]{:S(2)}, u32[]{:S(2)}) %all-to-all-start) | async-done | bytes 589856 | tf_op jit(solution)/shard_map/all_to_all | solution.py:287
  41.3 1.0 combine_space.1
  42.4 10.1 %all-to-all-start.1 = ((bf16[8,8,1152]{2,1,0:T(8,128)(2,1)}), bf16[8,8,1152]{2,1,0:T(8,128)(2,1)S(1)}, u32[]{:S(2)}, u32[]{:S(2)}) async-start(bf16[8,8,1152]{2,1,0:T(8,128)(2,1)} %combine_space.1), calls=%async_computation.1 | async-start | bytes 294912 | tf_op jit(solution)/shard_map/all_to_all | solution.py:290
  52.4 0.0 collective-permute-done.1.up_other
  52.4 0.0 collective-permute-done.2.down_other
  52.4 8.2 %all-to-all-done.1.arrived = bf16[8,8,1152]{2,1,0:T(8,128)(2,1)S(1)} async-done(((bf16[8,8,1152]{2,1,0:T(8,128)(2,1)}), bf16[8,8,1152]{2,1,0:T(8,128)(2,1)S(1)}, u32[]{:S(2)}, u32[]{:S(2)}) %all-to-all-start.1) | async-done | bytes 147488 | tf_op jit(solution)/shard_map/all_to_all | solution.py:290
  60.6 2.1 %mlp.1 = (bf16[8,8,1024]{2,1,0:T(8,128)(2,1)S(1)}, f32[8,1024]{1,0:T(8,128)S(1)}) custom-call(s32[2]{0:T(128)S(1)} %pad_add_fusion.position, bf16[8,8,1152]{2,1,0:T(8,128)(2,1)S(1)} %all-to-all-done.1.arrived, bf16[2,32,8,1024]{3,2,1,0:T(8,128)(2,1)S(1)} %bitcast.4, bf16[1024,256]{1,0:T(8,128)(2,1)S(1)} %copy-done.2, bf16[256,1024]{1,0:T(8,128)(2,1)S(1)} %copy-done.3, ...), custom_call_target="tpu_custom_call" | custom-call | bytes 1048576 | tf_op jit(solution)/shard_map/mlp/pallas_call | solution.py:291
  62.7 10.4 %all_to_all.20.parts = bf16[8,8,1024]{2,1,0:T(8,128)(2,1)S(1)} all-to-all(bf16[8,8,1024]{2,1,0:T(8,128)(2,1)S(1)} %get-tuple-element.22), channel_id=1, replica_groups=mesh['tm_0'=8,'tm_1'=2,'space_0'=8,'space_1'=4] {'tm_0'}, dimensions={0} | all-to-all | bytes 262144 | tf_op jit(solution)/shard_map/all_to_all | solution.py:297
  73.1 0.1 finish.1
  73.2 17.6 %all_to_all.21.latents.mine = bf16[32,8,1024]{2,1,0:T(8,128)(2,1)S(1)} all-to-all(bf16[32,8,1024]{2,1,0:T(8,128)(2,1)S(1)} %finish.1), channel_id=1, replica_groups=mesh['tm_0'=8,'tm_1'=2,'space_0'=8,'space_1'=4] {'space_0','space_1'}, dimensions={0} | all-to-all | bytes 1048576 | tf_op jit(solution)/shard_map/all_to_all | solution.py:299
  90.8 8.2 %collective-permute-start.3 = (bf16[32,8,1024]{2,1,0:T(8,128)(2,1)S(1)}, bf16[32,8,1024]{2,1,0:T(8,128)(2,1)S(1)}, u32[]{:S(2)}, u32[]{:S(2)}) collective-permute-start(bf16[32,8,1024]{2,1,0:T(8,128)(2,1)S(1)} %all_to_all.21.latents.mine), channel_id=1, source_target_pairs={{0,32},{32,0},{1,33},{33,1},{2,34},{34,2},{3,35},{35,3},{4,36},{36... | collective-permute-start | bytes 1572872 | tf_op jit(solution)/shard_map/ppermute | solution.py:300
  99.1 0.0 copy-start.5
  99.1 2.2 %write_first.1 = (f32[16,256]{1,0:T(8,128)S(1)}, f32[16,256]{1,0:T(8,128)S(1)}, f32[1024,256]{1,0:T(8,128)S(1)}) custom-call(bf16[32,8,1024]{2,1,0:T(8,128)(2,1)S(1)} %all_to_all.21.latents.mine, bf16[256,1024]{1,0:T(8,128)(2,1)S(1)} %get-tuple-element.24.keys), custom_call_target="tpu_custom_call" | custom-call | flops 268435456 | bytes 1048576 | tf_op jit(solution)/shard_map/write_first/pallas_call | solution.py:302
  101.3 0.0 collective-permute-done.3.latents
  101.3 0.0 copy-done.5
  101.3 4.2 %write_second.1 = (bf16[256,1024]{1,0:T(8,128)(2,1)}, bf16[2,8,1024]{2,1,0:T(8,128)(2,1)}) custom-call(s32[2]{0:T(128)S(1)} %pad_add_fusion.position, bf16[32,8,1024]{2,1,0:T(8,128)(2,1)S(1)} %collective-permute-done.3.latents, bf16[32,8,1024]{2,1,0:T(8,128)(2,1)S(1)} %all_to_all.21.latents.mine, bf16[256,1024]{1,0:T(8,128)(2,1)S(1)} %get-tuple-element.24.keys, ...), custom_call_target="tpu_custom_call" | custom-call | flops 268435456 | bytes 1048576 | tf_op jit(solution)/shard_map/write_second/pallas_call | solution.py:303
  (2 shorter events, 0.0 us)
Async XLA Ops:
  0.6 14.2 %collective-permute-start = (bf16[256,1024]{1,0:T(8,128)(2,1)}, bf16[256,1024]{1,0:T(8,128)(2,1)S(1)}, u32[]{:S(2)}, u32[]{:S(2)}) collective-permute-start(bf16[256,1024]{1,0:T(8,128)(2,1)} %tokens.3), channel_id=1, source_target_pairs={{0,32},{32,0},{1,33},{33,1},{2,34},{34,2},{3,35},{35,3},{4,36},{36... | collective-permute-start | bytes 1572872 | tf_op jit(solution)/shard_map/ppermute | solution.py:275
  9.5 1.2 %copy-start = (bf16[512,1024]{1,0:T(8,128)(2,1)S(1)}, bf16[512,1024]{1,0:T(8,128)(2,1)}, u32[]{:S(2)}) copy-start(bf16[512,1024]{1,0:T(8,128)(2,1)} %latents.3) | copy-start | bytes 3145732
  10.7 1.0 copy-start.4
  11.7 3.1 %copy-start.1 = (bf16[512,1024]{1,0:T(8,128)(2,1)S(1)}, bf16[512,1024]{1,0:T(8,128)(2,1)}, u32[]{:S(2)}) copy-start(bf16[512,1024]{1,0:T(8,128)(2,1)} %latents.3) | copy-start | bytes 3145732
  18.8 4.5 %copy-start.2 = (bf16[1024,256]{1,0:T(8,128)(2,1)S(1)}, bf16[1024,256]{1,0:T(8,128)(2,1)}, u32[]{:S(2)}) copy-start(bf16[1024,256]{1,0:T(8,128)(2,1)} %up.1) | copy-start | bytes 1572868
  18.8 6.7 %copy-start.3 = (bf16[256,1024]{1,0:T(8,128)(2,1)S(1)}, bf16[256,1024]{1,0:T(8,128)(2,1)}, u32[]{:S(2)}) copy-start(bf16[256,1024]{1,0:T(8,128)(2,1)} %down.1) | copy-start | bytes 1572868
  18.8 22.5 %all-to-all-start = ((bf16[32,8,1152]{2,1,0:T(8,128)(2,1)}), bf16[32,8,1152]{2,1,0:T(8,128)(2,1)S(1)}, u32[]{:S(2)}, u32[]{:S(2)}) async-start(bf16[32,8,1152]{2,1,0:T(8,128)(2,1)} %read_second.1), calls=%async_computation | async-start | bytes 1179648 | tf_op jit(solution)/shard_map/all_to_all | solution.py:287
  23.3 29.1 %collective-permute-start.1 = (bf16[1024,256]{1,0:T(8,128)(2,1)S(1)}, bf16[1024,256]{1,0:T(8,128)(2,1)}, u32[]{:S(2)}, u32[]{:S(2)}) collective-permute-start(bf16[1024,256]{1,0:T(8,128)(2,1)S(1)} %copy-done.2), channel_id=1, source_target_pairs={{0,32},{32,0},{1,33},{33,1},{2,34},{34,2},{3,35},{35,3},{4,36},{36... | collective-permute-start | bytes 1572872 | tf_op jit(solution)/shard_map/ppermute | solution.py:288
  25.5 26.9 %collective-permute-start.2 = (bf16[256,1024]{1,0:T(8,128)(2,1)S(1)}, bf16[256,1024]{1,0:T(8,128)(2,1)}, u32[]{:S(2)}, u32[]{:S(2)}) collective-permute-start(bf16[256,1024]{1,0:T(8,128)(2,1)S(1)} %copy-done.3), channel_id=1, source_target_pairs={{0,32},{32,0},{1,33},{33,1},{2,34},{34,2},{3,35},{35,3},{4,36},{36... | collective-permute-start | bytes 1572872 | tf_op jit(solution)/shard_map/ppermute | solution.py:288
  42.4 18.3 %all-to-all-start.1 = ((bf16[8,8,1152]{2,1,0:T(8,128)(2,1)}), bf16[8,8,1152]{2,1,0:T(8,128)(2,1)S(1)}, u32[]{:S(2)}, u32[]{:S(2)}) async-start(bf16[8,8,1152]{2,1,0:T(8,128)(2,1)} %combine_space.1), calls=%async_computation.1 | async-start | bytes 294912 | tf_op jit(solution)/shard_map/all_to_all | solution.py:290
  90.8 10.5 %collective-permute-start.3 = (bf16[32,8,1024]{2,1,0:T(8,128)(2,1)S(1)}, bf16[32,8,1024]{2,1,0:T(8,128)(2,1)S(1)}, u32[]{:S(2)}, u32[]{:S(2)}) collective-permute-start(bf16[32,8,1024]{2,1,0:T(8,128)(2,1)S(1)} %all_to_all.21.latents.mine), channel_id=1, source_target_pairs={{0,32},{32,0},{1,33},{33,1},{2,34},{34,2},{3,35},{35,3},{4,36},{36... | collective-permute-start | bytes 1572872 | tf_op jit(solution)/shard_map/ppermute | solution.py:300
  99.1 2.2 %copy-start.5 = (bf16[256,1024]{1,0:T(8,128)(2,1)S(1)}, bf16[256,1024]{1,0:T(8,128)(2,1)}, u32[]{:S(2)}) copy-start(bf16[256,1024]{1,0:T(8,128)(2,1)} %tokens.3) | copy-start | bytes 1572868

commit v3 on v2

--- a/solution.py
+++ b/solution.py
@@ -20,8 +20,12 @@
 SCALE = HD**-0.5 * math.log2(math.e)
 STATS = 128
 ONES = 16
-SLOTS = 3
-CHUNK = 64
+SLOTS = 6
+CHUNK = 32
+SCORE_ROWS = 128
+PEAK_ROWS = 32
+DELAYS = (0, 2, 3, 5)
+LN_ROWS = 16
 f32, bf16 = jnp.float32, jnp.bfloat16
 
 
@@ -41,38 +45,75 @@
         values_t[head, HD:, :] = jnp.ones((ONES, rows), bf16)
 
 
-def attend(keys, queries, values_t, scores, weights, old_peak, emit):
+def place_queries(queries_t, pair, part, at):
+    for side in range(2):
+        for other in range(2):
+            to = slice(at + other * HD, at + (other + 1) * HD)
+            mine = part[other * HD : (other + 1) * HD, :]
+            queries_t[2 * pair + side, to, :] = mine if other == side else jnp.zeros_like(mine)
+
+
+def put_queries(queries_t, queries, scaled):
+    for pair in range(H // 2):
+        part = queries[:, 2 * HD * pair : 2 * HD * (pair + 1)].T
+        if scaled:
+            exact = part.astype(f32) * SCALE
+            high = exact.astype(bf16)
+            place_queries(queries_t, pair, high, 0)
+            place_queries(queries_t, pair, (exact - high.astype(f32)).astype(bf16), 2 * HD)
+        else:
+            place_queries(queries_t, pair, part, 0)
+
+
+def put_normed(normed, tokens, also=None):
+    for at in range(0, tokens.shape[0], LN_ROWS):
+        rows = slice(at, at + LN_ROWS)
+        value = layer_norm(tokens[rows, :].astype(f32)).astype(bf16)
+        normed[rows, :] = value
+        if also is not None:
+            also[rows, :] = value
+
+
+def attend(keys, queries_t, values_t, scores, weights, old_peak, emit):
     peaks = {}
+    scaled = queries_t.shape[1] == 4 * HD
+
+    def scale(values):
+        return values if scaled else values * SCALE
 
     def score(head):
         pair = slice((head // 2) * 2 * HD, (head // 2 + 1) * 2 * HD)
-        query = queries(pair)
-        lane = lax.broadcasted_iota(jnp.int32, query.shape, 1)
-        query = jnp.where((lane >= HD) == (head % 2 == 1), query, jnp.zeros_like(query))
-        found = lax.dot_general(
-            keys[:, pair], query, (((1,), (1,)), ((), ())), preferred_element_type=f32
-        )
-        scores[head % SLOTS] = found
-        peak = jnp.max(found, axis=0, keepdims=True) * SCALE
+        for at in range(0, scores.shape[1], SCORE_ROWS):
+            rows = slice(at, at + SCORE_ROWS)
+            left = keys[rows, pair]
+            if scaled:
+                left = jnp.concatenate([left, left], axis=1)
+            scores[head % SLOTS, rows, :] = jnp.dot(left, queries_t[head], preferred_element_type=f32)
+
+    def find_peak(head):
+        top = scores[head % SLOTS, :PEAK_ROWS, :]
+        for at in range(PEAK_ROWS, scores.shape[1], PEAK_ROWS):
+            top = jnp.maximum(top, scores[head % SLOTS, at : at + PEAK_ROWS, :])
+        peak = scale(jnp.max(top, axis=0, keepdims=True))
         peaks[head] = peak if old_peak is None else jnp.maximum(peak, old_peak(head))
 
     def weigh(head):
         peak = jnp.broadcast_to(peaks[head], (CHUNK, peaks[head].shape[1]))
         for at in range(0, scores.shape[1], CHUNK):
             rows = slice(at, at + CHUNK)
-            weights[head % SLOTS, rows, :] = jnp.exp2(scores[head % SLOTS, rows, :] * SCALE - peak).astype(bf16)
+            weights[head % SLOTS, rows, :] = jnp.exp2(
+                scale(scores[head % SLOTS, rows, :]) - peak
+            ).astype(bf16)
 
     def apply(head):
         summed = jnp.dot(values_t[head], weights[head % SLOTS], preferred_element_type=f32)
         emit(head, peaks[head], summed[:HD], summed[HD : HD + 1])
 
-    for step in range(H + 2):
-        if step < H:
-            score(step)
-        if 0 <= step - 1 < H:
-            weigh(step - 1)
-        if 0 <= step - 2 < H:
-            apply(step - 2)
+    stages = (score, find_peak, weigh, apply)
+    for step in range(H + DELAYS[-1]):
+        for stage, delay in zip(stages, DELAYS):
+            if 0 <= step - delay < H:
+                stage(step - delay)
 
 
 def keep_in(peaks, totals, sums):
@@ -93,23 +134,27 @@
     return emit
 
 
-def half_of(latents, core, half):
-    return lambda pair: latents[pl.ds(pl.multiple_of(core * half, half), half), pair]
-
-
-def read_first(position, tokens, latents, keys, peaks, totals, sums, values_t, scores, weights):
-    value = tokens[...]
-    keys[...] = layer_norm(value.astype(f32)).astype(bf16)
-    put_values(values_t, value)
-    queries = half_of(latents, position[1], latents.shape[0] // 2)
-    attend(keys, queries, values_t, scores, weights, None, keep_in(peaks, totals, sums))
-
-
-def read_second(position, tokens, latents, peaks, totals, sums, packed, keys, values_t, scores, weights, stats):
-    value = tokens[...]
-    keys[...] = layer_norm(value.astype(f32)).astype(bf16)
-    put_values(values_t, value)
-    queries = half_of(latents, position[1], latents.shape[0] // 2)
+def read_first(
+    position, tokens_hbm, latents_hbm, keys_out, queries_t, peaks, totals, sums,
+    tokens, latents, keys, values_t, scores, weights, sems
+):
+    half = latents.shape[0]
+    start = pl.multiple_of(position[1] * half, half)
+    get_tokens = pltpu.make_async_copy(tokens_hbm, tokens, sems.at[0])
+    get_latents = pltpu.make_async_copy(latents_hbm.at[pl.ds(start, half)], latents, sems.at[1])
+    get_tokens.start()
+    get_latents.start()
+    get_tokens.wait()
+    put_normed(keys, tokens, keys_out)
+    put_values(values_t, tokens)
+    get_latents.wait()
+    put_queries(queries_t, latents, False)
+    attend(keys, queries_t, values_t, scores, weights, None, keep_in(peaks, totals, sums))
+
+
+def read_second(tokens, queries_t, peaks, totals, sums, packed, keys, values_t, scores, weights, stats):
+    put_normed(keys, tokens)
+    put_values(values_t, tokens)
     tiles, rows, _ = packed.shape
     stats[...] = jnp.zeros_like(stats)
     held = {}
@@ -128,7 +173,7 @@
             packed[:, :, (head - 1) * HD : (head + 1) * HD] = pack(both)
 
     attend(
-        keys, queries, values_t, scores, weights,
+        keys, queries_t, values_t, scores, weights,
         lambda head: peaks[head : head + 1, :],
         joined(peaks, totals, sums, then),
     )
@@ -165,9 +210,15 @@
     out[...] = jnp.broadcast_to(tile[None], out.shape)
 
 
-def mlp(position, arrived, latents, up, down, up_other, down_other, out, middle):
+def hold(*refs):
+    half = len(refs) // 2
+    for source, target in zip(refs[:half], refs[half:]):
+        target[...] = source[...]
+
+
+def mlp(arrived, latents, up, down, up_other, down_other, out, middle):
     summed, total, _ = combine(arrived[...].astype(f32))
-    own = latents[position[1], position[0]].astype(f32)
+    own = latents[...].astype(f32)
     middle[...] = own + summed * expand(1.0 / total)
     normed = layer_norm(middle[...]).astype(bf16)
     part = None
@@ -184,25 +235,30 @@
     out[...] = jnp.broadcast_to(new[None], out.shape)
 
 
-def prepare_write(latents, lat, values_t):
-    new = latents[...].astype(f32)
-    new = new.reshape(new.shape[0] * new.shape[1], new.shape[2])
-    lat[...] = new.astype(bf16)
-    put_values(values_t, layer_norm(new).astype(bf16))
-
-
-def write_first(latents, keys, peaks, totals, sums, lat, values_t, scores, weights):
-    prepare_write(latents, lat, values_t)
-    attend(
-        lat, lambda pair: keys[:, pair], values_t, scores, weights, None,
-        keep_in(peaks, totals, sums),
-    )
+def prepare_queries(keys, queries_t):
+    put_queries(queries_t, keys, True)
+
+
+def prepare_write(latents, lat, values, values_t):
+    tiles, rows, _ = latents.shape
+    for at in range(0, tiles, LN_ROWS // rows):
+        new = latents[at : at + LN_ROWS // rows].astype(f32).reshape(LN_ROWS, WIDTH)
+        to = slice(at * rows, at * rows + LN_ROWS)
+        lat[to, :] = new.astype(bf16)
+        values[to, :] = layer_norm(new).astype(bf16)
+    put_values(values_t, values)
+
+
+def write_first(latents, queries_t, peaks, totals, sums, lat, values, values_t, scores, weights):
+    prepare_write(latents, lat, values, values_t)
+    attend(lat, queries_t, values_t, scores, weights, None, keep_in(peaks, totals, sums))
 
 
 def write_second(
-    position, latents, mine, keys, tokens, peaks, totals, sums, out, owned, lat, values_t, scores, weights
+    position, latents, mine, queries_t, tokens, peaks, totals, sums, out, owned,
+    lat, values, values_t, scores, weights
 ):
-    prepare_write(latents, lat, values_t)
+    prepare_write(latents, lat, values, values_t)
     per = owned.shape[0]
     first = position[0] * per
     tiles = latents.shape[0]
@@ -227,16 +283,16 @@
             out[:, pair] = (tokens[:, pair].astype(f32) + both.T).astype(bf16)
 
     attend(
-        lat, lambda pair: keys[:, pair], values_t, scores, weights,
+        lat, queries_t, values_t, scores, weights,
         lambda head: peaks[head : head + 1, :],
         joined(peaks, totals, sums, then),
     )
 
 
-def call(kernel, outs, scratch=(), inputs=1, scalars=False, flops=0):
+def call(kernel, outs, scratch=(), inputs=1, scalars=False, flops=0, far=False, limit=16 << 20):
     whole = pl.BlockSpec(memory_space=pltpu.VMEM)
     single = not isinstance(outs, (list, tuple))
-    specs = [whole] * inputs
+    specs = [pl.BlockSpec(memory_space=pltpu.HBM) if far else whole] * inputs
     if scalars:
         specs = [pl.BlockSpec(memory_space=pltpu.SMEM)] + specs
     return pl.pallas_call(
@@ -245,7 +301,7 @@
         in_specs=specs,
         out_specs=whole if single else [whole] * len(outs),
         scratch_shapes=list(scratch),
-        compiler_params=pltpu.CompilerParams(vmem_limit_bytes=48 << 20),
+        compiler_params=pltpu.CompilerParams(vmem_limit_bytes=limit),
         name=kernel.__name__,
         cost_estimate=pl.CostEstimate(flops=flops, transcendentals=flops // 256, bytes_accessed=1 << 20),
     )
@@ -273,39 +329,53 @@
         return [shape((H, queries), f32), shape((H, queries), f32), shape((width, queries), f32)]
 
     other = lax.ppermute(tokens, CORE, swap)
-    keys, *part = call(
-        read_first, [shape((count, width), bf16), *state(half)], work(count, half),
-        inputs=2, scalars=True, flops=heavy,
+    block = lambda rows: pltpu.VMEM((rows, width), bf16)
+    keys, queries_t, *part = call(
+        read_first,
+        [shape((count, width), bf16), shape((H, 2 * HD, half), bf16), *state(half)],
+        [block(count), block(half), block(count), *work(count, half), pltpu.SemaphoreType.DMA((2,))],
+        inputs=2, scalars=True, flops=heavy, far=True, limit=50 << 20,
     )(position, tokens, latents)
     packed = call(
         read_second,
         shape((n_space, rows, width + STATS), bf16),
-        [pltpu.VMEM((count, width), bf16), *work(count, half), pltpu.VMEM((STATS, half), f32)],
-        inputs=5, scalars=True, flops=heavy,
-    )(position, other, latents, *part)
-    packed, up_late, down_late = lax.optimization_barrier((packed, up_weight, down_weight))
+        [block(count), *work(count, half), pltpu.VMEM((STATS, half), f32)],
+        inputs=5, flops=heavy,
+    )(other, queries_t, *part)
+    packed, up_late, down_late, keys, late = lax.optimization_barrier(
+        (packed, up_weight, down_weight, keys, latents)
+    )
     packed = lax.all_to_all(packed, SPACE, 0, 0, tiled=True)
     up_other, down_other = lax.ppermute(up_late, CORE, swap), lax.ppermute(down_late, CORE, swap)
+    queries_t = call(
+        prepare_queries, shape((H, 4 * HD, count), bf16), flops=1 << 20, limit=60 << 20
+    )(keys)
+    mine = lax.dynamic_slice_in_dim(late, core * half + place * rows, rows, 0)
+    packed, queries_t, up_other, down_other, mine = lax.optimization_barrier(
+        (packed, queries_t, up_other, down_other, mine)
+    )
     tiles = call(combine_space, shape((n_z, rows, width + STATS), bf16))(packed)
+    tiles, *weights = lax.optimization_barrier((tiles, up_late, down_late, up_other, down_other))
     tiles = lax.all_to_all(tiles, Z, 0, 0, tiled=True)
+    weights = call(hold, [shape(w.shape, bf16) for w in weights], inputs=4, flops=1 << 20)(*weights)
+    tiles, *weights = lax.optimization_barrier((tiles, *weights))
     parts, middle = call(
-        mlp, [shape((n_z, rows, width), bf16), shape((rows, width), f32)], inputs=6, scalars=True
-    )(
-        position, tiles, latents.reshape(2, n_space, rows, width),
-        up_weight, down_weight, up_other, down_other,
-    )
+        mlp, [shape((n_z, rows, width), bf16), shape((rows, width), f32)], inputs=6
+    )(tiles, mine, *weights)
     parts = lax.all_to_all(parts, Z, 0, 0, tiled=True)
     new = call(finish, shape((n_space, rows, width), bf16), inputs=2)(parts, middle)
     mine = lax.all_to_all(new, SPACE, 0, 0, tiled=True)
     theirs = lax.ppermute(mine, CORE, swap)
-    lat = pltpu.VMEM((half, width), bf16)
-    part = call(write_first, state(count), [lat, *work(half, count)], inputs=2, flops=heavy)(mine, keys)
+    part = call(
+        write_first, state(count), [block(half), block(half), *work(half, count)],
+        inputs=2, flops=heavy,
+    )(mine, queries_t)
     new_tokens, new_latents = call(
         write_second,
         [shape((count, width), bf16), shape((2, rows, width), bf16)],
-        [lat, *work(half, count)],
+        [block(half), block(half), *work(half, count)],
         inputs=7, scalars=True, flops=heavy,
-    )(position, theirs, mine, keys, tokens, *part)
+    )(position, theirs, mine, queries_t, tokens, *part)
     return (new_tokens, new_latents.reshape(2 * rows, width))
 
 

time: 106 us -> 102 us (0.962)
  waiting for transfers between devices: 21.9 us -> 15.4 us
  local copies, waits for them, and re-layouts: 2.28 us -> 4.68 us
    all_to_all x1, waiting for transfers between devices: 13.7 us -> 9.39 us  [on_device(): packed = lax.all_to_all(packed, SPACE, 0, 0, tiled=True)]
    all_to_all x1, waiting for transfers between devices: 8.19 us -> 5.98 us  [on_device(): tiles = lax.all_to_all(tiles, Z, 0, 0, tiled=True)]
    unnamed x12 -> x20, local copies, waits for them, and re-layouts: 2.28 us -> 3.96 us
    pallas_call x3 -> x5, Pallas kernels: 9.24 us -> 10.7 us  [the longest x1 3.28 us: on_device(): call(read_first, [shape((count, width), bf16), shape((H, 2 * HD, half), b...]
    pallas_call x1, Pallas kernels: 2.12 us -> 0.92 us  [on_device(): call(mlp, [shape((n_z, rows, width), bf16), shape((rows, width), f32)], i...]
  transfers between devices with their start and end apart: 6 -> 6, of which waited for: 2 -> 2; matrix products, arithmetic and copies ran while one was open for 0% -> 1% of each run, Pallas kernels for 6% -> 8%
where the time goes in v3:
time: 102 us; the launch traced here: 101 us
  starting transfers between devices  35.8 us (35%)
  blocking collectives  28.1 us (28%)
  Pallas kernels  16.2 us (16%)
  waiting for transfers between devices  15.4 us (15%)
  local copies, waits for them, and re-layouts  4.68 us (5%)
    all_to_all x1, blocking collectives, on_device(): mine = lax.all_to_all(new, SPACE, 0, 0, tiled=True)  17.7 us
    all_to_all x1, blocking collectives, on_device(): parts = lax.all_to_all(parts, Z, 0, 0, tiled=True)  10.4 us
    all_to_all x1, starting transfers between devices, on_device(): tiles = lax.all_to_all(tiles, Z, 0, 0, tiled=True)  10.1 us
    all_to_all x1, waiting for transfers between devices, on_device(): packed = lax.all_to_all(packed, SPACE, 0, 0, tiled=True)  9.39 us
    ppermute x1, starting transfers between devices, on_device(): other = lax.ppermute(tokens, CORE, swap)  8.75 us
    ppermute x1, starting transfers between devices, on_device(): theirs = lax.ppermute(mine, CORE, swap)  8.25 us
    all_to_all x1, waiting for transfers between devices, on_device(): tiles = lax.all_to_all(tiles, Z, 0, 0, tiled=True)  5.98 us
    all_to_all x1, starting transfers between devices, on_device(): packed = lax.all_to_all(packed, SPACE, 0, 0, tiled=True)  4.32 us
  transfers between devices with their start and end apart: 6, of which 2 were waited for; matrix products, arithmetic and copies ran while one was open for 1% of the time, Pallas kernels for 8%

profile of v3, /device:TPU:1, one launch (start us, length us, event | category | flops | bytes accessed | tf_op | source)
XLA Modules:
  0.0 101.0 jit_solution(6095351964096298763)
XLA Ops:
  0.6 8.7 %collective-permute-start = (bf16[256,1024]{1,0:T(8,128)(2,1)}, bf16[256,1024]{1,0:T(8,128)(2,1)S(1)}, u32[]{:S(2)}, u32[]{:S(2)}) collective-permute-start(bf16[256,1024]{1,0:T(8,128)(2,1)} %tokens.1), channel_id=1, source_target_pairs={{0,32},{32,0},{1,33},{33,1},{2,34},{34,2},{3,35},{35,3},{4,36},{36... | collective-permute-start | bytes 1572872 | tf_op jit(solution)/shard_map/ppermute | solution.py:331
  9.4 0.1 pad_add_fusion.position
  9.5 1.0 %copy-done.1 = bf16[256,1024]{1,0:T(8,128)(2,1)S(1)} copy-done((bf16[256,1024]{1,0:T(8,128)(2,1)S(1)}, bf16[256,1024]{1,0:T(8,128)(2,1)}, u32[]{:S(2)}) %copy-start.1) | copy-done | bytes 524312
  10.5 3.3 %read_first.1 = (bf16[256,1024]{1,0:T(8,128)(2,1)S(1)}, bf16[16,128,256]{2,1,0:T(8,128)(2,1)S(1)}, f32[16,256]{1,0:T(8,128)S(1)}, f32[16,256]{1,0:T(8,128)S(1)}, f32[1024,256]{1,0:T(8,128)S(1)}) custom-call(s32[2]{0:T(128)S(1)} %pad_add_fusion.position, bf16[256,1024]{1,0:T(8,128)(2,1)S(1)} %copy-done.1, bf16[512,1024]{1,0:T(8,128)(2,1)} %latents_hbm.1), custom_call_target="tpu_custom_call" | custom-call | flops 268435456 | bytes 1048576 | tf_op jit(solution)/shard_map/read_first/pallas_call | solution.py:333
  13.8 0.0 copy-start.3
  13.8 0.0 collective-permute-done.tokens
  13.8 0.0 copy-start.4
  13.8 0.0 copy-start.5
  13.8 3.0 %read_second.1 = bf16[32,8,1152]{2,1,0:T(8,128)(2,1)} custom-call(bf16[256,1024]{1,0:T(8,128)(2,1)S(1)} %collective-permute-done.tokens, bf16[16,128,256]{2,1,0:T(8,128)(2,1)S(1)} %get-tuple-element.38.queries_t, f32[16,256]{1,0:T(8,128)S(1)} %get-tuple-element.39.peaks, f32[16,256]{1,0:T(8,128)S(1)} %get-tuple-element.40.totals, ...), custom_call_target="tpu_custom_call" | custom-call | flops 268435456 | bytes 1048576 | tf_op jit(solution)/shard_map/read_second/pallas_call | solution.py:339
  16.8 4.3 %all-to-all-start = ((bf16[32,8,1152]{2,1,0:T(8,128)(2,1)}), bf16[32,8,1152]{2,1,0:T(8,128)(2,1)S(1)}, u32[]{:S(2)}, u32[]{:S(2)}) async-start(bf16[32,8,1152]{2,1,0:T(8,128)(2,1)} %read_second.1), calls=%async_computation | async-start | bytes 1179648 | tf_op jit(solution)/shard_map/all_to_all | solution.py:348
  21.2 2.2 %collective-permute-start.1 = (bf16[1024,256]{1,0:T(8,128)(2,1)S(1)}, bf16[1024,256]{1,0:T(8,128)(2,1)S(1)}, u32[]{:S(2)}, u32[]{:S(2)}) collective-permute-start(bf16[1024,256]{1,0:T(8,128)(2,1)S(1)} %copy-done.4), channel_id=1, source_target_pairs={{0,32},{32,0},{1,33},{33,1},{2,34},{34,2},{3,35},{35,3},{4,36},{36... | collective-permute-start | bytes 1572872 | tf_op jit(solution)/shard_map/ppermute | solution.py:349
  23.4 2.1 %collective-permute-start.2 = (bf16[256,1024]{1,0:T(8,128)(2,1)S(1)}, bf16[256,1024]{1,0:T(8,128)(2,1)S(1)}, u32[]{:S(2)}, u32[]{:S(2)}) collective-permute-start(bf16[256,1024]{1,0:T(8,128)(2,1)S(1)} %copy-done.5), channel_id=1, source_target_pairs={{0,32},{32,0},{1,33},{33,1},{2,34},{34,2},{3,35},{35,3},{4,36},{36... | collective-permute-start | bytes 1572872 | tf_op jit(solution)/shard_map/ppermute | solution.py:349
  25.5 2.7 %prepare_queries.1.queries_t = bf16[16,256,256]{2,1,0:T(8,128)(2,1)} custom-call(bf16[256,1024]{1,0:T(8,128)(2,1)} %copy-done.3), custom_call_target="tpu_custom_call" | custom-call | flops 1048576 | bytes 1048576 | tf_op jit(solution)/shard_map/prepare_queries/pallas_call | solution.py:350
  28.2 0.7 constant_dynamic-slice_fusion.latents
  28.9 0.0 collective-permute-done.1.refs_2_
  28.9 0.0 collective-permute-done.2.refs_3_
  28.9 0.8 copy-done.8
  29.8 9.4 %all-to-all-done.arrived = bf16[32,8,1152]{2,1,0:T(8,128)(2,1)S(1)} async-done(((bf16[32,8,1152]{2,1,0:T(8,128)(2,1)}), bf16[32,8,1152]{2,1,0:T(8,128)(2,1)S(1)}, u32[]{:S(2)}, u32[]{:S(2)}) %all-to-all-start) | async-done | bytes 589856 | tf_op jit(solution)/shard_map/all_to_all | solution.py:348
  39.2 1.0 %combine_space.1 = bf16[8,8,1152]{2,1,0:T(8,128)(2,1)} custom-call(bf16[32,8,1152]{2,1,0:T(8,128)(2,1)S(1)} %all-to-all-done.arrived), custom_call_target="tpu_custom_call" | custom-call | bytes 1048576 | tf_op jit(solution)/shard_map/combine_space/pallas_call | solution.py:357
  40.2 10.1 %all-to-all-start.1 = ((bf16[8,8,1152]{2,1,0:T(8,128)(2,1)}), bf16[8,8,1152]{2,1,0:T(8,128)(2,1)S(1)}, u32[]{:S(2)}, u32[]{:S(2)}) async-start(bf16[8,8,1152]{2,1,0:T(8,128)(2,1)} %combine_space.1), calls=%async_computation.1 | async-start | bytes 294912 | tf_op jit(solution)/shard_map/all_to_all | solution.py:359
  50.3 1.0 %copy-done.7 = bf16[1024,256]{1,0:T(8,128)(2,1)S(1)} copy-done((bf16[1024,256]{1,0:T(8,128)(2,1)S(1)}, bf16[1024,256]{1,0:T(8,128)(2,1)}, u32[]{:S(2)}) %copy-start.7) | copy-done | bytes 524312
  51.4 1.0 %copy-done.9 = bf16[256,1024]{1,0:T(8,128)(2,1)S(1)} copy-done((bf16[256,1024]{1,0:T(8,128)(2,1)S(1)}, bf16[256,1024]{1,0:T(8,128)(2,1)}, u32[]{:S(2)}) %copy-start.9) | copy-done | bytes 524312
  52.4 0.1 hold.1
  52.5 6.0 %all-to-all-done.1.arrived = bf16[8,8,1152]{2,1,0:T(8,128)(2,1)S(1)} async-done(((bf16[8,8,1152]{2,1,0:T(8,128)(2,1)}), bf16[8,8,1152]{2,1,0:T(8,128)(2,1)S(1)}, u32[]{:S(2)}, u32[]{:S(2)}) %all-to-all-start.1) | async-done | bytes 147488 | tf_op jit(solution)/shard_map/all_to_all | solution.py:359
  58.5 0.9 mlp.1
  59.4 10.4 %all_to_all.20.parts = bf16[8,8,1024]{2,1,0:T(8,128)(2,1)S(1)} all-to-all(bf16[8,8,1024]{2,1,0:T(8,128)(2,1)S(1)} %get-tuple-element.66), channel_id=1, replica_groups=mesh['tm_0'=8,'tm_1'=2,'space_0'=8,'space_1'=4] {'tm_0'}, dimensions={0} | all-to-all | bytes 262144 | tf_op jit(solution)/shard_map/all_to_all | solution.py:365
  69.8 0.1 finish.1
  69.9 17.7 %all_to_all.21.latents.mine = bf16[32,8,1024]{2,1,0:T(8,128)(2,1)S(1)} all-to-all(bf16[32,8,1024]{2,1,0:T(8,128)(2,1)S(1)} %finish.1), channel_id=1, replica_groups=mesh['tm_0'=8,'tm_1'=2,'space_0'=8,'space_1'=4] {'space_0','space_1'}, dimensions={0} | all-to-all | bytes 1048576 | tf_op jit(solution)/shard_map/all_to_all | solution.py:367
  87.6 8.2 %collective-permute-start.3 = (bf16[32,8,1024]{2,1,0:T(8,128)(2,1)S(1)}, bf16[32,8,1024]{2,1,0:T(8,128)(2,1)S(1)}, u32[]{:S(2)}, u32[]{:S(2)}) collective-permute-start(bf16[32,8,1024]{2,1,0:T(8,128)(2,1)S(1)} %all_to_all.21.latents.mine), channel_id=1, source_target_pairs={{0,32},{32,0},{1,33},{33,1},{2,34},{34,2},{3,35},{35,3},{4,36},{36... | collective-permute-start | bytes 1572872 | tf_op jit(solution)/shard_map/ppermute | solution.py:368
  95.9 1.7 %write_first.1 = (f32[16,256]{1,0:T(8,128)S(1)}, f32[16,256]{1,0:T(8,128)S(1)}, f32[1024,256]{1,0:T(8,128)S(1)}) custom-call(bf16[32,8,1024]{2,1,0:T(8,128)(2,1)S(1)} %all_to_all.21.latents.mine, bf16[16,256,256]{2,1,0:T(8,128)(2,1)S(1)} %copy-done), custom_call_target="tpu_custom_call" | custom-call | flops 268435456 | bytes 1048576 | tf_op jit(solution)/shard_map/write_first/pallas_call | solution.py:369
  97.5 0.0 collective-permute-done.3.latents
  97.6 3.5 %write_second.1 = (bf16[256,1024]{1,0:T(8,128)(2,1)}, bf16[2,8,1024]{2,1,0:T(8,128)(2,1)}) custom-call(s32[2]{0:T(128)S(1)} %pad_add_fusion.position, bf16[32,8,1024]{2,1,0:T(8,128)(2,1)S(1)} %collective-permute-done.3.latents, bf16[32,8,1024]{2,1,0:T(8,128)(2,1)S(1)} %all_to_all.21.latents.mine, bf16[16,256,256]{2,1,0:T(8,128)(2,1)S(1)} %copy-done, ...), custom_call_target="tpu_custom_call" | custom-call | flops 268435456 | bytes 1048576 | tf_op jit(solution)/shard_map/write_second/pallas_call | solution.py:373
  (13 shorter events, 0.0 us)
Async XLA Ops:
  0.6 13.2 %collective-permute-start = (bf16[256,1024]{1,0:T(8,128)(2,1)}, bf16[256,1024]{1,0:T(8,128)(2,1)S(1)}, u32[]{:S(2)}, u32[]{:S(2)}) collective-permute-start(bf16[256,1024]{1,0:T(8,128)(2,1)} %tokens.1), channel_id=1, source_target_pairs={{0,32},{32,0},{1,33},{33,1},{2,34},{34,2},{3,35},{35,3},{4,36},{36... | collective-permute-start | bytes 1572872 | tf_op jit(solution)/shard_map/ppermute | solution.py:331
  9.5 1.0 %copy-start.1 = (bf16[256,1024]{1,0:T(8,128)(2,1)S(1)}, bf16[256,1024]{1,0:T(8,128)(2,1)}, u32[]{:S(2)}) copy-start(bf16[256,1024]{1,0:T(8,128)(2,1)} %tokens.1) | copy-start | bytes 1572868
  13.8 3.0 %copy-start.3 = (bf16[256,1024]{1,0:T(8,128)(2,1)}, bf16[256,1024]{1,0:T(8,128)(2,1)S(1)}, u32[]{:S(2)}) copy-start(bf16[256,1024]{1,0:T(8,128)(2,1)S(1)} %get-tuple-element.44.keys) | copy-start | bytes 1572868
  13.8 7.3 %copy-start.4 = (bf16[1024,256]{1,0:T(8,128)(2,1)S(1)}, bf16[1024,256]{1,0:T(8,128)(2,1)}, u32[]{:S(2)}) copy-start(bf16[1024,256]{1,0:T(8,128)(2,1)} %refs_0_) | copy-start | bytes 1572868
  13.8 9.5 %copy-start.5 = (bf16[256,1024]{1,0:T(8,128)(2,1)S(1)}, bf16[256,1024]{1,0:T(8,128)(2,1)}, u32[]{:S(2)}) copy-start(bf16[256,1024]{1,0:T(8,128)(2,1)} %refs_1_) | copy-start | bytes 1572868
  16.8 22.3 %all-to-all-start = ((bf16[32,8,1152]{2,1,0:T(8,128)(2,1)}), bf16[32,8,1152]{2,1,0:T(8,128)(2,1)S(1)}, u32[]{:S(2)}, u32[]{:S(2)}) async-start(bf16[32,8,1152]{2,1,0:T(8,128)(2,1)} %read_second.1), calls=%async_computation | async-start | bytes 1179648 | tf_op jit(solution)/shard_map/all_to_all | solution.py:348
  21.2 7.8 %collective-permute-start.1 = (bf16[1024,256]{1,0:T(8,128)(2,1)S(1)}, bf16[1024,256]{1,0:T(8,128)(2,1)S(1)}, u32[]{:S(2)}, u32[]{:S(2)}) collective-permute-start(bf16[1024,256]{1,0:T(8,128)(2,1)S(1)} %copy-done.4), channel_id=1, source_target_pairs={{0,32},{32,0},{1,33},{33,1},{2,34},{34,2},{3,35},{35,3},{4,36},{36... | collective-permute-start | bytes 1572872 | tf_op jit(solution)/shard_map/ppermute | solution.py:349
  23.4 5.5 %collective-permute-start.2 = (bf16[256,1024]{1,0:T(8,128)(2,1)S(1)}, bf16[256,1024]{1,0:T(8,128)(2,1)S(1)}, u32[]{:S(2)}, u32[]{:S(2)}) collective-permute-start(bf16[256,1024]{1,0:T(8,128)(2,1)S(1)} %copy-done.5), channel_id=1, source_target_pairs={{0,32},{32,0},{1,33},{33,1},{2,34},{34,2},{3,35},{35,3},{4,36},{36... | collective-permute-start | bytes 1572872 | tf_op jit(solution)/shard_map/ppermute | solution.py:349
  28.9 11.3 %copy-start.6 = (bf16[1024,256]{1,0:T(8,128)(2,1)}, bf16[1024,256]{1,0:T(8,128)(2,1)S(1)}, u32[]{:S(2)}) copy-start(bf16[1024,256]{1,0:T(8,128)(2,1)S(1)} %collective-permute-done.1.refs_2_) | copy-start | bytes 1572868
  28.9 0.8 copy-start.8
  40.2 18.3 %all-to-all-start.1 = ((bf16[8,8,1152]{2,1,0:T(8,128)(2,1)}), bf16[8,8,1152]{2,1,0:T(8,128)(2,1)S(1)}, u32[]{:S(2)}, u32[]{:S(2)}) async-start(bf16[8,8,1152]{2,1,0:T(8,128)(2,1)} %combine_space.1), calls=%async_computation.1 | async-start | bytes 294912 | tf_op jit(solution)/shard_map/all_to_all | solution.py:359
  50.3 1.0 %copy-start.7 = (bf16[1024,256]{1,0:T(8,128)(2,1)S(1)}, bf16[1024,256]{1,0:T(8,128)(2,1)}, u32[]{:S(2)}) copy-start(bf16[1024,256]{1,0:T(8,128)(2,1)} %copy-done.6) | copy-start | bytes 1572868
  51.3 1.0 %copy-start.9 = (bf16[256,1024]{1,0:T(8,128)(2,1)S(1)}, bf16[256,1024]{1,0:T(8,128)(2,1)}, u32[]{:S(2)}) copy-start(bf16[256,1024]{1,0:T(8,128)(2,1)} %copy-done.8) | copy-start | bytes 1572868
  58.5 37.4 %copy-start = (bf16[16,256,256]{2,1,0:T(8,128)(2,1)S(1)}, bf16[16,256,256]{2,1,0:T(8,128)(2,1)}, u32[]{:S(2)}) copy-start(bf16[16,256,256]{2,1,0:T(8,128)(2,1)} %prepare_queries.1.queries_t) | copy-start | bytes 6291460
  69.8 27.7 %copy-start.2 = (bf16[256,1024]{1,0:T(8,128)(2,1)S(1)}, bf16[256,1024]{1,0:T(8,128)(2,1)}, u32[]{:S(2)}) copy-start(bf16[256,1024]{1,0:T(8,128)(2,1)} %tokens.1) | copy-start | bytes 1572868
  87.6 9.9 %collective-permute-start.3 = (bf16[32,8,1024]{2,1,0:T(8,128)(2,1)S(1)}, bf16[32,8,1024]{2,1,0:T(8,128)(2,1)S(1)}, u32[]{:S(2)}, u32[]{:S(2)}) collective-permute-start(bf16[32,8,1024]{2,1,0:T(8,128)(2,1)S(1)} %all_to_all.21.latents.mine), channel_id=1, source_target_pairs={{0,32},{32,0},{1,33},{33,1},{2,34},{34,2},{3,35},{35,3},{4,36},{36... | collective-permute-start | bytes 1572872 | tf_op jit(solution)/shard_map/ppermute | solution.py:368

commit v4 on v3

--- a/solution.py
+++ b/solution.py
@@ -65,13 +65,10 @@
             place_queries(queries_t, pair, part, 0)
 
 
-def put_normed(normed, tokens, also=None):
-    for at in range(0, tokens.shape[0], LN_ROWS):
+def put_normed(normed, tokens, first, last):
+    for at in range(first, last, LN_ROWS):
         rows = slice(at, at + LN_ROWS)
-        value = layer_norm(tokens[rows, :].astype(f32)).astype(bf16)
-        normed[rows, :] = value
-        if also is not None:
-            also[rows, :] = value
+        normed[rows, :] = layer_norm(tokens[rows, :].astype(f32)).astype(bf16)
 
 
 def attend(keys, queries_t, values_t, scores, weights, old_peak, emit):
@@ -134,33 +131,62 @@
     return emit
 
 
-def read_first(
-    position, tokens_hbm, latents_hbm, keys_out, queries_t, peaks, totals, sums,
-    tokens, latents, keys, values_t, scores, weights, sems
+def prepare_read(
+    position, tokens_hbm, latents_hbm, keys, values_t, queries_t, tokens, latents, sems
 ):
-    half = latents.shape[0]
-    start = pl.multiple_of(position[1] * half, half)
-    get_tokens = pltpu.make_async_copy(tokens_hbm, tokens, sems.at[0])
-    get_latents = pltpu.make_async_copy(latents_hbm.at[pl.ds(start, half)], latents, sems.at[1])
-    get_tokens.start()
-    get_latents.start()
-    get_tokens.wait()
-    put_normed(keys, tokens, keys_out)
+    half, count = latents.shape[0], tokens.shape[0]
+    start = position[1] * half
+    pieces = sems.shape[0] // 2
+    copies = []
+    for i in range(pieces):
+        size = count // pieces
+        rows = pl.ds(i * size, size)
+        copies.append(pltpu.make_async_copy(tokens_hbm.at[rows], tokens.at[rows], sems.at[i]))
+    for i in range(pieces):
+        size = half // pieces
+        source = pl.ds(pl.multiple_of(start + i * size, size), size)
+        copies.append(
+            pltpu.make_async_copy(
+                latents_hbm.at[source], latents.at[pl.ds(i * size, size)], sems.at[pieces + i]
+            )
+        )
+    for copy in copies:
+        copy.start()
+    for i in range(pieces):
+        copies[i].wait()
+        put_normed(keys, tokens, i * (count // pieces), (i + 1) * (count // pieces))
     put_values(values_t, tokens)
-    get_latents.wait()
+    for copy in copies[pieces:]:
+        copy.wait()
     put_queries(queries_t, latents, False)
+
+
+def read_first(keys, values_t, queries_t, keys_hbm, peaks, totals, sums, scores, weights, sem):
+    keep = pltpu.make_async_copy(keys, keys_hbm, sem)
+    keep.start()
     attend(keys, queries_t, values_t, scores, weights, None, keep_in(peaks, totals, sums))
-
-
-def read_second(tokens, queries_t, peaks, totals, sums, packed, keys, values_t, scores, weights, stats):
-    put_normed(keys, tokens)
+    keep.wait()
+
+
+def read_second(
+    tokens, queries_t, peaks, totals, sums, packed_hbm, keys, values_t, scores, weights, stats, packed, sems
+):
+    put_normed(keys, tokens, 0, tokens.shape[0])
     put_values(values_t, tokens)
     tiles, rows, _ = packed.shape
     stats[...] = jnp.zeros_like(stats)
     held = {}
 
+    copies = []
+
     def pack(part):
         return part.T.reshape(tiles, rows, part.shape[0]).astype(bf16)
+
+    def send(first, last):
+        part = packed.at[:, :, first:last]
+        copy = pltpu.make_async_copy(part, packed_hbm.at[:, :, first:last], sems.at[len(copies)])
+        copy.start()
+        copies.append(copy)
 
     def then(head, peak, summed, total):
         sent = peak.astype(bf16).astype(f32)
@@ -171,6 +197,8 @@
         if head % 2 == 1:
             both = jnp.concatenate([held[head - 1], held[head]], axis=0)
             packed[:, :, (head - 1) * HD : (head + 1) * HD] = pack(both)
+        if head == H // 2 - 1:
+            send(0, WIDTH // 2)
 
     attend(
         keys, queries_t, values_t, scores, weights,
@@ -178,6 +206,9 @@
         joined(peaks, totals, sums, then),
     )
     packed[:, :, WIDTH:] = pack(stats[...])
+    send(WIDTH // 2, WIDTH + STATS)
+    for copy in copies:
+        copy.wait()
 
 
 def expand(factor):
@@ -211,9 +242,16 @@
 
 
 def hold(*refs):
+    *refs, sems = refs
     half = len(refs) // 2
-    for source, target in zip(refs[:half], refs[half:]):
-        target[...] = source[...]
+    copies = [
+        pltpu.make_async_copy(source, target, sems.at[i])
+        for i, (source, target) in enumerate(zip(refs[:half], refs[half:]))
+    ]
+    for copy in copies:
+        copy.start()
+    for copy in copies:
+        copy.wait()
 
 
 def mlp(arrived, latents, up, down, up_other, down_other, out, middle):
@@ -255,8 +293,8 @@
 
 
 def write_second(
-    position, latents, mine, queries_t, tokens, peaks, totals, sums, out, owned,
-    lat, values, values_t, scores, weights
+    position, latents, mine, queries_t, tokens, peaks, totals, sums, out_hbm, owned,
+    lat, values, values_t, scores, weights, out, sems
 ):
     prepare_write(latents, lat, values, values_t)
     per = owned.shape[0]
@@ -274,6 +312,7 @@
         owned[...] = mine[pl.ds(start, per)]
 
     held = {}
+    copies = []
 
     def then(head, peak, summed, total):
         held[head] = summed * (1.0 / total)
@@ -281,25 +320,37 @@
             both = jnp.concatenate([held[head - 1], held[head]], axis=0)
             pair = slice((head - 1) * HD, (head + 1) * HD)
             out[:, pair] = (tokens[:, pair].astype(f32) + both.T).astype(bf16)
+        if head % (H // 2) == H // 2 - 1:
+            lanes = slice(head * HD + HD - WIDTH // 2, head * HD + HD)
+            copy = pltpu.make_async_copy(
+                out.at[:, lanes], out_hbm.at[:, lanes], sems.at[len(copies)]
+            )
+            copy.start()
+            copies.append(copy)
 
     attend(
         lat, queries_t, values_t, scores, weights,
         lambda head: peaks[head : head + 1, :],
         joined(peaks, totals, sums, then),
     )
-
-
-def call(kernel, outs, scratch=(), inputs=1, scalars=False, flops=0, far=False, limit=16 << 20):
+    for copy in copies:
+        copy.wait()
+
+
+def call(kernel, outs, scratch=(), inputs=1, scalars=False, flops=0, far=False, far_out=False, limit=16 << 20):
     whole = pl.BlockSpec(memory_space=pltpu.VMEM)
     single = not isinstance(outs, (list, tuple))
     specs = [pl.BlockSpec(memory_space=pltpu.HBM) if far else whole] * inputs
+    out_specs = [whole] * (1 if single else len(outs))
+    if far_out:
+        out_specs[0] = pl.BlockSpec(memory_space=pltpu.HBM)
     if scalars:
         specs = [pl.BlockSpec(memory_space=pltpu.SMEM)] + specs
     return pl.pallas_call(
         kernel,
         out_shape=outs,
         in_specs=specs,
-        out_specs=whole if single else [whole] * len(outs),
+        out_specs=out_specs[0] if single else out_specs,
         scratch_shapes=list(scratch),
         compiler_params=pltpu.CompilerParams(vmem_limit_bytes=limit),
         name=kernel.__name__,
@@ -328,19 +379,34 @@
     def state(queries):
         return [shape((H, queries), f32), shape((H, queries), f32), shape((width, queries), f32)]
 
-    other = lax.ppermute(tokens, CORE, swap)
     block = lambda rows: pltpu.VMEM((rows, width), bf16)
-    keys, queries_t, *part = call(
-        read_first,
-        [shape((count, width), bf16), shape((H, 2 * HD, half), bf16), *state(half)],
-        [block(count), block(half), block(count), *work(count, half), pltpu.SemaphoreType.DMA((2,))],
-        inputs=2, scalars=True, flops=heavy, far=True, limit=50 << 20,
+    values, *buffers = work(count, half)
+    keys, values_t, queries_t = call(
+        prepare_read,
+        [
+            shape((count, width), bf16), shape((H, HD + ONES, count), bf16),
+            shape((H, 2 * HD, half), bf16),
+        ],
+        [block(count), block(half), pltpu.SemaphoreType.DMA((8,))],
+        inputs=2, scalars=True, flops=heavy // 8, far=True, limit=52019 << 10,
     )(position, tokens, latents)
+    swapped, keys, values_t, queries_t = lax.optimization_barrier(
+        (tokens, keys, values_t, queries_t)
+    )
+    other = lax.ppermute(swapped, CORE, swap)
+    keys, *part = call(
+        read_first, [shape((count, width), bf16), *state(half)],
+        [*buffers, pltpu.SemaphoreType.DMA],
+        inputs=3, flops=heavy, far_out=True, limit=50 << 20,
+    )(keys, values_t, queries_t)
+    tile = (n_space, rows, width + STATS)
     packed = call(
-        read_second,
-        shape((n_space, rows, width + STATS), bf16),
-        [block(count), *work(count, half), pltpu.VMEM((STATS, half), f32)],
-        inputs=5, flops=heavy,
+        read_second, shape(tile, bf16),
+        [
+            block(count), *work(count, half), pltpu.VMEM((STATS, half), f32), pltpu.VMEM(tile, bf16),
+            pltpu.SemaphoreType.DMA((2,)),
+        ],
+        inputs=5, flops=heavy, far_out=True,
     )(other, queries_t, *part)
     packed, up_late, down_late, keys, late = lax.optimization_barrier(
         (packed, up_weight, down_weight, keys, latents)
@@ -357,7 +423,10 @@
     tiles = call(combine_space, shape((n_z, rows, width + STATS), bf16))(packed)
     tiles, *weights = lax.optimization_barrier((tiles, up_late, down_late, up_other, down_other))
     tiles = lax.all_to_all(tiles, Z, 0, 0, tiled=True)
-    weights = call(hold, [shape(w.shape, bf16) for w in weights], inputs=4, flops=1 << 20)(*weights)
+    weights = call(
+        hold, [shape(w.shape, bf16) for w in weights], [pltpu.SemaphoreType.DMA((4,))],
+        inputs=4, flops=1 << 20, far=True, limit=52838 << 10,
+    )(*weights)
     tiles, *weights = lax.optimization_barrier((tiles, *weights))
     parts, middle = call(
         mlp, [shape((n_z, rows, width), bf16), shape((rows, width), f32)], inputs=6
@@ -373,8 +442,11 @@
     new_tokens, new_latents = call(
         write_second,
         [shape((count, width), bf16), shape((2, rows, width), bf16)],
-        [block(half), block(half), *work(half, count)],
-        inputs=7, scalars=True, flops=heavy,
+        [
+            block(half), block(half), *work(half, count), block(count),
+            pltpu.SemaphoreType.DMA((2,)),
+        ],
+        inputs=7, scalars=True, flops=heavy, far_out=True,
     )(position, theirs, mine, queries_t, tokens, *part)
     return (new_tokens, new_latents.reshape(2 * rows, width))
 

time: 102 us -> 102 us (level)
  local copies, waits for them, and re-layouts: 4.68 us -> 0.74 us
  Pallas kernels: 16.2 us -> 19.5 us
    unnamed x20 -> x12, local copies, waits for them, and re-layouts: 3.96 us -> 0.03 us
    pallas_call x3 -> x4, Pallas kernels: 6.38 us -> 8.6 us  [the longest x1 2.79 us: on_device(): call(read_second, shape(tile, bf16), [block(count), *work(count, half), p...]
    pallas_call x1, Pallas kernels: 3.47 us -> 4.52 us  [on_device(): call(write_second, [shape((count, width), bf16), shape((2, rows, width),...]
  transfers between devices with their start and end apart: 6 -> 6, of which waited for: 2 -> 3; matrix products, arithmetic and copies ran while one was open for 1% -> 1% of each run, Pallas kernels for 8% -> 7%
where the time goes in v4:
time: 102 us
  starting transfers between devices  36.1 us (35%)
  blocking collectives  28 us (27%)
  Pallas kernels  19.5 us (19%)
  waiting for transfers between devices  16.4 us (16%)
    all_to_all x1, blocking collectives, on_device(): mine = lax.all_to_all(new, SPACE, 0, 0, tiled=True)  17.7 us
    all_to_all x1, blocking collectives, on_device(): parts = lax.all_to_all(parts, Z, 0, 0, tiled=True)  10.3 us
    all_to_all x1, starting transfers between devices, on_device(): tiles = lax.all_to_all(tiles, Z, 0, 0, tiled=True)  10 us
    all_to_all x1, waiting for transfers between devices, on_device(): packed = lax.all_to_all(packed, SPACE, 0, 0, tiled=True)  9.68 us
    ppermute x1, starting transfers between devices, on_device(): other = lax.ppermute(swapped, CORE, swap)  8.75 us
    ppermute x1, starting transfers between devices, on_device(): theirs = lax.ppermute(mine, CORE, swap)  8.54 us
    all_to_all x1, waiting for transfers between devices, on_device(): tiles = lax.all_to_all(tiles, Z, 0, 0, tiled=True)  6.65 us
    pallas_call x1, Pallas kernels, on_device(): call(write_second, [shape((count, width), bf16), shape((2, rows, width),...  4.52 us
  transfers between devices with their start and end apart: 6, of which 3 were waited for; matrix products, arithmetic and copies ran while one was open for 1% of the time, Pallas kernels for 7%

profile of v4, /device:TPU:1, one launch (start us, length us, event | category | flops | bytes accessed | tf_op | source)
XLA Modules:
  0.0 101.7 jit_solution(15095963664057779098)
XLA Ops:
  0.6 0.1 pad_add_fusion.position
  0.7 2.7 %prepare_read.1 = (bf16[256,1024]{1,0:T(8,128)(2,1)S(1)}, bf16[16,80,256]{2,1,0:T(8,128)(2,1)S(1)}, bf16[16,128,256]{2,1,0:T(8,128)(2,1)S(1)}) custom-call(s32[2]{0:T(128)S(1)} %pad_add_fusion.position, bf16[256,1024]{1,0:T(8,128)(2,1)} %tokens.1, bf16[512,1024]{1,0:T(8,128)(2,1)} %latents_hbm.1), custom_call_target="tpu_custom_call" | custom-call | flops 33554432 | bytes 1048576 | tf_op jit(solution)/shard_map/prepare_read/pallas_call | solution.py:384
  3.4 8.7 %collective-permute-start = (bf16[256,1024]{1,0:T(8,128)(2,1)}, bf16[256,1024]{1,0:T(8,128)(2,1)S(1)}, u32[]{:S(2)}, u32[]{:S(2)}) collective-permute-start(bf16[256,1024]{1,0:T(8,128)(2,1)} %tokens.1), channel_id=1, source_target_pairs={{0,32},{32,0},{1,33},{33,1},{2,34},{34,2},{3,35},{35,3},{4,36},{36... | collective-permute-start | bytes 1572872 | tf_op jit(solution)/shard_map/ppermute | solution.py:396
  12.1 1.6 %read_first.1 = (bf16[256,1024]{1,0:T(8,128)(2,1)S(1)}, f32[16,256]{1,0:T(8,128)S(1)}, f32[16,256]{1,0:T(8,128)S(1)}, f32[1024,256]{1,0:T(8,128)S(1)}) custom-call(bf16[256,1024]{1,0:T(8,128)(2,1)S(1)} %get-tuple-element.49.keys, bf16[16,80,256]{2,1,0:T(8,128)(2,1)S(1)} %get-tuple-element.50.values_t, bf16[16,128,256]{2,1,0:T(8,128)(2,1)S(1)} %get-tuple-element.48.queries_t), custom_call_target="tpu_custom_call" | custom-call | flops 268435456 | bytes 1048576 | tf_op jit(solution)/shard_map/read_first/pallas_call | solution.py:397
  13.7 0.0 copy-start.1
  13.8 0.1 collective-permute-done.tokens
  13.9 2.8 %read_second.1 = bf16[32,8,1152]{2,1,0:T(8,128)(2,1)} custom-call(bf16[256,1024]{1,0:T(8,128)(2,1)S(1)} %collective-permute-done.tokens, bf16[16,128,256]{2,1,0:T(8,128)(2,1)S(1)} %get-tuple-element.48.queries_t, f32[16,256]{1,0:T(8,128)S(1)} %get-tuple-element.51.peaks, f32[16,256]{1,0:T(8,128)S(1)} %get-tuple-element.52.totals, ...), custom_call_target="tpu_custom_call" | custom-call | flops 268435456 | bytes 1048576 | tf_op jit(solution)/shard_map/read_second/pallas_call | solution.py:403
  16.7 0.0 copy-done.1
  16.7 4.3 %all-to-all-start = ((bf16[32,8,1152]{2,1,0:T(8,128)(2,1)}), bf16[32,8,1152]{2,1,0:T(8,128)(2,1)S(1)}, u32[]{:S(2)}, u32[]{:S(2)}) async-start(bf16[32,8,1152]{2,1,0:T(8,128)(2,1)} %read_second.1), calls=%async_computation | async-start | bytes 1179648 | tf_op jit(solution)/shard_map/all_to_all | solution.py:414
  21.0 0.0 copy-done.2
  21.0 2.6 %collective-permute-start.1 = (bf16[1024,256]{1,0:T(8,128)(2,1)S(1)}, bf16[1024,256]{1,0:T(8,128)(2,1)S(1)}, u32[]{:S(2)}, u32[]{:S(2)}) collective-permute-start(bf16[1024,256]{1,0:T(8,128)(2,1)S(1)} %copy-done.2), channel_id=1, source_target_pairs={{0,32},{32,0},{1,33},{33,1},{2,34},{34,2},{3,35},{35,3},{4,36},{36... | collective-permute-start | bytes 1572872 | tf_op jit(solution)/shard_map/ppermute | solution.py:415
  23.6 0.0 copy-done.3
  23.6 1.9 %collective-permute-start.2 = (bf16[256,1024]{1,0:T(8,128)(2,1)S(1)}, bf16[256,1024]{1,0:T(8,128)(2,1)S(1)}, u32[]{:S(2)}, u32[]{:S(2)}) collective-permute-start(bf16[256,1024]{1,0:T(8,128)(2,1)S(1)} %copy-done.3), channel_id=1, source_target_pairs={{0,32},{32,0},{1,33},{33,1},{2,34},{34,2},{3,35},{35,3},{4,36},{36... | collective-permute-start | bytes 1572872 | tf_op jit(solution)/shard_map/ppermute | solution.py:415
  25.6 2.7 %prepare_queries.1.queries_t = bf16[16,256,256]{2,1,0:T(8,128)(2,1)} custom-call(bf16[256,1024]{1,0:T(8,128)(2,1)} %copy-done.1), custom_call_target="tpu_custom_call" | custom-call | flops 1048576 | bytes 1048576 | tf_op jit(solution)/shard_map/prepare_queries/pallas_call | solution.py:416
  28.3 0.7 constant_dynamic-slice_fusion.latents
  29.0 0.0 collective-permute-done.1.refs_2_
  29.0 0.0 collective-permute-done.2.refs_3_
  29.0 0.0 copy-start.5
  29.0 9.7 %all-to-all-done.arrived = bf16[32,8,1152]{2,1,0:T(8,128)(2,1)S(1)} async-done(((bf16[32,8,1152]{2,1,0:T(8,128)(2,1)}), bf16[32,8,1152]{2,1,0:T(8,128)(2,1)S(1)}, u32[]{:S(2)}, u32[]{:S(2)}) %all-to-all-start) | async-done | bytes 589856 | tf_op jit(solution)/shard_map/all_to_all | solution.py:414
  38.7 1.0 %combine_space.1 = bf16[8,8,1152]{2,1,0:T(8,128)(2,1)} custom-call(bf16[32,8,1152]{2,1,0:T(8,128)(2,1)S(1)} %all-to-all-done.arrived), custom_call_target="tpu_custom_call" | custom-call | bytes 1048576 | tf_op jit(solution)/shard_map/combine_space/pallas_call | solution.py:423
  39.7 0.0 copy-done.4
  39.7 10.0 %all-to-all-start.1 = ((bf16[8,8,1152]{2,1,0:T(8,128)(2,1)}), bf16[8,8,1152]{2,1,0:T(8,128)(2,1)S(1)}, u32[]{:S(2)}, u32[]{:S(2)}) async-start(bf16[8,8,1152]{2,1,0:T(8,128)(2,1)} %combine_space.1), calls=%async_computation.1 | async-start | bytes 294912 | tf_op jit(solution)/shard_map/all_to_all | solution.py:425
  49.7 1.5 %hold.1 = (bf16[1024,256]{1,0:T(8,128)(2,1)S(1)}, bf16[256,1024]{1,0:T(8,128)(2,1)S(1)}, bf16[1024,256]{1,0:T(8,128)(2,1)S(1)}, bf16[256,1024]{1,0:T(8,128)(2,1)S(1)}) custom-call(bf16[1024,256]{1,0:T(8,128)(2,1)} %refs_0_, bf16[256,1024]{1,0:T(8,128)(2,1)} %refs_1_, bf16[1024,256]{1,0:T(8,128)(2,1)} %copy-done.4, bf16[256,1024]{1,0:T(8,128)(2,1)} %copy-done.5), custom_call_target="tpu_custom_call" | custom-call | flops 1048576 | bytes 1048576 | tf_op jit(solution)/shard_map/hold/pallas_call | solution.py:426
  51.3 6.6 %all-to-all-done.1.arrived = bf16[8,8,1152]{2,1,0:T(8,128)(2,1)S(1)} async-done(((bf16[8,8,1152]{2,1,0:T(8,128)(2,1)}), bf16[8,8,1152]{2,1,0:T(8,128)(2,1)S(1)}, u32[]{:S(2)}, u32[]{:S(2)}) %all-to-all-start.1) | async-done | bytes 147488 | tf_op jit(solution)/shard_map/all_to_all | solution.py:425
  58.0 0.9 mlp.1
  58.9 10.3 %all_to_all.20.parts = bf16[8,8,1024]{2,1,0:T(8,128)(2,1)S(1)} all-to-all(bf16[8,8,1024]{2,1,0:T(8,128)(2,1)S(1)} %get-tuple-element.78), channel_id=1, replica_groups=mesh['tm_0'=8,'tm_1'=2,'space_0'=8,'space_1'=4] {'tm_0'}, dimensions={0} | all-to-all | bytes 262144 | tf_op jit(solution)/shard_map/all_to_all | solution.py:434
  69.2 0.1 finish.1
  69.2 17.7 %all_to_all.21.latents.mine = bf16[32,8,1024]{2,1,0:T(8,128)(2,1)S(1)} all-to-all(bf16[32,8,1024]{2,1,0:T(8,128)(2,1)S(1)} %finish.1), channel_id=1, replica_groups=mesh['tm_0'=8,'tm_1'=2,'space_0'=8,'space_1'=4] {'space_0','space_1'}, dimensions={0} | all-to-all | bytes 1048576 | tf_op jit(solution)/shard_map/all_to_all | solution.py:436
  87.0 8.5 %collective-permute-start.3 = (bf16[32,8,1024]{2,1,0:T(8,128)(2,1)S(1)}, bf16[32,8,1024]{2,1,0:T(8,128)(2,1)S(1)}, u32[]{:S(2)}, u32[]{:S(2)}) collective-permute-start(bf16[32,8,1024]{2,1,0:T(8,128)(2,1)S(1)} %all_to_all.21.latents.mine), channel_id=1, source_target_pairs={{0,32},{32,0},{1,33},{33,1},{2,34},{34,2},{3,35},{35,3},{4,36},{36... | collective-permute-start | bytes 1572872 | tf_op jit(solution)/shard_map/ppermute | solution.py:437
  95.5 1.7 %write_first.1 = (f32[16,256]{1,0:T(8,128)S(1)}, f32[16,256]{1,0:T(8,128)S(1)}, f32[1024,256]{1,0:T(8,128)S(1)}) custom-call(bf16[32,8,1024]{2,1,0:T(8,128)(2,1)S(1)} %all_to_all.21.latents.mine, bf16[16,256,256]{2,1,0:T(8,128)(2,1)S(1)} %copy-done), custom_call_target="tpu_custom_call" | custom-call | flops 268435456 | bytes 1048576 | tf_op jit(solution)/shard_map/write_first/pallas_call | solution.py:438
  97.2 0.0 collective-permute-done.3.latents
  97.2 4.5 %write_second.1 = (bf16[256,1024]{1,0:T(8,128)(2,1)}, bf16[2,8,1024]{2,1,0:T(8,128)(2,1)}) custom-call(s32[2]{0:T(128)S(1)} %pad_add_fusion.position, bf16[32,8,1024]{2,1,0:T(8,128)(2,1)S(1)} %collective-permute-done.3.latents, bf16[32,8,1024]{2,1,0:T(8,128)(2,1)S(1)} %all_to_all.21.latents.mine, bf16[16,256,256]{2,1,0:T(8,128)(2,1)S(1)} %copy-done, ...), custom_call_target="tpu_custom_call" | custom-call | flops 268435456 | bytes 1048576 | tf_op jit(solution)/shard_map/write_second/pallas_call | solution.py:442
  (6 shorter events, 0.0 us)
Async XLA Ops:
  3.4 10.5 %collective-permute-start = (bf16[256,1024]{1,0:T(8,128)(2,1)}, bf16[256,1024]{1,0:T(8,128)(2,1)S(1)}, u32[]{:S(2)}, u32[]{:S(2)}) collective-permute-start(bf16[256,1024]{1,0:T(8,128)(2,1)} %tokens.1), channel_id=1, source_target_pairs={{0,32},{32,0},{1,33},{33,1},{2,34},{34,2},{3,35},{35,3},{4,36},{36... | collective-permute-start | bytes 1572872 | tf_op jit(solution)/shard_map/ppermute | solution.py:396
  13.7 2.9 %copy-start.1 = (bf16[256,1024]{1,0:T(8,128)(2,1)}, bf16[256,1024]{1,0:T(8,128)(2,1)S(1)}, u32[]{:S(2)}) copy-start(bf16[256,1024]{1,0:T(8,128)(2,1)S(1)} %get-tuple-element.56.keys) | copy-start | bytes 1572868
  13.9 7.2 %copy-start.2 = (bf16[1024,256]{1,0:T(8,128)(2,1)S(1)}, bf16[1024,256]{1,0:T(8,128)(2,1)}, u32[]{:S(2)}) copy-start(bf16[1024,256]{1,0:T(8,128)(2,1)} %refs_0_) | copy-start | bytes 1572868
  13.9 9.7 %copy-start.3 = (bf16[256,1024]{1,0:T(8,128)(2,1)S(1)}, bf16[256,1024]{1,0:T(8,128)(2,1)}, u32[]{:S(2)}) copy-start(bf16[256,1024]{1,0:T(8,128)(2,1)} %refs_1_) | copy-start | bytes 1572868
  16.7 22.0 %all-to-all-start = ((bf16[32,8,1152]{2,1,0:T(8,128)(2,1)}), bf16[32,8,1152]{2,1,0:T(8,128)(2,1)S(1)}, u32[]{:S(2)}, u32[]{:S(2)}) async-start(bf16[32,8,1152]{2,1,0:T(8,128)(2,1)} %read_second.1), calls=%async_computation | async-start | bytes 1179648 | tf_op jit(solution)/shard_map/all_to_all | solution.py:414
  21.0 7.9 %collective-permute-start.1 = (bf16[1024,256]{1,0:T(8,128)(2,1)S(1)}, bf16[1024,256]{1,0:T(8,128)(2,1)S(1)}, u32[]{:S(2)}, u32[]{:S(2)}) collective-permute-start(bf16[1024,256]{1,0:T(8,128)(2,1)S(1)} %copy-done.2), channel_id=1, source_target_pairs={{0,32},{32,0},{1,33},{33,1},{2,34},{34,2},{3,35},{35,3},{4,36},{36... | collective-permute-start | bytes 1572872 | tf_op jit(solution)/shard_map/ppermute | solution.py:415
  23.6 5.4 %collective-permute-start.2 = (bf16[256,1024]{1,0:T(8,128)(2,1)S(1)}, bf16[256,1024]{1,0:T(8,128)(2,1)S(1)}, u32[]{:S(2)}, u32[]{:S(2)}) collective-permute-start(bf16[256,1024]{1,0:T(8,128)(2,1)S(1)} %copy-done.3), channel_id=1, source_target_pairs={{0,32},{32,0},{1,33},{33,1},{2,34},{34,2},{3,35},{35,3},{4,36},{36... | collective-permute-start | bytes 1572872 | tf_op jit(solution)/shard_map/ppermute | solution.py:415
  29.0 10.7 %copy-start.4 = (bf16[1024,256]{1,0:T(8,128)(2,1)}, bf16[1024,256]{1,0:T(8,128)(2,1)S(1)}, u32[]{:S(2)}) copy-start(bf16[1024,256]{1,0:T(8,128)(2,1)S(1)} %collective-permute-done.1.refs_2_) | copy-start | bytes 1572868
  29.0 10.7 %copy-start.5 = (bf16[256,1024]{1,0:T(8,128)(2,1)}, bf16[256,1024]{1,0:T(8,128)(2,1)S(1)}, u32[]{:S(2)}) copy-start(bf16[256,1024]{1,0:T(8,128)(2,1)S(1)} %collective-permute-done.2.refs_3_) | copy-start | bytes 1572868
  39.7 18.2 %all-to-all-start.1 = ((bf16[8,8,1152]{2,1,0:T(8,128)(2,1)}), bf16[8,8,1152]{2,1,0:T(8,128)(2,1)S(1)}, u32[]{:S(2)}, u32[]{:S(2)}) async-start(bf16[8,8,1152]{2,1,0:T(8,128)(2,1)} %combine_space.1), calls=%async_computation.1 | async-start | bytes 294912 | tf_op jit(solution)/shard_map/all_to_all | solution.py:425
  57.9 37.6 %copy-start = (bf16[16,256,256]{2,1,0:T(8,128)(2,1)S(1)}, bf16[16,256,256]{2,1,0:T(8,128)(2,1)}, u32[]{:S(2)}) copy-start(bf16[16,256,256]{2,1,0:T(8,128)(2,1)} %prepare_queries.1.queries_t) | copy-start | bytes 6291460
  87.0 10.2 %collective-permute-start.3 = (bf16[32,8,1024]{2,1,0:T(8,128)(2,1)S(1)}, bf16[32,8,1024]{2,1,0:T(8,128)(2,1)S(1)}, u32[]{:S(2)}, u32[]{:S(2)}) collective-permute-start(bf16[32,8,1024]{2,1,0:T(8,128)(2,1)S(1)} %all_to_all.21.latents.mine), channel_id=1, source_target_pairs={{0,32},{32,0},{1,33},{33,1},{2,34},{34,2},{3,35},{35,3},{4,36},{36... | collective-permute-start | bytes 1572872 | tf_op jit(solution)/shard_map/ppermute | solution.py:437

commit v5 on v4

--- a/solution.py
+++ b/solution.py
@@ -18,6 +18,7 @@
 TM_SPACE = TM + SPACE
 epsilon = 1e-05
 SCALE = HD**-0.5 * math.log2(math.e)
+PARTS = {7: (0, 8), 13: (8, 14), 15: (14, 16)}
 STATS = 128
 ONES = 16
 SLOTS = 6
@@ -65,8 +66,8 @@
             place_queries(queries_t, pair, part, 0)
 
 
-def put_normed(normed, tokens, first, last):
-    for at in range(first, last, LN_ROWS):
+def put_normed(normed, tokens):
+    for at in range(0, tokens.shape[0], LN_ROWS):
         rows = slice(at, at + LN_ROWS)
         normed[rows, :] = layer_norm(tokens[rows, :].astype(f32)).astype(bf16)
 
@@ -131,39 +132,22 @@
     return emit
 
 
-def prepare_read(
-    position, tokens_hbm, latents_hbm, keys, values_t, queries_t, tokens, latents, sems
+def prepare_read(position, latents_hbm, queries_t, latents, sem):
+    half = latents.shape[0]
+    start = pl.multiple_of(position[1] * half, half)
+    get = pltpu.make_async_copy(latents_hbm.at[pl.ds(start, half)], latents, sem)
+    get.start()
+    get.wait()
+    put_queries(queries_t, latents, False)
+
+
+def read_first(
+    tokens, queries_t, keys_hbm, peaks, totals, sums, keys, values_t, scores, weights, sem
 ):
-    half, count = latents.shape[0], tokens.shape[0]
-    start = position[1] * half
-    pieces = sems.shape[0] // 2
-    copies = []
-    for i in range(pieces):
-        size = count // pieces
-        rows = pl.ds(i * size, size)
-        copies.append(pltpu.make_async_copy(tokens_hbm.at[rows], tokens.at[rows], sems.at[i]))
-    for i in range(pieces):
-        size = half // pieces
-        source = pl.ds(pl.multiple_of(start + i * size, size), size)
-        copies.append(
-            pltpu.make_async_copy(
-                latents_hbm.at[source], latents.at[pl.ds(i * size, size)], sems.at[pieces + i]
-            )
-        )
-    for copy in copies:
-        copy.start()
-    for i in range(pieces):
-        copies[i].wait()
-        put_normed(keys, tokens, i * (count // pieces), (i + 1) * (count // pieces))
-    put_values(values_t, tokens)
-    for copy in copies[pieces:]:
-        copy.wait()
-    put_queries(queries_t, latents, False)
-
-
-def read_first(keys, values_t, queries_t, keys_hbm, peaks, totals, sums, scores, weights, sem):
+    put_normed(keys, tokens)
     keep = pltpu.make_async_copy(keys, keys_hbm, sem)
     keep.start()
+    put_values(values_t, tokens)
     attend(keys, queries_t, values_t, scores, weights, None, keep_in(peaks, totals, sums))
     keep.wait()
 
@@ -171,7 +155,7 @@
 def read_second(
     tokens, queries_t, peaks, totals, sums, packed_hbm, keys, values_t, scores, weights, stats, packed, sems
 ):
-    put_normed(keys, tokens, 0, tokens.shape[0])
+    put_normed(keys, tokens)
     put_values(values_t, tokens)
     tiles, rows, _ = packed.shape
     stats[...] = jnp.zeros_like(stats)
@@ -197,8 +181,8 @@
         if head % 2 == 1:
             both = jnp.concatenate([held[head - 1], held[head]], axis=0)
             packed[:, :, (head - 1) * HD : (head + 1) * HD] = pack(both)
-        if head == H // 2 - 1:
-            send(0, WIDTH // 2)
+        if head in PARTS and head < H - 1:
+            send(PARTS[head][0] * HD, PARTS[head][1] * HD)
 
     attend(
         keys, queries_t, values_t, scores, weights,
@@ -206,7 +190,7 @@
         joined(peaks, totals, sums, then),
     )
     packed[:, :, WIDTH:] = pack(stats[...])
-    send(WIDTH // 2, WIDTH + STATS)
+    send(PARTS[H - 1][0] * HD, WIDTH + STATS)
     for copy in copies:
         copy.wait()
 
@@ -293,9 +277,11 @@
 
 
 def write_second(
-    position, latents, mine, queries_t, tokens, peaks, totals, sums, out_hbm, owned,
-    lat, values, values_t, scores, weights, out, sems
+    position, latents, mine, queries_t, tokens_hbm, peaks, totals, sums, out_hbm, owned,
+    lat, values, values_t, scores, weights, out, tokens, sems
 ):
+    get = pltpu.make_async_copy(tokens_hbm, tokens, sems.at[3])
+    get.start()
     prepare_write(latents, lat, values, values_t)
     per = owned.shape[0]
     first = position[0] * per
@@ -315,13 +301,15 @@
     copies = []
 
     def then(head, peak, summed, total):
+        if head == 0:
+            get.wait()
         held[head] = summed * (1.0 / total)
         if head % 2 == 1:
             both = jnp.concatenate([held[head - 1], held[head]], axis=0)
             pair = slice((head - 1) * HD, (head + 1) * HD)
             out[:, pair] = (tokens[:, pair].astype(f32) + both.T).astype(bf16)
-        if head % (H // 2) == H // 2 - 1:
-            lanes = slice(head * HD + HD - WIDTH // 2, head * HD + HD)
+        if head in PARTS:
+            lanes = slice(PARTS[head][0] * HD, PARTS[head][1] * HD)
             copy = pltpu.make_async_copy(
                 out.at[:, lanes], out_hbm.at[:, lanes], sems.at[len(copies)]
             )
@@ -337,10 +325,10 @@
         copy.wait()
 
 
-def call(kernel, outs, scratch=(), inputs=1, scalars=False, flops=0, far=False, far_out=False, limit=16 << 20):
+def call(kernel, outs, scratch=(), inputs=1, scalars=False, flops=0, far=(), far_out=False, limit=16 << 20):
     whole = pl.BlockSpec(memory_space=pltpu.VMEM)
     single = not isinstance(outs, (list, tuple))
-    specs = [pl.BlockSpec(memory_space=pltpu.HBM) if far else whole] * inputs
+    specs = [pl.BlockSpec(memory_space=pltpu.HBM) if i in far else whole for i in range(inputs)]
     out_specs = [whole] * (1 if single else len(outs))
     if far_out:
         out_specs[0] = pl.BlockSpec(memory_space=pltpu.HBM)
@@ -380,31 +368,23 @@
         return [shape((H, queries), f32), shape((H, queries), f32), shape((width, queries), f32)]
 
     block = lambda rows: pltpu.VMEM((rows, width), bf16)
-    values, *buffers = work(count, half)
-    keys, values_t, queries_t = call(
-        prepare_read,
-        [
-            shape((count, width), bf16), shape((H, HD + ONES, count), bf16),
-            shape((H, 2 * HD, half), bf16),
-        ],
-        [block(count), block(half), pltpu.SemaphoreType.DMA((8,))],
-        inputs=2, scalars=True, flops=heavy // 8, far=True, limit=52019 << 10,
-    )(position, tokens, latents)
-    swapped, keys, values_t, queries_t = lax.optimization_barrier(
-        (tokens, keys, values_t, queries_t)
-    )
+    queries_t = call(
+        prepare_read, shape((H, 2 * HD, half), bf16), [block(half), pltpu.SemaphoreType.DMA],
+        inputs=1, scalars=True, flops=heavy // 8, far=(0,), limit=53248 << 10,
+    )(position, latents)
+    swapped, queries_t = lax.optimization_barrier((tokens, queries_t))
     other = lax.ppermute(swapped, CORE, swap)
     keys, *part = call(
         read_first, [shape((count, width), bf16), *state(half)],
-        [*buffers, pltpu.SemaphoreType.DMA],
-        inputs=3, flops=heavy, far_out=True, limit=50 << 20,
-    )(keys, values_t, queries_t)
+        [block(count), *work(count, half), pltpu.SemaphoreType.DMA],
+        inputs=2, flops=heavy, far_out=True,
+    )(tokens, queries_t)
     tile = (n_space, rows, width + STATS)
     packed = call(
         read_second, shape(tile, bf16),
         [
             block(count), *work(count, half), pltpu.VMEM((STATS, half), f32), pltpu.VMEM(tile, bf16),
-            pltpu.SemaphoreType.DMA((2,)),
+            pltpu.SemaphoreType.DMA((4,)),
         ],
         inputs=5, flops=heavy, far_out=True,
     )(other, queries_t, *part)
@@ -414,7 +394,7 @@
     packed = lax.all_to_all(packed, SPACE, 0, 0, tiled=True)
     up_other, down_other = lax.ppermute(up_late, CORE, swap), lax.ppermute(down_late, CORE, swap)
     queries_t = call(
-        prepare_queries, shape((H, 4 * HD, count), bf16), flops=1 << 20, limit=60 << 20
+        prepare_queries, shape((H, 4 * HD, count), bf16), flops=1 << 20, limit=53862 << 10
     )(keys)
     mine = lax.dynamic_slice_in_dim(late, core * half + place * rows, rows, 0)
     packed, queries_t, up_other, down_other, mine = lax.optimization_barrier(
@@ -425,7 +405,7 @@
     tiles = lax.all_to_all(tiles, Z, 0, 0, tiled=True)
     weights = call(
         hold, [shape(w.shape, bf16) for w in weights], [pltpu.SemaphoreType.DMA((4,))],
-        inputs=4, flops=1 << 20, far=True, limit=52838 << 10,
+        inputs=4, flops=1 << 20, far=range(4), limit=52838 << 10,
     )(*weights)
     tiles, *weights = lax.optimization_barrier((tiles, *weights))
     parts, middle = call(
@@ -443,10 +423,10 @@
         write_second,
         [shape((count, width), bf16), shape((2, rows, width), bf16)],
         [
-            block(half), block(half), *work(half, count), block(count),
-            pltpu.SemaphoreType.DMA((2,)),
+            block(half), block(half), *work(half, count), block(count), block(count),
+            pltpu.SemaphoreType.DMA((4,)),
         ],
-        inputs=7, scalars=True, flops=heavy, far_out=True,
+        inputs=7, scalars=True, flops=heavy, far=(3,), far_out=True,
     )(position, theirs, mine, queries_t, tokens, *part)
     return (new_tokens, new_latents.reshape(2 * rows, width))
 

time: 102 us -> 101 us (level)
  Pallas kernels: 19.5 us -> 17.6 us
  waiting for transfers between devices: 16.4 us -> 17.9 us
    all_to_all x1, waiting for transfers between devices: 9.68 us -> 11.3 us  [on_device(): packed = lax.all_to_all(packed, SPACE, 0, 0, tiled=True)]
    pallas_call x1, Pallas kernels: 2.71 us -> 1.67 us  [on_device(): call(prepare_queries, shape((H, 4 * HD, count), bf16), flops=1 << 20, lim...]
  transfers between devices with their start and end apart: 6 -> 6, of which waited for: 3 -> 2; matrix products, arithmetic and copies ran while one was open for 1% -> 1% of each run, Pallas kernels for 7% -> 7%
where the time goes in v5:
time: 101 us
  starting transfers between devices  35.7 us (35%)
  blocking collectives  28 us (28%)
  waiting for transfers between devices  17.9 us (18%)
  Pallas kernels  17.6 us (17%)
    all_to_all x1, blocking collectives, on_device(): mine = lax.all_to_all(new, SPACE, 0, 0, tiled=True)  17.6 us
    all_to_all x1, waiting for transfers between devices, on_device(): packed = lax.all_to_all(packed, SPACE, 0, 0, tiled=True)  11.3 us
    all_to_all x1, blocking collectives, on_device(): parts = lax.all_to_all(parts, Z, 0, 0, tiled=True)  10.4 us
    all_to_all x1, starting transfers between devices, on_device(): tiles = lax.all_to_all(tiles, Z, 0, 0, tiled=True)  10 us
    ppermute x1, starting transfers between devices, on_device(): other = lax.ppermute(swapped, CORE, swap)  8.75 us
    ppermute x1, starting transfers between devices, on_device(): theirs = lax.ppermute(mine, CORE, swap)  8.25 us
    all_to_all x1, waiting for transfers between devices, on_device(): tiles = lax.all_to_all(tiles, Z, 0, 0, tiled=True)  6.65 us
    all_to_all x1, starting transfers between devices, on_device(): packed = lax.all_to_all(packed, SPACE, 0, 0, tiled=True)  4.34 us
  transfers between devices with their start and end apart: 6, of which 2 were waited for; matrix products, arithmetic and copies ran while one was open for 1% of the time, Pallas kernels for 7%

profile of v5, /device:TPU:1, one launch (start us, length us, event | category | flops | bytes accessed | tf_op | source)
XLA Modules:
  0.0 100.9 jit_solution(1170974165773801526)
XLA Ops:
  0.6 0.0 copy-start.1
  0.6 0.1 pad_add_fusion.position
  0.7 1.8 %prepare_read.1.queries_t = bf16[16,128,256]{2,1,0:T(8,128)(2,1)S(1)} custom-call(s32[2]{0:T(128)S(1)} %pad_add_fusion.position, bf16[512,1024]{1,0:T(8,128)(2,1)} %latents_hbm.1), custom_call_target="tpu_custom_call" | custom-call | flops 33554432 | bytes 1048576 | tf_op jit(solution)/shard_map/prepare_read/pallas_call | solution.py:371
  2.5 0.0 copy-done.1
  2.5 8.7 %collective-permute-start = (bf16[256,1024]{1,0:T(8,128)(2,1)S(1)}, bf16[256,1024]{1,0:T(8,128)(2,1)S(1)}, u32[]{:S(2)}, u32[]{:S(2)}) collective-permute-start(bf16[256,1024]{1,0:T(8,128)(2,1)S(1)} %copy-done.1), channel_id=1, source_target_pairs={{0,32},{32,0},{1,33},{33,1},{2,34},{34,2},{3,35},{35,3},{4,36},{36... | collective-permute-start | bytes 1572872 | tf_op jit(solution)/shard_map/ppermute | solution.py:376
  11.3 2.0 %read_first.1 = (bf16[256,1024]{1,0:T(8,128)(2,1)S(1)}, f32[16,256]{1,0:T(8,128)S(1)}, f32[16,256]{1,0:T(8,128)S(1)}, f32[1024,256]{1,0:T(8,128)S(1)}) custom-call(bf16[256,1024]{1,0:T(8,128)(2,1)S(1)} %copy-done.1, bf16[16,128,256]{2,1,0:T(8,128)(2,1)S(1)} %prepare_read.1.queries_t), custom_call_target="tpu_custom_call" | custom-call | flops 268435456 | bytes 1048576 | tf_op jit(solution)/shard_map/read_first/pallas_call | solution.py:377
  13.3 0.0 collective-permute-done.tokens
  13.3 0.0 copy-start.2
  13.3 0.0 copy-start.3
  13.3 2.8 %read_second.1 = bf16[32,8,1152]{2,1,0:T(8,128)(2,1)} custom-call(bf16[256,1024]{1,0:T(8,128)(2,1)S(1)} %collective-permute-done.tokens, bf16[16,128,256]{2,1,0:T(8,128)(2,1)S(1)} %prepare_read.1.queries_t, f32[16,256]{1,0:T(8,128)S(1)} %get-tuple-element.41.peaks, f32[16,256]{1,0:T(8,128)S(1)} %get-tuple-element.42.totals, ...), custom_call_target="tpu_custom_call" | custom-call | flops 268435456 | bytes 1048576 | tf_op jit(solution)/shard_map/read_second/pallas_call | solution.py:383
  16.1 4.3 %all-to-all-start = ((bf16[32,8,1152]{2,1,0:T(8,128)(2,1)}), bf16[32,8,1152]{2,1,0:T(8,128)(2,1)S(1)}, u32[]{:S(2)}, u32[]{:S(2)}) async-start(bf16[32,8,1152]{2,1,0:T(8,128)(2,1)} %read_second.1), calls=%async_computation | async-start | bytes 1179648 | tf_op jit(solution)/shard_map/all_to_all | solution.py:394
  20.5 0.0 copy-done.2
  20.5 2.2 %collective-permute-start.1 = (bf16[1024,256]{1,0:T(8,128)(2,1)S(1)}, bf16[1024,256]{1,0:T(8,128)(2,1)S(1)}, u32[]{:S(2)}, u32[]{:S(2)}) collective-permute-start(bf16[1024,256]{1,0:T(8,128)(2,1)S(1)} %copy-done.2), channel_id=1, source_target_pairs={{0,32},{32,0},{1,33},{33,1},{2,34},{34,2},{3,35},{35,3},{4,36},{36... | collective-permute-start | bytes 1572872 | tf_op jit(solution)/shard_map/ppermute | solution.py:395
  22.7 2.1 %collective-permute-start.2 = (bf16[256,1024]{1,0:T(8,128)(2,1)S(1)}, bf16[256,1024]{1,0:T(8,128)(2,1)}, u32[]{:S(2)}, u32[]{:S(2)}) collective-permute-start(bf16[256,1024]{1,0:T(8,128)(2,1)S(1)} %copy-done.3), channel_id=1, source_target_pairs={{0,32},{32,0},{1,33},{33,1},{2,34},{34,2},{3,35},{35,3},{4,36},{36... | collective-permute-start | bytes 1572872 | tf_op jit(solution)/shard_map/ppermute | solution.py:395
  24.8 1.7 %prepare_queries.1.queries_t = bf16[16,256,256]{2,1,0:T(8,128)(2,1)} custom-call(bf16[256,1024]{1,0:T(8,128)(2,1)S(1)} %get-tuple-element.46.keys), custom_call_target="tpu_custom_call" | custom-call | flops 1048576 | bytes 1048576 | tf_op jit(solution)/shard_map/prepare_queries/pallas_call | solution.py:396
  26.5 0.7 constant_dynamic-slice_fusion.latents
  27.2 0.0 collective-permute-done.1.refs_2_
  27.2 0.0 collective-permute-done.2.refs_3_
  27.2 11.3 %all-to-all-done.arrived = bf16[32,8,1152]{2,1,0:T(8,128)(2,1)S(1)} async-done(((bf16[32,8,1152]{2,1,0:T(8,128)(2,1)}), bf16[32,8,1152]{2,1,0:T(8,128)(2,1)S(1)}, u32[]{:S(2)}, u32[]{:S(2)}) %all-to-all-start) | async-done | bytes 589856 | tf_op jit(solution)/shard_map/all_to_all | solution.py:394
  38.5 1.0 %combine_space.1 = bf16[8,8,1152]{2,1,0:T(8,128)(2,1)} custom-call(bf16[32,8,1152]{2,1,0:T(8,128)(2,1)S(1)} %all-to-all-done.arrived), custom_call_target="tpu_custom_call" | custom-call | bytes 1048576 | tf_op jit(solution)/shard_map/combine_space/pallas_call | solution.py:403
  39.5 10.0 %all-to-all-start.1 = ((bf16[8,8,1152]{2,1,0:T(8,128)(2,1)}), bf16[8,8,1152]{2,1,0:T(8,128)(2,1)S(1)}, u32[]{:S(2)}, u32[]{:S(2)}) async-start(bf16[8,8,1152]{2,1,0:T(8,128)(2,1)} %combine_space.1), calls=%async_computation.1 | async-start | bytes 294912 | tf_op jit(solution)/shard_map/all_to_all | solution.py:405
  49.6 1.5 %hold.1 = (bf16[1024,256]{1,0:T(8,128)(2,1)S(1)}, bf16[256,1024]{1,0:T(8,128)(2,1)S(1)}, bf16[1024,256]{1,0:T(8,128)(2,1)S(1)}, bf16[256,1024]{1,0:T(8,128)(2,1)S(1)}) custom-call(bf16[1024,256]{1,0:T(8,128)(2,1)} %refs_0_, bf16[256,1024]{1,0:T(8,128)(2,1)} %refs_1_, bf16[1024,256]{1,0:T(8,128)(2,1)} %copy-done.4, ...), custom_call_target="tpu_custom_call" | custom-call | flops 1048576 | bytes 1048576 | tf_op jit(solution)/shard_map/hold/pallas_call | solution.py:406
  51.1 6.6 %all-to-all-done.1.arrived = bf16[8,8,1152]{2,1,0:T(8,128)(2,1)S(1)} async-done(((bf16[8,8,1152]{2,1,0:T(8,128)(2,1)}), bf16[8,8,1152]{2,1,0:T(8,128)(2,1)S(1)}, u32[]{:S(2)}, u32[]{:S(2)}) %all-to-all-start.1) | async-done | bytes 147488 | tf_op jit(solution)/shard_map/all_to_all | solution.py:405
  57.8 0.9 mlp.1
  58.7 10.4 %all_to_all.20.parts = bf16[8,8,1024]{2,1,0:T(8,128)(2,1)S(1)} all-to-all(bf16[8,8,1024]{2,1,0:T(8,128)(2,1)S(1)} %get-tuple-element.68), channel_id=1, replica_groups=mesh['tm_0'=8,'tm_1'=2,'space_0'=8,'space_1'=4] {'tm_0'}, dimensions={0} | all-to-all | bytes 262144 | tf_op jit(solution)/shard_map/all_to_all | solution.py:414
  69.1 0.1 finish.1
  69.2 17.6 %all_to_all.21.latents.mine = bf16[32,8,1024]{2,1,0:T(8,128)(2,1)S(1)} all-to-all(bf16[32,8,1024]{2,1,0:T(8,128)(2,1)S(1)} %finish.1), channel_id=1, replica_groups=mesh['tm_0'=8,'tm_1'=2,'space_0'=8,'space_1'=4] {'space_0','space_1'}, dimensions={0} | all-to-all | bytes 1048576 | tf_op jit(solution)/shard_map/all_to_all | solution.py:416
  86.8 8.2 %collective-permute-start.3 = (bf16[32,8,1024]{2,1,0:T(8,128)(2,1)S(1)}, bf16[32,8,1024]{2,1,0:T(8,128)(2,1)S(1)}, u32[]{:S(2)}, u32[]{:S(2)}) collective-permute-start(bf16[32,8,1024]{2,1,0:T(8,128)(2,1)S(1)} %all_to_all.21.latents.mine), channel_id=1, source_target_pairs={{0,32},{32,0},{1,33},{33,1},{2,34},{34,2},{3,35},{35,3},{4,36},{36... | collective-permute-start | bytes 1572872 | tf_op jit(solution)/shard_map/ppermute | solution.py:417
  95.0 0.0 copy-done
  95.0 1.7 %write_first.1 = (f32[16,256]{1,0:T(8,128)S(1)}, f32[16,256]{1,0:T(8,128)S(1)}, f32[1024,256]{1,0:T(8,128)S(1)}) custom-call(bf16[32,8,1024]{2,1,0:T(8,128)(2,1)S(1)} %all_to_all.21.latents.mine, bf16[16,256,256]{2,1,0:T(8,128)(2,1)S(1)} %copy-done), custom_call_target="tpu_custom_call" | custom-call | flops 268435456 | bytes 1048576 | tf_op jit(solution)/shard_map/write_first/pallas_call | solution.py:418
  96.7 0.0 collective-permute-done.3.latents
  96.7 4.2 %write_second.1 = (bf16[256,1024]{1,0:T(8,128)(2,1)}, bf16[2,8,1024]{2,1,0:T(8,128)(2,1)}) custom-call(s32[2]{0:T(128)S(1)} %pad_add_fusion.position, bf16[32,8,1024]{2,1,0:T(8,128)(2,1)S(1)} %collective-permute-done.3.latents, bf16[32,8,1024]{2,1,0:T(8,128)(2,1)S(1)} %all_to_all.21.latents.mine, bf16[16,256,256]{2,1,0:T(8,128)(2,1)S(1)} %copy-done, ...), custom_call_target="tpu_custom_call" | custom-call | flops 268435456 | bytes 1048576 | tf_op jit(solution)/shard_map/write_second/pallas_call | solution.py:422
  (4 shorter events, 0.0 us)
Async XLA Ops:
  0.6 1.9 %copy-start.1 = (bf16[256,1024]{1,0:T(8,128)(2,1)S(1)}, bf16[256,1024]{1,0:T(8,128)(2,1)}, u32[]{:S(2)}) copy-start(bf16[256,1024]{1,0:T(8,128)(2,1)} %tokens_hbm.1) | copy-start | bytes 1572868
  2.5 10.7 %collective-permute-start = (bf16[256,1024]{1,0:T(8,128)(2,1)S(1)}, bf16[256,1024]{1,0:T(8,128)(2,1)S(1)}, u32[]{:S(2)}, u32[]{:S(2)}) collective-permute-start(bf16[256,1024]{1,0:T(8,128)(2,1)S(1)} %copy-done.1), channel_id=1, source_target_pairs={{0,32},{32,0},{1,33},{33,1},{2,34},{34,2},{3,35},{35,3},{4,36},{36... | collective-permute-start | bytes 1572872 | tf_op jit(solution)/shard_map/ppermute | solution.py:376
  13.3 7.2 %copy-start.2 = (bf16[1024,256]{1,0:T(8,128)(2,1)S(1)}, bf16[1024,256]{1,0:T(8,128)(2,1)}, u32[]{:S(2)}) copy-start(bf16[1024,256]{1,0:T(8,128)(2,1)} %refs_0_) | copy-start | bytes 1572868
  13.3 9.4 %copy-start.3 = (bf16[256,1024]{1,0:T(8,128)(2,1)S(1)}, bf16[256,1024]{1,0:T(8,128)(2,1)}, u32[]{:S(2)}) copy-start(bf16[256,1024]{1,0:T(8,128)(2,1)} %refs_1_) | copy-start | bytes 1572868
  16.1 22.4 %all-to-all-start = ((bf16[32,8,1152]{2,1,0:T(8,128)(2,1)}), bf16[32,8,1152]{2,1,0:T(8,128)(2,1)S(1)}, u32[]{:S(2)}, u32[]{:S(2)}) async-start(bf16[32,8,1152]{2,1,0:T(8,128)(2,1)} %read_second.1), calls=%async_computation | async-start | bytes 1179648 | tf_op jit(solution)/shard_map/all_to_all | solution.py:394
  20.5 6.8 %collective-permute-start.1 = (bf16[1024,256]{1,0:T(8,128)(2,1)S(1)}, bf16[1024,256]{1,0:T(8,128)(2,1)S(1)}, u32[]{:S(2)}, u32[]{:S(2)}) collective-permute-start(bf16[1024,256]{1,0:T(8,128)(2,1)S(1)} %copy-done.2), channel_id=1, source_target_pairs={{0,32},{32,0},{1,33},{33,1},{2,34},{34,2},{3,35},{35,3},{4,36},{36... | collective-permute-start | bytes 1572872 | tf_op jit(solution)/shard_map/ppermute | solution.py:395
  22.7 4.5 %collective-permute-start.2 = (bf16[256,1024]{1,0:T(8,128)(2,1)S(1)}, bf16[256,1024]{1,0:T(8,128)(2,1)}, u32[]{:S(2)}, u32[]{:S(2)}) collective-permute-start(bf16[256,1024]{1,0:T(8,128)(2,1)S(1)} %copy-done.3), channel_id=1, source_target_pairs={{0,32},{32,0},{1,33},{33,1},{2,34},{34,2},{3,35},{35,3},{4,36},{36... | collective-permute-start | bytes 1572872 | tf_op jit(solution)/shard_map/ppermute | solution.py:395
  27.2 12.3 %copy-start.4 = (bf16[1024,256]{1,0:T(8,128)(2,1)}, bf16[1024,256]{1,0:T(8,128)(2,1)S(1)}, u32[]{:S(2)}) copy-start(bf16[1024,256]{1,0:T(8,128)(2,1)S(1)} %collective-permute-done.1.refs_2_) | copy-start | bytes 1572868
  39.5 18.2 %all-to-all-start.1 = ((bf16[8,8,1152]{2,1,0:T(8,128)(2,1)}), bf16[8,8,1152]{2,1,0:T(8,128)(2,1)S(1)}, u32[]{:S(2)}, u32[]{:S(2)}) async-start(bf16[8,8,1152]{2,1,0:T(8,128)(2,1)} %combine_space.1), calls=%async_computation.1 | async-start | bytes 294912 | tf_op jit(solution)/shard_map/all_to_all | solution.py:405
  57.8 37.3 %copy-start = (bf16[16,256,256]{2,1,0:T(8,128)(2,1)S(1)}, bf16[16,256,256]{2,1,0:T(8,128)(2,1)}, u32[]{:S(2)}) copy-start(bf16[16,256,256]{2,1,0:T(8,128)(2,1)} %prepare_queries.1.queries_t) | copy-start | bytes 6291460
  86.8 9.9 %collective-permute-start.3 = (bf16[32,8,1024]{2,1,0:T(8,128)(2,1)S(1)}, bf16[32,8,1024]{2,1,0:T(8,128)(2,1)S(1)}, u32[]{:S(2)}, u32[]{:S(2)}) collective-permute-start(bf16[32,8,1024]{2,1,0:T(8,128)(2,1)S(1)} %all_to_all.21.latents.mine), channel_id=1, source_target_pairs={{0,32},{32,0},{1,33},{33,1},{2,34},{34,2},{3,35},{35,3},{4,36},{36... | collective-permute-start | bytes 1572872 | tf_op jit(solution)/shard_map/ppermute | solution.py:417

commit v6 on v5

--- a/solution.py
+++ b/solution.py
@@ -271,17 +271,20 @@
     put_values(values_t, values)
 
 
-def write_first(latents, queries_t, peaks, totals, sums, lat, values, values_t, scores, weights):
+def write_first(
+    latents, queries_t, tokens_hbm, peaks, totals, sums, tokens, lat, values, values_t, scores, weights, sem
+):
+    get = pltpu.make_async_copy(tokens_hbm, tokens, sem)
+    get.start()
     prepare_write(latents, lat, values, values_t)
     attend(lat, queries_t, values_t, scores, weights, None, keep_in(peaks, totals, sums))
+    get.wait()
 
 
 def write_second(
-    position, latents, mine, queries_t, tokens_hbm, peaks, totals, sums, out_hbm, owned,
-    lat, values, values_t, scores, weights, out, tokens, sems
+    position, latents, mine, queries_t, tokens, peaks, totals, sums, out, owned,
+    lat, values, values_t, scores, weights
 ):
-    get = pltpu.make_async_copy(tokens_hbm, tokens, sems.at[3])
-    get.start()
     prepare_write(latents, lat, values, values_t)
     per = owned.shape[0]
     first = position[0] * per
@@ -298,31 +301,19 @@
         owned[...] = mine[pl.ds(start, per)]
 
     held = {}
-    copies = []
 
     def then(head, peak, summed, total):
-        if head == 0:
-            get.wait()
         held[head] = summed * (1.0 / total)
         if head % 2 == 1:
             both = jnp.concatenate([held[head - 1], held[head]], axis=0)
             pair = slice((head - 1) * HD, (head + 1) * HD)
             out[:, pair] = (tokens[:, pair].astype(f32) + both.T).astype(bf16)
-        if head in PARTS:
-            lanes = slice(PARTS[head][0] * HD, PARTS[head][1] * HD)
-            copy = pltpu.make_async_copy(
-                out.at[:, lanes], out_hbm.at[:, lanes], sems.at[len(copies)]
-            )
-            copy.start()
-            copies.append(copy)
 
     attend(
         lat, queries_t, values_t, scores, weights,
         lambda head: peaks[head : head + 1, :],
         joined(peaks, totals, sums, then),
     )
-    for copy in copies:
-        copy.wait()
 
 
 def call(kernel, outs, scratch=(), inputs=1, scalars=False, flops=0, far=(), far_out=False, limit=16 << 20):
@@ -384,7 +375,7 @@
         read_second, shape(tile, bf16),
         [
             block(count), *work(count, half), pltpu.VMEM((STATS, half), f32), pltpu.VMEM(tile, bf16),
-            pltpu.SemaphoreType.DMA((4,)),
+            pltpu.SemaphoreType.DMA((3,)),
         ],
         inputs=5, flops=heavy, far_out=True,
     )(other, queries_t, *part)
@@ -415,19 +406,17 @@
     new = call(finish, shape((n_space, rows, width), bf16), inputs=2)(parts, middle)
     mine = lax.all_to_all(new, SPACE, 0, 0, tiled=True)
     theirs = lax.ppermute(mine, CORE, swap)
-    part = call(
-        write_first, state(count), [block(half), block(half), *work(half, count)],
-        inputs=2, flops=heavy,
-    )(mine, queries_t)
+    *part, held = call(
+        write_first, [*state(count), shape((count, width), bf16)],
+        [block(half), block(half), *work(half, count), pltpu.SemaphoreType.DMA],
+        inputs=3, flops=heavy, far=(2,),
+    )(mine, queries_t, tokens)
     new_tokens, new_latents = call(
         write_second,
         [shape((count, width), bf16), shape((2, rows, width), bf16)],
-        [
-            block(half), block(half), *work(half, count), block(count), block(count),
-            pltpu.SemaphoreType.DMA((4,)),
-        ],
-        inputs=7, scalars=True, flops=heavy, far=(3,), far_out=True,
-    )(position, theirs, mine, queries_t, tokens, *part)
+        [block(half), block(half), *work(half, count)],
+        inputs=7, scalars=True, flops=heavy,
+    )(position, theirs, mine, queries_t, held, *part)
     return (new_tokens, new_latents.reshape(2 * rows, width))
 
 

time: 101 us -> 101 us (level)
  no operation moved by 1% of the time
where the time goes in v6:
time: 101 us; the launch traced here: 100 us
  starting transfers between devices  35.7 us (35%)
  blocking collectives  28 us (28%)
  waiting for transfers between devices  17.9 us (18%)
  Pallas kernels  16.9 us (17%)
    all_to_all x1, blocking collectives, on_device(): mine = lax.all_to_all(new, SPACE, 0, 0, tiled=True)  17.6 us
    all_to_all x1, waiting for transfers between devices, on_device(): packed = lax.all_to_all(packed, SPACE, 0, 0, tiled=True)  11.3 us
    all_to_all x1, blocking collectives, on_device(): parts = lax.all_to_all(parts, Z, 0, 0, tiled=True)  10.4 us
    all_to_all x1, starting transfers between devices, on_device(): tiles = lax.all_to_all(tiles, Z, 0, 0, tiled=True)  10 us
    ppermute x1, starting transfers between devices, on_device(): other = lax.ppermute(swapped, CORE, swap)  8.75 us
    ppermute x1, starting transfers between devices, on_device(): theirs = lax.ppermute(mine, CORE, swap)  8.25 us
    all_to_all x1, waiting for transfers between devices, on_device(): tiles = lax.all_to_all(tiles, Z, 0, 0, tiled=True)  6.65 us
    all_to_all x1, starting transfers between devices, on_device(): packed = lax.all_to_all(packed, SPACE, 0, 0, tiled=True)  4.34 us
  transfers between devices with their start and end apart: 6, of which 2 were waited for; matrix products, arithmetic and copies ran while one was open for 1% of the time, Pallas kernels for 7%

profile of v6, /device:TPU:1, one launch (start us, length us, event | category | flops | bytes accessed | tf_op | source)
XLA Modules:
  0.0 100.2 jit_solution(2924223844323432401)
XLA Ops:
  0.6 0.0 copy-start.1
  0.6 0.1 pad_add_fusion.position
  0.7 1.8 %prepare_read.1.queries_t = bf16[16,128,256]{2,1,0:T(8,128)(2,1)S(1)} custom-call(s32[2]{0:T(128)S(1)} %pad_add_fusion.position, bf16[512,1024]{1,0:T(8,128)(2,1)} %latents_hbm.1), custom_call_target="tpu_custom_call" | custom-call | flops 33554432 | bytes 1048576 | tf_op jit(solution)/shard_map/prepare_read/pallas_call | solution.py:362
  2.5 0.0 copy-done.1
  2.5 8.7 %collective-permute-start = (bf16[256,1024]{1,0:T(8,128)(2,1)S(1)}, bf16[256,1024]{1,0:T(8,128)(2,1)S(1)}, u32[]{:S(2)}, u32[]{:S(2)}) collective-permute-start(bf16[256,1024]{1,0:T(8,128)(2,1)S(1)} %copy-done.1), channel_id=1, source_target_pairs={{0,32},{32,0},{1,33},{33,1},{2,34},{34,2},{3,35},{35,3},{4,36},{36... | collective-permute-start | bytes 1572872 | tf_op jit(solution)/shard_map/ppermute | solution.py:367
  11.3 2.0 %read_first.1 = (bf16[256,1024]{1,0:T(8,128)(2,1)S(1)}, f32[16,256]{1,0:T(8,128)S(1)}, f32[16,256]{1,0:T(8,128)S(1)}, f32[1024,256]{1,0:T(8,128)S(1)}) custom-call(bf16[256,1024]{1,0:T(8,128)(2,1)S(1)} %copy-done.1, bf16[16,128,256]{2,1,0:T(8,128)(2,1)S(1)} %prepare_read.1.queries_t), custom_call_target="tpu_custom_call" | custom-call | flops 268435456 | bytes 1048576 | tf_op jit(solution)/shard_map/read_first/pallas_call | solution.py:368
  13.3 0.0 collective-permute-done.tokens
  13.3 0.0 copy-start.2
  13.3 0.0 copy-start.3
  13.3 2.8 %read_second.1 = bf16[32,8,1152]{2,1,0:T(8,128)(2,1)} custom-call(bf16[256,1024]{1,0:T(8,128)(2,1)S(1)} %collective-permute-done.tokens, bf16[16,128,256]{2,1,0:T(8,128)(2,1)S(1)} %prepare_read.1.queries_t, f32[16,256]{1,0:T(8,128)S(1)} %get-tuple-element.42.peaks, f32[16,256]{1,0:T(8,128)S(1)} %get-tuple-element.43.totals, ...), custom_call_target="tpu_custom_call" | custom-call | flops 268435456 | bytes 1048576 | tf_op jit(solution)/shard_map/read_second/pallas_call | solution.py:374
  16.1 4.3 %all-to-all-start = ((bf16[32,8,1152]{2,1,0:T(8,128)(2,1)}), bf16[32,8,1152]{2,1,0:T(8,128)(2,1)S(1)}, u32[]{:S(2)}, u32[]{:S(2)}) async-start(bf16[32,8,1152]{2,1,0:T(8,128)(2,1)} %read_second.1), calls=%async_computation | async-start | bytes 1179648 | tf_op jit(solution)/shard_map/all_to_all | solution.py:385
  20.5 0.0 copy-done.2
  20.5 2.2 %collective-permute-start.1 = (bf16[1024,256]{1,0:T(8,128)(2,1)S(1)}, bf16[1024,256]{1,0:T(8,128)(2,1)S(1)}, u32[]{:S(2)}, u32[]{:S(2)}) collective-permute-start(bf16[1024,256]{1,0:T(8,128)(2,1)S(1)} %copy-done.2), channel_id=1, source_target_pairs={{0,32},{32,0},{1,33},{33,1},{2,34},{34,2},{3,35},{35,3},{4,36},{36... | collective-permute-start | bytes 1572872 | tf_op jit(solution)/shard_map/ppermute | solution.py:386
  22.7 0.0 copy-done.3
  22.7 2.1 %collective-permute-start.2 = (bf16[256,1024]{1,0:T(8,128)(2,1)S(1)}, bf16[256,1024]{1,0:T(8,128)(2,1)}, u32[]{:S(2)}, u32[]{:S(2)}) collective-permute-start(bf16[256,1024]{1,0:T(8,128)(2,1)S(1)} %copy-done.3), channel_id=1, source_target_pairs={{0,32},{32,0},{1,33},{33,1},{2,34},{34,2},{3,35},{35,3},{4,36},{36... | collective-permute-start | bytes 1572872 | tf_op jit(solution)/shard_map/ppermute | solution.py:386
  24.8 1.7 %prepare_queries.1.queries_t = bf16[16,256,256]{2,1,0:T(8,128)(2,1)} custom-call(bf16[256,1024]{1,0:T(8,128)(2,1)S(1)} %get-tuple-element.47.keys), custom_call_target="tpu_custom_call" | custom-call | flops 1048576 | bytes 1048576 | tf_op jit(solution)/shard_map/prepare_queries/pallas_call | solution.py:387
  26.5 0.7 constant_dynamic-slice_fusion.latents
  27.2 0.0 collective-permute-done.1.refs_2_
  27.2 0.0 collective-permute-done.2.refs_3_
  27.2 11.3 %all-to-all-done.arrived = bf16[32,8,1152]{2,1,0:T(8,128)(2,1)S(1)} async-done(((bf16[32,8,1152]{2,1,0:T(8,128)(2,1)}), bf16[32,8,1152]{2,1,0:T(8,128)(2,1)S(1)}, u32[]{:S(2)}, u32[]{:S(2)}) %all-to-all-start) | async-done | bytes 589856 | tf_op jit(solution)/shard_map/all_to_all | solution.py:385
  38.5 1.0 %combine_space.1 = bf16[8,8,1152]{2,1,0:T(8,128)(2,1)} custom-call(bf16[32,8,1152]{2,1,0:T(8,128)(2,1)S(1)} %all-to-all-done.arrived), custom_call_target="tpu_custom_call" | custom-call | bytes 1048576 | tf_op jit(solution)/shard_map/combine_space/pallas_call | solution.py:394
  39.5 10.0 %all-to-all-start.1 = ((bf16[8,8,1152]{2,1,0:T(8,128)(2,1)}), bf16[8,8,1152]{2,1,0:T(8,128)(2,1)S(1)}, u32[]{:S(2)}, u32[]{:S(2)}) async-start(bf16[8,8,1152]{2,1,0:T(8,128)(2,1)} %combine_space.1), calls=%async_computation.1 | async-start | bytes 294912 | tf_op jit(solution)/shard_map/all_to_all | solution.py:396
  49.6 1.5 %hold.1 = (bf16[1024,256]{1,0:T(8,128)(2,1)S(1)}, bf16[256,1024]{1,0:T(8,128)(2,1)S(1)}, bf16[1024,256]{1,0:T(8,128)(2,1)S(1)}, bf16[256,1024]{1,0:T(8,128)(2,1)S(1)}) custom-call(bf16[1024,256]{1,0:T(8,128)(2,1)} %refs_0_, bf16[256,1024]{1,0:T(8,128)(2,1)} %refs_1_, bf16[1024,256]{1,0:T(8,128)(2,1)} %copy-done.4, ...), custom_call_target="tpu_custom_call" | custom-call | flops 1048576 | bytes 1048576 | tf_op jit(solution)/shard_map/hold/pallas_call | solution.py:397
  51.1 6.6 %all-to-all-done.1.arrived = bf16[8,8,1152]{2,1,0:T(8,128)(2,1)S(1)} async-done(((bf16[8,8,1152]{2,1,0:T(8,128)(2,1)}), bf16[8,8,1152]{2,1,0:T(8,128)(2,1)S(1)}, u32[]{:S(2)}, u32[]{:S(2)}) %all-to-all-start.1) | async-done | bytes 147488 | tf_op jit(solution)/shard_map/all_to_all | solution.py:396
  57.8 0.9 mlp.1
  58.7 10.4 %all_to_all.20.parts = bf16[8,8,1024]{2,1,0:T(8,128)(2,1)S(1)} all-to-all(bf16[8,8,1024]{2,1,0:T(8,128)(2,1)S(1)} %get-tuple-element.69), channel_id=1, replica_groups=mesh['tm_0'=8,'tm_1'=2,'space_0'=8,'space_1'=4] {'tm_0'}, dimensions={0} | all-to-all | bytes 262144 | tf_op jit(solution)/shard_map/all_to_all | solution.py:405
  69.1 0.1 finish.1
  69.2 17.6 %all_to_all.21.latents.mine = bf16[32,8,1024]{2,1,0:T(8,128)(2,1)S(1)} all-to-all(bf16[32,8,1024]{2,1,0:T(8,128)(2,1)S(1)} %finish.1), channel_id=1, replica_groups=mesh['tm_0'=8,'tm_1'=2,'space_0'=8,'space_1'=4] {'space_0','space_1'}, dimensions={0} | all-to-all | bytes 1048576 | tf_op jit(solution)/shard_map/all_to_all | solution.py:407
  86.8 8.2 %collective-permute-start.3 = (bf16[32,8,1024]{2,1,0:T(8,128)(2,1)S(1)}, bf16[32,8,1024]{2,1,0:T(8,128)(2,1)S(1)}, u32[]{:S(2)}, u32[]{:S(2)}) collective-permute-start(bf16[32,8,1024]{2,1,0:T(8,128)(2,1)S(1)} %all_to_all.21.latents.mine), channel_id=1, source_target_pairs={{0,32},{32,0},{1,33},{33,1},{2,34},{34,2},{3,35},{35,3},{4,36},{36... | collective-permute-start | bytes 1572872 | tf_op jit(solution)/shard_map/ppermute | solution.py:408
  95.0 1.7 %write_first.1 = (f32[16,256]{1,0:T(8,128)S(1)}, f32[16,256]{1,0:T(8,128)S(1)}, f32[1024,256]{1,0:T(8,128)S(1)}, bf16[256,1024]{1,0:T(8,128)(2,1)S(1)}) custom-call(bf16[32,8,1024]{2,1,0:T(8,128)(2,1)S(1)} %all_to_all.21.latents.mine, bf16[16,256,256]{2,1,0:T(8,128)(2,1)S(1)} %copy-done, bf16[256,1024]{1,0:T(8,128)(2,1)S(1)} %copy-done.1), custom_call_target="tpu_custom_call" | custom-call | flops 268435456 | bytes 1048576 | tf_op jit(solution)/shard_map/write_first/pallas_call | solution.py:409
  96.8 0.0 collective-permute-done.3.latents
  96.8 3.4 %write_second.1 = (bf16[256,1024]{1,0:T(8,128)(2,1)}, bf16[2,8,1024]{2,1,0:T(8,128)(2,1)}) custom-call(s32[2]{0:T(128)S(1)} %pad_add_fusion.position, bf16[32,8,1024]{2,1,0:T(8,128)(2,1)S(1)} %collective-permute-done.3.latents, bf16[32,8,1024]{2,1,0:T(8,128)(2,1)S(1)} %all_to_all.21.latents.mine, bf16[16,256,256]{2,1,0:T(8,128)(2,1)S(1)} %copy-done, ...), custom_call_target="tpu_custom_call" | custom-call | flops 268435456 | bytes 1048576 | tf_op jit(solution)/shard_map/write_second/pallas_call | solution.py:414
  (4 shorter events, 0.0 us)
Async XLA Ops:
  0.6 1.9 %copy-start.1 = (bf16[256,1024]{1,0:T(8,128)(2,1)S(1)}, bf16[256,1024]{1,0:T(8,128)(2,1)}, u32[]{:S(2)}) copy-start(bf16[256,1024]{1,0:T(8,128)(2,1)} %tokens_hbm.1) | copy-start | bytes 1572868
  2.5 10.7 %collective-permute-start = (bf16[256,1024]{1,0:T(8,128)(2,1)S(1)}, bf16[256,1024]{1,0:T(8,128)(2,1)S(1)}, u32[]{:S(2)}, u32[]{:S(2)}) collective-permute-start(bf16[256,1024]{1,0:T(8,128)(2,1)S(1)} %copy-done.1), channel_id=1, source_target_pairs={{0,32},{32,0},{1,33},{33,1},{2,34},{34,2},{3,35},{35,3},{4,36},{36... | collective-permute-start | bytes 1572872 | tf_op jit(solution)/shard_map/ppermute | solution.py:367
  13.3 7.2 %copy-start.2 = (bf16[1024,256]{1,0:T(8,128)(2,1)S(1)}, bf16[1024,256]{1,0:T(8,128)(2,1)}, u32[]{:S(2)}) copy-start(bf16[1024,256]{1,0:T(8,128)(2,1)} %refs_0_) | copy-start | bytes 1572868
  13.3 9.4 %copy-start.3 = (bf16[256,1024]{1,0:T(8,128)(2,1)S(1)}, bf16[256,1024]{1,0:T(8,128)(2,1)}, u32[]{:S(2)}) copy-start(bf16[256,1024]{1,0:T(8,128)(2,1)} %refs_1_) | copy-start | bytes 1572868
  16.1 22.4 %all-to-all-start = ((bf16[32,8,1152]{2,1,0:T(8,128)(2,1)}), bf16[32,8,1152]{2,1,0:T(8,128)(2,1)S(1)}, u32[]{:S(2)}, u32[]{:S(2)}) async-start(bf16[32,8,1152]{2,1,0:T(8,128)(2,1)} %read_second.1), calls=%async_computation | async-start | bytes 1179648 | tf_op jit(solution)/shard_map/all_to_all | solution.py:385
  20.5 6.8 %collective-permute-start.1 = (bf16[1024,256]{1,0:T(8,128)(2,1)S(1)}, bf16[1024,256]{1,0:T(8,128)(2,1)S(1)}, u32[]{:S(2)}, u32[]{:S(2)}) collective-permute-start(bf16[1024,256]{1,0:T(8,128)(2,1)S(1)} %copy-done.2), channel_id=1, source_target_pairs={{0,32},{32,0},{1,33},{33,1},{2,34},{34,2},{3,35},{35,3},{4,36},{36... | collective-permute-start | bytes 1572872 | tf_op jit(solution)/shard_map/ppermute | solution.py:386
  22.7 4.5 %collective-permute-start.2 = (bf16[256,1024]{1,0:T(8,128)(2,1)S(1)}, bf16[256,1024]{1,0:T(8,128)(2,1)}, u32[]{:S(2)}, u32[]{:S(2)}) collective-permute-start(bf16[256,1024]{1,0:T(8,128)(2,1)S(1)} %copy-done.3), channel_id=1, source_target_pairs={{0,32},{32,0},{1,33},{33,1},{2,34},{34,2},{3,35},{35,3},{4,36},{36... | collective-permute-start | bytes 1572872 | tf_op jit(solution)/shard_map/ppermute | solution.py:386
  27.2 12.3 %copy-start.4 = (bf16[1024,256]{1,0:T(8,128)(2,1)}, bf16[1024,256]{1,0:T(8,128)(2,1)S(1)}, u32[]{:S(2)}) copy-start(bf16[1024,256]{1,0:T(8,128)(2,1)S(1)} %collective-permute-done.1.refs_2_) | copy-start | bytes 1572868
  39.5 18.2 %all-to-all-start.1 = ((bf16[8,8,1152]{2,1,0:T(8,128)(2,1)}), bf16[8,8,1152]{2,1,0:T(8,128)(2,1)S(1)}, u32[]{:S(2)}, u32[]{:S(2)}) async-start(bf16[8,8,1152]{2,1,0:T(8,128)(2,1)} %combine_space.1), calls=%async_computation.1 | async-start | bytes 294912 | tf_op jit(solution)/shard_map/all_to_all | solution.py:396
  57.8 37.3 %copy-start = (bf16[16,256,256]{2,1,0:T(8,128)(2,1)S(1)}, bf16[16,256,256]{2,1,0:T(8,128)(2,1)}, u32[]{:S(2)}) copy-start(bf16[16,256,256]{2,1,0:T(8,128)(2,1)} %prepare_queries.1.queries_t) | copy-start | bytes 6291460
  86.8 10.0 %collective-permute-start.3 = (bf16[32,8,1024]{2,1,0:T(8,128)(2,1)S(1)}, bf16[32,8,1024]{2,1,0:T(8,128)(2,1)S(1)}, u32[]{:S(2)}, u32[]{:S(2)}) collective-permute-start(bf16[32,8,1024]{2,1,0:T(8,128)(2,1)S(1)} %all_to_all.21.latents.mine), channel_id=1, source_target_pairs={{0,32},{32,0},{1,33},{33,1},{2,34},{34,2},{3,35},{35,3},{4,36},{36... | collective-permute-start | bytes 1572872 | tf_op jit(solution)/shard_map/ppermute | solution.py:408

commit v7 on v6

--- a/solution.py
+++ b/solution.py
@@ -388,17 +388,14 @@
         prepare_queries, shape((H, 4 * HD, count), bf16), flops=1 << 20, limit=53862 << 10
     )(keys)
     mine = lax.dynamic_slice_in_dim(late, core * half + place * rows, rows, 0)
-    packed, queries_t, up_other, down_other, mine = lax.optimization_barrier(
-        (packed, queries_t, up_other, down_other, mine)
-    )
-    tiles = call(combine_space, shape((n_z, rows, width + STATS), bf16))(packed)
-    tiles, *weights = lax.optimization_barrier((tiles, up_late, down_late, up_other, down_other))
-    tiles = lax.all_to_all(tiles, Z, 0, 0, tiled=True)
+    weights = [up_late, down_late, up_other, down_other]
     weights = call(
         hold, [shape(w.shape, bf16) for w in weights], [pltpu.SemaphoreType.DMA((4,))],
-        inputs=4, flops=1 << 20, far=range(4), limit=52838 << 10,
+        inputs=4, flops=1 << 20, far=range(4), limit=52224 << 10,
     )(*weights)
-    tiles, *weights = lax.optimization_barrier((tiles, *weights))
+    packed, queries_t, mine, *weights = lax.optimization_barrier((packed, queries_t, mine, *weights))
+    tiles = call(combine_space, shape((n_z, rows, width + STATS), bf16))(packed)
+    tiles = lax.all_to_all(tiles, Z, 0, 0, tiled=True)
     parts, middle = call(
         mlp, [shape((n_z, rows, width), bf16), shape((rows, width), f32)], inputs=6
     )(tiles, mine, *weights)

time: 101 us -> 99.8 us (0.988)
  blocking collectives: 28 us -> 46 us
  starting transfers between devices: 35.7 us -> 25.7 us
  waiting for transfers between devices: 17.9 us -> 9.07 us
    all_to_all x0 -> x1, blocking collectives: none -> 18 us  [on_device(): tiles = lax.all_to_all(tiles, Z, 0, 0, tiled=True)]
    all_to_all x1 -> x0, starting transfers between devices: 10 us -> none  [on_device(): tiles = lax.all_to_all(tiles, Z, 0, 0, tiled=True)]
    all_to_all x1 -> x0, waiting for transfers between devices: 6.65 us -> none  [on_device(): tiles = lax.all_to_all(tiles, Z, 0, 0, tiled=True)]
    all_to_all x1, waiting for transfers between devices: 11.3 us -> 9.06 us  [on_device(): packed = lax.all_to_all(packed, SPACE, 0, 0, tiled=True)]
  transfers between devices with their start and end apart: 6 -> 5, of which waited for: 2 -> 1; matrix products, arithmetic and copies ran while one was open for 1% -> 1% of each run, Pallas kernels for 7% -> 7%
where the time goes in v7:
time: 99.8 us; the launch traced here: 99.3 us
  blocking collectives  46 us (46%)
  starting transfers between devices  25.7 us (26%)
  Pallas kernels  16.1 us (16%)
  waiting for transfers between devices  9.07 us (9%)
  local copies, waits for them, and re-layouts  1.54 us (2%)
    all_to_all x1, blocking collectives, on_device(): tiles = lax.all_to_all(tiles, Z, 0, 0, tiled=True)  18 us
    all_to_all x1, blocking collectives, on_device(): mine = lax.all_to_all(new, SPACE, 0, 0, tiled=True)  17.6 us
    all_to_all x1, blocking collectives, on_device(): parts = lax.all_to_all(parts, Z, 0, 0, tiled=True)  10.4 us
    all_to_all x1, waiting for transfers between devices, on_device(): packed = lax.all_to_all(packed, SPACE, 0, 0, tiled=True)  9.06 us
    ppermute x1, starting transfers between devices, on_device(): other = lax.ppermute(swapped, CORE, swap)  8.75 us
    ppermute x1, starting transfers between devices, on_device(): theirs = lax.ppermute(mine, CORE, swap)  8.25 us
    all_to_all x1, starting transfers between devices, on_device(): packed = lax.all_to_all(packed, SPACE, 0, 0, tiled=True)  4.33 us
    pallas_call x1, Pallas kernels, on_device(): call(write_second, [shape((count, width), bf16), shape((2, rows, width),...  3.44 us
  transfers between devices with their start and end apart: 5, of which 1 were waited for; matrix products, arithmetic and copies ran while one was open for 1% of the time, Pallas kernels for 7%

profile of v7, /device:TPU:1, one launch (start us, length us, event | category | flops | bytes accessed | tf_op | source)
XLA Modules:
  0.0 99.3 jit_solution(5860418836487558074)
XLA Ops:
  0.6 0.0 copy-start.2
  0.6 0.1 pad_add_fusion.position
  0.7 1.8 %prepare_read.1.queries_t = bf16[16,128,256]{2,1,0:T(8,128)(2,1)S(1)} custom-call(s32[2]{0:T(128)S(1)} %pad_add_fusion.position, bf16[512,1024]{1,0:T(8,128)(2,1)} %latents_hbm.1), custom_call_target="tpu_custom_call" | custom-call | flops 33554432 | bytes 1048576 | tf_op jit(solution)/shard_map/prepare_read/pallas_call | solution.py:362
  2.5 0.0 copy-done.2
  2.5 8.7 %collective-permute-start = (bf16[256,1024]{1,0:T(8,128)(2,1)S(1)}, bf16[256,1024]{1,0:T(8,128)(2,1)S(1)}, u32[]{:S(2)}, u32[]{:S(2)}) collective-permute-start(bf16[256,1024]{1,0:T(8,128)(2,1)S(1)} %copy-done.2), channel_id=1, source_target_pairs={{0,32},{32,0},{1,33},{33,1},{2,34},{34,2},{3,35},{35,3},{4,36},{36... | collective-permute-start | bytes 1572872 | tf_op jit(solution)/shard_map/ppermute | solution.py:367
  11.3 2.0 %read_first.1 = (bf16[256,1024]{1,0:T(8,128)(2,1)S(1)}, f32[16,256]{1,0:T(8,128)S(1)}, f32[16,256]{1,0:T(8,128)S(1)}, f32[1024,256]{1,0:T(8,128)S(1)}) custom-call(bf16[256,1024]{1,0:T(8,128)(2,1)S(1)} %copy-done.2, bf16[16,128,256]{2,1,0:T(8,128)(2,1)S(1)} %prepare_read.1.queries_t), custom_call_target="tpu_custom_call" | custom-call | flops 268435456 | bytes 1048576 | tf_op jit(solution)/shard_map/read_first/pallas_call | solution.py:368
  13.3 0.0 collective-permute-done.tokens
  13.3 0.0 copy-start.1
  13.3 0.0 copy-start.4
  13.3 2.8 %read_second.1 = bf16[32,8,1152]{2,1,0:T(8,128)(2,1)} custom-call(bf16[256,1024]{1,0:T(8,128)(2,1)S(1)} %collective-permute-done.tokens, bf16[16,128,256]{2,1,0:T(8,128)(2,1)S(1)} %prepare_read.1.queries_t, f32[16,256]{1,0:T(8,128)S(1)} %get-tuple-element.34.peaks, f32[16,256]{1,0:T(8,128)S(1)} %get-tuple-element.35.totals, ...), custom_call_target="tpu_custom_call" | custom-call | flops 268435456 | bytes 1048576 | tf_op jit(solution)/shard_map/read_second/pallas_call | solution.py:374
  16.1 4.3 %all-to-all-start = ((bf16[32,8,1152]{2,1,0:T(8,128)(2,1)}), bf16[32,8,1152]{2,1,0:T(8,128)(2,1)S(1)}, u32[]{:S(2)}, u32[]{:S(2)}) async-start(bf16[32,8,1152]{2,1,0:T(8,128)(2,1)} %read_second.1), calls=%async_computation | async-start | bytes 1179648 | tf_op jit(solution)/shard_map/all_to_all | solution.py:385
  20.4 0.0 copy-done.1
  20.4 2.2 %collective-permute-start.1 = (bf16[1024,256]{1,0:T(8,128)(2,1)S(1)}, bf16[1024,256]{1,0:T(8,128)(2,1)S(1)}, u32[]{:S(2)}, u32[]{:S(2)}) collective-permute-start(bf16[1024,256]{1,0:T(8,128)(2,1)S(1)} %copy-done.1), channel_id=1, source_target_pairs={{0,32},{32,0},{1,33},{33,1},{2,34},{34,2},{3,35},{35,3},{4,36},{36... | collective-permute-start | bytes 1572872 | tf_op jit(solution)/shard_map/ppermute | solution.py:386
  22.6 0.0 copy-done.4
  22.7 2.1 %collective-permute-start.2 = (bf16[256,1024]{1,0:T(8,128)(2,1)S(1)}, bf16[256,1024]{1,0:T(8,128)(2,1)}, u32[]{:S(2)}, u32[]{:S(2)}) collective-permute-start(bf16[256,1024]{1,0:T(8,128)(2,1)S(1)} %copy-done.4), channel_id=1, source_target_pairs={{0,32},{32,0},{1,33},{33,1},{2,34},{34,2},{3,35},{35,3},{4,36},{36... | collective-permute-start | bytes 1572872 | tf_op jit(solution)/shard_map/ppermute | solution.py:386
  24.8 1.7 %prepare_queries.1.queries_t = bf16[16,256,256]{2,1,0:T(8,128)(2,1)} custom-call(bf16[256,1024]{1,0:T(8,128)(2,1)S(1)} %get-tuple-element.39.keys), custom_call_target="tpu_custom_call" | custom-call | flops 1048576 | bytes 1048576 | tf_op jit(solution)/shard_map/prepare_queries/pallas_call | solution.py:387
  26.5 0.7 constant_dynamic-slice_fusion.latents
  27.2 0.0 collective-permute-done.1.refs_2_
  27.2 0.8 copy-done.5
  28.0 0.0 collective-permute-done.2.refs_3_
  28.0 1.4 %hold.1 = (bf16[1024,256]{1,0:T(8,128)(2,1)S(1)}, bf16[256,1024]{1,0:T(8,128)(2,1)S(1)}, bf16[1024,256]{1,0:T(8,128)(2,1)S(1)}, bf16[256,1024]{1,0:T(8,128)(2,1)S(1)}) custom-call(bf16[1024,256]{1,0:T(8,128)(2,1)S(1)} %copy-done.1, bf16[256,1024]{1,0:T(8,128)(2,1)} %refs_1_, bf16[1024,256]{1,0:T(8,128)(2,1)} %copy-done.5, ...), custom_call_target="tpu_custom_call" | custom-call | flops 1048576 | bytes 1048576 | tf_op jit(solution)/shard_map/hold/pallas_call | solution.py:392
  29.4 9.1 %all-to-all-done.arrived = bf16[32,8,1152]{2,1,0:T(8,128)(2,1)S(1)} async-done(((bf16[32,8,1152]{2,1,0:T(8,128)(2,1)}), bf16[32,8,1152]{2,1,0:T(8,128)(2,1)S(1)}, u32[]{:S(2)}, u32[]{:S(2)}) %all-to-all-start) | async-done | bytes 589856 | tf_op jit(solution)/shard_map/all_to_all | solution.py:385
  38.5 0.4 combine_space.1
  38.9 18.0 %all_to_all.20.arrived = bf16[8,8,1152]{2,1,0:T(8,128)(2,1)S(1)} all-to-all(bf16[8,8,1152]{2,1,0:T(8,128)(2,1)S(1)} %combine_space.1), channel_id=1, replica_groups=mesh['tm_0'=8,'tm_1'=2,'space_0'=8,'space_1'=4] {'tm_0'}, dimensions={0} | all-to-all | bytes 294912 | tf_op jit(solution)/shard_map/all_to_all | solution.py:398
  56.9 0.9 mlp.1
  57.8 10.4 %all_to_all.21.parts = bf16[8,8,1024]{2,1,0:T(8,128)(2,1)S(1)} all-to-all(bf16[8,8,1024]{2,1,0:T(8,128)(2,1)S(1)} %get-tuple-element.53), channel_id=1, replica_groups=mesh['tm_0'=8,'tm_1'=2,'space_0'=8,'space_1'=4] {'tm_0'}, dimensions={0} | all-to-all | bytes 262144 | tf_op jit(solution)/shard_map/all_to_all | solution.py:402
  68.2 0.1 finish.1
  68.3 17.6 %all_to_all.22.latents.mine = bf16[32,8,1024]{2,1,0:T(8,128)(2,1)S(1)} all-to-all(bf16[32,8,1024]{2,1,0:T(8,128)(2,1)S(1)} %finish.1), channel_id=1, replica_groups=mesh['tm_0'=8,'tm_1'=2,'space_0'=8,'space_1'=4] {'space_0','space_1'}, dimensions={0} | all-to-all | bytes 1048576 | tf_op jit(solution)/shard_map/all_to_all | solution.py:404
  85.9 8.2 %collective-permute-start.3 = (bf16[32,8,1024]{2,1,0:T(8,128)(2,1)S(1)}, bf16[32,8,1024]{2,1,0:T(8,128)(2,1)S(1)}, u32[]{:S(2)}, u32[]{:S(2)}) collective-permute-start(bf16[32,8,1024]{2,1,0:T(8,128)(2,1)S(1)} %all_to_all.22.latents.mine), channel_id=1, source_target_pairs={{0,32},{32,0},{1,33},{33,1},{2,34},{34,2},{3,35},{35,3},{4,36},{36... | collective-permute-start | bytes 1572872 | tf_op jit(solution)/shard_map/ppermute | solution.py:405
  94.2 1.7 %write_first.1 = (f32[16,256]{1,0:T(8,128)S(1)}, f32[16,256]{1,0:T(8,128)S(1)}, f32[1024,256]{1,0:T(8,128)S(1)}, bf16[256,1024]{1,0:T(8,128)(2,1)S(1)}) custom-call(bf16[32,8,1024]{2,1,0:T(8,128)(2,1)S(1)} %all_to_all.22.latents.mine, bf16[16,256,256]{2,1,0:T(8,128)(2,1)S(1)} %copy-done, bf16[256,1024]{1,0:T(8,128)(2,1)S(1)} %copy-done.3), custom_call_target="tpu_custom_call" | custom-call | flops 268435456 | bytes 1048576 | tf_op jit(solution)/shard_map/write_first/pallas_call | solution.py:406
  95.9 0.0 collective-permute-done.3.latents
  95.9 3.4 %write_second.1 = (bf16[256,1024]{1,0:T(8,128)(2,1)}, bf16[2,8,1024]{2,1,0:T(8,128)(2,1)}) custom-call(s32[2]{0:T(128)S(1)} %pad_add_fusion.position, bf16[32,8,1024]{2,1,0:T(8,128)(2,1)S(1)} %collective-permute-done.3.latents, bf16[32,8,1024]{2,1,0:T(8,128)(2,1)S(1)} %all_to_all.22.latents.mine, bf16[16,256,256]{2,1,0:T(8,128)(2,1)S(1)} %copy-done, ...), custom_call_target="tpu_custom_call" | custom-call | flops 268435456 | bytes 1048576 | tf_op jit(solution)/shard_map/write_second/pallas_call | solution.py:411
  (5 shorter events, 0.0 us)
Async XLA Ops:
  0.6 1.9 %copy-start.2 = (bf16[256,1024]{1,0:T(8,128)(2,1)S(1)}, bf16[256,1024]{1,0:T(8,128)(2,1)}, u32[]{:S(2)}) copy-start(bf16[256,1024]{1,0:T(8,128)(2,1)} %tokens_hbm.1) | copy-start | bytes 1572868
  2.5 10.7 %collective-permute-start = (bf16[256,1024]{1,0:T(8,128)(2,1)S(1)}, bf16[256,1024]{1,0:T(8,128)(2,1)S(1)}, u32[]{:S(2)}, u32[]{:S(2)}) collective-permute-start(bf16[256,1024]{1,0:T(8,128)(2,1)S(1)} %copy-done.2), channel_id=1, source_target_pairs={{0,32},{32,0},{1,33},{33,1},{2,34},{34,2},{3,35},{35,3},{4,36},{36... | collective-permute-start | bytes 1572872 | tf_op jit(solution)/shard_map/ppermute | solution.py:367
  13.3 7.1 %copy-start.1 = (bf16[1024,256]{1,0:T(8,128)(2,1)S(1)}, bf16[1024,256]{1,0:T(8,128)(2,1)}, u32[]{:S(2)}) copy-start(bf16[1024,256]{1,0:T(8,128)(2,1)} %refs_0_) | copy-start | bytes 1572868
  13.3 9.3 %copy-start.4 = (bf16[256,1024]{1,0:T(8,128)(2,1)S(1)}, bf16[256,1024]{1,0:T(8,128)(2,1)}, u32[]{:S(2)}) copy-start(bf16[256,1024]{1,0:T(8,128)(2,1)} %refs_1_) | copy-start | bytes 1572868
  16.1 22.4 %all-to-all-start = ((bf16[32,8,1152]{2,1,0:T(8,128)(2,1)}), bf16[32,8,1152]{2,1,0:T(8,128)(2,1)S(1)}, u32[]{:S(2)}, u32[]{:S(2)}) async-start(bf16[32,8,1152]{2,1,0:T(8,128)(2,1)} %read_second.1), calls=%async_computation | async-start | bytes 1179648 | tf_op jit(solution)/shard_map/all_to_all | solution.py:385
  20.4 6.7 %collective-permute-start.1 = (bf16[1024,256]{1,0:T(8,128)(2,1)S(1)}, bf16[1024,256]{1,0:T(8,128)(2,1)S(1)}, u32[]{:S(2)}, u32[]{:S(2)}) collective-permute-start(bf16[1024,256]{1,0:T(8,128)(2,1)S(1)} %copy-done.1), channel_id=1, source_target_pairs={{0,32},{32,0},{1,33},{33,1},{2,34},{34,2},{3,35},{35,3},{4,36},{36... | collective-permute-start | bytes 1572872 | tf_op jit(solution)/shard_map/ppermute | solution.py:386
  22.7 5.3 %collective-permute-start.2 = (bf16[256,1024]{1,0:T(8,128)(2,1)S(1)}, bf16[256,1024]{1,0:T(8,128)(2,1)}, u32[]{:S(2)}, u32[]{:S(2)}) collective-permute-start(bf16[256,1024]{1,0:T(8,128)(2,1)S(1)} %copy-done.4), channel_id=1, source_target_pairs={{0,32},{32,0},{1,33},{33,1},{2,34},{34,2},{3,35},{35,3},{4,36},{36... | collective-permute-start | bytes 1572872 | tf_op jit(solution)/shard_map/ppermute | solution.py:386
  27.2 0.8 copy-start.5
  56.9 37.3 %copy-start = (bf16[16,256,256]{2,1,0:T(8,128)(2,1)S(1)}, bf16[16,256,256]{2,1,0:T(8,128)(2,1)}, u32[]{:S(2)}) copy-start(bf16[16,256,256]{2,1,0:T(8,128)(2,1)} %prepare_queries.1.queries_t) | copy-start | bytes 6291460
  56.9 37.3 %copy-start.3 = (bf16[256,1024]{1,0:T(8,128)(2,1)S(1)}, bf16[256,1024]{1,0:T(8,128)(2,1)}, u32[]{:S(2)}) copy-start(bf16[256,1024]{1,0:T(8,128)(2,1)} %tokens_hbm.1) | copy-start | bytes 1572868
  85.9 10.0 %collective-permute-start.3 = (bf16[32,8,1024]{2,1,0:T(8,128)(2,1)S(1)}, bf16[32,8,1024]{2,1,0:T(8,128)(2,1)S(1)}, u32[]{:S(2)}, u32[]{:S(2)}) collective-permute-start(bf16[32,8,1024]{2,1,0:T(8,128)(2,1)S(1)} %all_to_all.22.latents.mine), channel_id=1, source_target_pairs={{0,32},{32,0},{1,33},{33,1},{2,34},{34,2},{3,35},{35,3},{4,36},{36... | collective-permute-start | bytes 1572872 | tf_op jit(solution)/shard_map/ppermute | solution.py:405
